TPU v7x, 32 devices: a whole 2x2x4 slice. The times are simulated.
32 devices in a mesh: dp: 8 (over z, y), tensor: 4 (over x, core).
Axes of the slice: x: 2, y: 2, z: 4, core: 2. Of those that a mesh axis runs over, the one named last changes fastest.
Arguments:
- layer_input: bfloat16 [4096, 2048], P(('dp', 'tensor')), may hold values from -6 to 6
- segment_ids: int32 [8, 512], P('dp'), may hold values from 0 to 2, never falling along the last dimension, each value on 1 to 256 neighbouring positions
- routes: int32 [4096, 6], P(('dp', 'tensor')), may hold values from 0 to 15, all different within a row
- route_weight: float32 [4096, 6], P(('dp', 'tensor')), may hold values from 0.1 to 1
- place_order: int32 [32, 768], P(('dp', 'tensor')), may hold values from 0 to 767, each once within a row
- attention_gain: bfloat16 [2048], P('dp'), may hold values from 0.099609375 to 1.8984375
- query_weight: bfloat16 [2048, 3072], P('dp', 'tensor'), may hold values from -0.125 to 0.125
- latent_weight: bfloat16 [2048, 576], P('dp'), may hold values from -0.125 to 0.125
- latent_gain: bfloat16 [512], P('dp'), may hold values from 0.099609375 to 1.8984375
- latent_up: bfloat16 [512, 4096], P('dp', 'tensor'), may hold values from -0.25 to 0.25
- output_weight: bfloat16 [2048, 2048], P('tensor', 'dp'), may hold values from -1 to 1
- experts_gain: bfloat16 [2048], P('dp'), may hold values from 0.099609375 to 1.8984375
- expert_gate: bfloat16 [16, 2048, 1408], P('dp', None, 'tensor'), may hold values from -0.125 to 0.125
- expert_up: bfloat16 [16, 2048, 1408], P('dp', None, 'tensor'), may hold values from -0.125 to 0.125
- expert_down: bfloat16 [16, 1408, 2048], P('dp', 'tensor'), may hold values from -0.15625 to 0.15625
- shared_gate: bfloat16 [2048, 2816], P('dp'), may hold values from -0.125 to 0.125
- shared_up: bfloat16 [2048, 2816], P('dp'), may hold values from -0.125 to 0.125
- shared_down: bfloat16 [2816, 2048], P(None, 'dp'), may hold values from -0.109375 to 0.109375
- out_cotangent: bfloat16 [4096, 2048], P(('dp', 'tensor')), may hold values from -6 to 6
Outputs:
- layer_output: bfloat16 [4096, 2048], P(('dp', 'tensor'))
- grad_input: float32 [4096, 2048], P(('dp', 'tensor'))
- grad_attention_gain: float32 [2048], P(('dp', 'tensor'))
- grad_query_weight: float32 [2048, 3072], P('dp', 'tensor')
- grad_latent_weight: float32 [2048, 576], P(('dp', 'tensor'))
- grad_latent_gain: float32 [512], P(('dp', 'tensor'))
- grad_latent_up: float32 [512, 4096], P('dp', 'tensor')
- grad_output_weight: float32 [2048, 2048], P('tensor', 'dp')
- grad_experts_gain: float32 [2048], P(('dp', 'tensor'))
- grad_expert_gate: float32 [16, 2048, 1408], P('dp', None, 'tensor')
- grad_expert_up: float32 [16, 2048, 1408], P('dp', None, 'tensor')
- grad_expert_down: float32 [16, 1408, 2048], P('dp', 'tensor')
- grad_shared_gate: float32 [2048, 2816], P('dp', 'tensor')
- grad_shared_up: float32 [2048, 2816], P('dp', 'tensor')
- grad_shared_down: float32 [2816, 2048], P('tensor', 'dp')
Inputs may be any that keep to these rules, and one draw needn't show every extreme that they name: `routes`: each row names 6 different experts, and every expert is named by some row. `place_order`: each row holds every number from 0 to 767 once. `segment_ids`: document numbers never fall along a sequence; a document has 1 to 256 tokens.
All inputs are finite; a program needn't handle non-finite values.
Results may differ from a plain program's by a relative error of at most 0.02.
Values may be sent and summed in bfloat16 or wider, within the bound.
No kernel may reach another device: no remote copies, remote signals or barrier semaphores. Data moves between devices by JAX's collectives and lax.ppermute only.
A program may use at most 384 MiB of HBM per device.

v0:
```python
import jax
import jax.numpy as jnp
from jax import lax
from jax.sharding import PartitionSpec as P

D = 2048
QK_NOPE = 128
QK_ROPE = 64
V_DIM = 128
KV_RANK = 512
TOPK = 6


NORM_EPS = 1e-06


def root_norm(values, gain_row):
    factor = lax.rsqrt(jnp.mean(values * values, axis=-1, keepdims=True) + NORM_EPS)
    return values * factor * gain_row


def turn_tables(positions, half_width):
    frequency = 10000.0 ** (-jnp.arange(half_width, dtype=jnp.float32) / half_width)
    angles = positions.astype(jnp.float32)[:, None] * frequency[None, :]
    return (jnp.cos(angles), jnp.sin(angles))


def rotate(values, cosine, sine_table):
    half_width = values.shape[-1] // 2
    first_half = values[..., :half_width]
    second_half = values[..., half_width:]
    return jnp.concatenate(
        [
            first_half * cosine - second_half * sine_table,
            first_half * sine_table + second_half * cosine,
        ],
        axis=-1,
    )


def sigmoid_pair(values):
    logistic = jax.nn.sigmoid(values)
    return (values * logistic, logistic * (1.0 + values * (1.0 - logistic)))


def slot_places(expert_ids, rank_order, expert_count):
    pair_count = expert_ids.shape[0]
    inverse = (
        jnp.zeros((pair_count,), jnp.int32)
        .at[rank_order]
        .set(jnp.arange(pair_count, dtype=jnp.int32))
    )
    ranked = expert_ids[inverse]
    onehot = (ranked[:, None] == jnp.arange(expert_count, dtype=jnp.int32)[None, :]).astype(
        jnp.int32
    )
    earlier = jnp.cumsum(onehot, axis=0) - onehot
    ranked_place = jnp.sum(earlier * onehot, axis=1)
    return ranked_place[rank_order]


def to_experts(buffer, dp_count, tensor_count):
    slot_rows = buffer.shape[0] // dp_count
    feature_count = buffer.shape[1]
    copies = jnp.broadcast_to(
        buffer.reshape(dp_count, 1, slot_rows, feature_count),
        (dp_count, tensor_count, slot_rows, feature_count),
    )
    return lax.all_to_all(
        copies.reshape(dp_count * tensor_count, slot_rows, feature_count),
        ("dp", "tensor"),
        split_axis=0,
        concat_axis=0,
        tiled=True,
    )


def from_experts(partial_rows, dp_count, tensor_count):
    slot_rows = partial_rows.shape[1]
    feature_count = partial_rows.shape[2]
    returned = lax.all_to_all(
        partial_rows.astype(jnp.bfloat16), ("dp", "tensor"), split_axis=0, concat_axis=0, tiled=True
    )
    return jnp.sum(
        returned.reshape(dp_count, tensor_count, slot_rows, feature_count),
        axis=1,
        dtype=jnp.float32,
    ).reshape(dp_count * slot_rows, feature_count)


def local(
    layer_input,
    segment_ids,
    routes,
    route_weight,
    place_order,
    attention_gain,
    query_weight,
    latent_weight,
    latent_gain,
    latent_up,
    output_weight,
    experts_gain,
    expert_gate,
    expert_up,
    expert_down,
    shared_gate,
    shared_up,
    shared_down,
    out_cotangent,
):
    tensor_count = lax.axis_size("tensor")
    dp_count = lax.axis_size("dp")
    shard_rows = layer_input.shape[0]
    seq_len = segment_ids.shape[1]
    gathered = (
        lax.all_gather(attention_gain, "dp", axis=0, tiled=True),
        lax.all_gather(query_weight, "dp", axis=0, tiled=True),
        lax.all_gather(latent_weight, "dp", axis=0, tiled=True),
        lax.all_gather(latent_gain, "dp", axis=0, tiled=True),
        lax.all_gather(latent_up, "dp", axis=0, tiled=True),
        lax.all_gather(output_weight, "dp", axis=1, tiled=True),
        lax.all_gather(experts_gain, "dp", axis=0, tiled=True),
        lax.all_gather(shared_gate, "dp", axis=0, tiled=True),
        lax.all_gather(shared_up, "dp", axis=0, tiled=True),
        lax.all_gather(shared_down, "dp", axis=1, tiled=True),
    )
    (
        gain_mixer,
        weight_query,
        weight_latent,
        gain_latent,
        weight_up,
        weight_out,
        gain_experts,
        gate_common,
        up_common,
        down_common,
    ) = gathered
    mixer_scale = gain_mixer.astype(jnp.float32)
    latent_scale = gain_latent.astype(jnp.float32)
    experts_scale = gain_experts.astype(jnp.float32)
    input_float = layer_input.astype(jnp.float32)
    normed_first = root_norm(input_float, mixer_scale).astype(jnp.bfloat16)
    latent_all = jnp.dot(normed_first, weight_latent, preferred_element_type=jnp.float32)
    latent_raw = latent_all[:, :KV_RANK]
    latent_norm = root_norm(latent_raw, latent_scale).astype(jnp.bfloat16)
    shard_positions = lax.axis_index("tensor") * shard_rows + jnp.arange(
        shard_rows, dtype=jnp.int32
    )
    shard_cos, shard_sin = turn_tables(shard_positions, QK_ROPE // 2)
    rope_shard = rotate(latent_all[:, KV_RANK:], shard_cos, shard_sin).astype(jnp.bfloat16)
    normed_full, latent_full, rope_full = (
        lax.all_gather(normed_first, "tensor", axis=0, tiled=True),
        lax.all_gather(latent_norm, "tensor", axis=0, tiled=True),
        lax.all_gather(rope_shard, "tensor", axis=0, tiled=True),
    )
    head_dim = QK_NOPE + QK_ROPE
    local_heads = weight_query.shape[1] // head_dim
    seq_cos, seq_sin = turn_tables(jnp.arange(seq_len, dtype=jnp.int32), QK_ROPE // 2)
    query_raw = jnp.dot(normed_full, weight_query, preferred_element_type=jnp.float32).reshape(
        seq_len, local_heads, head_dim
    )
    query_cat = jnp.concatenate(
        [
            query_raw[..., :QK_NOPE],
            rotate(query_raw[..., QK_NOPE:], seq_cos[:, None, :], seq_sin[:, None, :]),
        ],
        axis=-1,
    ).astype(jnp.bfloat16)
    key_value = (
        jnp.dot(latent_full, weight_up, preferred_element_type=jnp.float32)
        .astype(jnp.bfloat16)
        .reshape(seq_len, local_heads, QK_NOPE + V_DIM)
    )
    key_rows = jnp.concatenate(
        [
            key_value[..., :QK_NOPE],
            jnp.broadcast_to(rope_full[:, None, :], (seq_len, local_heads, QK_ROPE)),
        ],
        axis=-1,
    )
    values = key_value[..., QK_NOPE:]
    doc_ids = segment_ids[0]
    block_rows = min(512, seq_len)
    block_count = seq_len // block_rows
    scaling = head_dim ** (-0.5)
    key_positions = jnp.arange(seq_len, dtype=jnp.int32)

    def block_scores(block_index):
        block_start = block_index * block_rows
        raw_scores = (
            jnp.einsum("qhd,khd->hqk", query_cat, key_rows, preferred_element_type=jnp.float32)
            * scaling
        )
        query_positions = block_start + jnp.arange(block_rows, dtype=jnp.int32)
        allowed = (doc_ids[:, None] == doc_ids[None, :]) & (
            key_positions[None, :] <= query_positions[:, None]
        )
        return (block_start, query_cat, raw_scores, allowed)

    def attend_block(block_index):
        block_start, query_block, raw_scores, allowed = block_scores(block_index)
        masked = jnp.where(allowed[None], raw_scores, -1e30)
        row_max = jnp.max(masked, axis=-1, keepdims=True)
        exp_terms = jnp.exp(masked - row_max)
        row_total = jnp.sum(exp_terms, axis=-1, keepdims=True)
        prob_rows = (exp_terms / row_total).astype(jnp.bfloat16)
        heads_block = jnp.einsum(
            "hqk,khd->qhd", prob_rows, values, preferred_element_type=jnp.float32
        )
        return (heads_block.astype(jnp.bfloat16), (row_max + jnp.log(row_total))[..., 0])

    heads_blocks, log_totals = lax.map(attend_block, jnp.arange(block_count, dtype=jnp.int32))
    heads_out = heads_blocks.reshape(seq_len, local_heads * V_DIM)
    mixer_terms = jnp.dot(heads_out, weight_out, preferred_element_type=jnp.float32)
    mixer_out = lax.psum_scatter(mixer_terms, "tensor", scatter_dimension=0, tiled=True)
    hidden_state = input_float + mixer_out
    normed_second = root_norm(hidden_state, experts_scale).astype(jnp.bfloat16)
    gate_shared = jnp.dot(normed_second, gate_common, preferred_element_type=jnp.float32)
    up_shared = jnp.dot(normed_second, up_common, preferred_element_type=jnp.float32)
    silu_shared, slope_shared = sigmoid_pair(gate_shared)
    hidden_shared = (silu_shared * up_shared).astype(jnp.bfloat16)
    shared_partial = jnp.dot(hidden_shared, down_common, preferred_element_type=jnp.float32)
    expert_local = expert_gate.shape[0]
    expert_total = expert_local * dp_count
    capacity = max(2, 5 * shard_rows * TOPK // (4 * expert_total))
    pair_count = shard_rows * TOPK
    expert_ids = routes.reshape(pair_count)
    places = slot_places(expert_ids, place_order[0], expert_total)
    kept_mask = places < capacity
    slot_index = jnp.where(kept_mask, expert_ids * capacity + places, expert_total * capacity)
    pair_tokens = jnp.arange(pair_count, dtype=jnp.int32) // TOPK
    slot_tokens = (
        jnp.full((expert_total * capacity,), shard_rows, jnp.int32)
        .at[slot_index]
        .set(pair_tokens, mode="drop")
    )
    send_rows = jnp.take(normed_second, slot_tokens, axis=0, mode="fill", fill_value=0)
    arrived = to_experts(send_rows, dp_count, tensor_count)
    source_count = arrived.shape[0]
    rows_in = arrived.reshape(source_count, expert_local, capacity, D)
    gate_val = jnp.einsum(
        "sjcd,jdf->sjcf", rows_in, expert_gate, preferred_element_type=jnp.float32
    )
    up_val = jnp.einsum("sjcd,jdf->sjcf", rows_in, expert_up, preferred_element_type=jnp.float32)
    silu_gate, slope_gate = sigmoid_pair(gate_val)
    hidden_rows = (silu_gate * up_val).astype(jnp.bfloat16)
    expert_terms = jnp.einsum(
        "sjcf,jfd->sjcd", hidden_rows, expert_down, preferred_element_type=jnp.float32
    ).reshape(source_count, expert_local * capacity, D)
    expert_result = from_experts(expert_terms, dp_count, tensor_count)
    pair_weights = route_weight.reshape(pair_count)
    pair_out = (
        jnp.take(expert_result, slot_index, axis=0, mode="fill", fill_value=0.0)
        * pair_weights[:, None]
    )
    routed_out = jnp.sum(pair_out.reshape(shard_rows, TOPK, D), axis=1)
    cotangent = out_cotangent.astype(jnp.float32)
    pair_grads = (jnp.take(cotangent, pair_tokens, axis=0) * pair_weights[:, None]).astype(
        jnp.bfloat16
    )
    grad_slots = (
        jnp.zeros((expert_total * capacity, D), jnp.bfloat16)
        .at[slot_index]
        .set(pair_grads, mode="drop")
    )
    grad_arrived = to_experts(grad_slots, dp_count, tensor_count).reshape(
        source_count, expert_local, capacity, D
    )
    grad_expert_down = jnp.einsum(
        "sjcf,sjcd->jfd", hidden_rows, grad_arrived, preferred_element_type=jnp.float32
    )
    grad_hidden_rows = jnp.einsum(
        "sjcd,jfd->sjcf", grad_arrived, expert_down, preferred_element_type=jnp.float32
    )
    grad_gate_rows = (grad_hidden_rows * up_val * slope_gate).astype(jnp.bfloat16)
    grad_up_rows = (grad_hidden_rows * silu_gate).astype(jnp.bfloat16)
    grad_expert_gate = jnp.einsum(
        "sjcd,sjcf->jdf", rows_in, grad_gate_rows, preferred_element_type=jnp.float32
    )
    grad_expert_up = jnp.einsum(
        "sjcd,sjcf->jdf", rows_in, grad_up_rows, preferred_element_type=jnp.float32
    )
    input_terms = jnp.einsum(
        "sjcf,jdf->sjcd", grad_gate_rows, expert_gate, preferred_element_type=jnp.float32
    ) + jnp.einsum("sjcf,jdf->sjcd", grad_up_rows, expert_up, preferred_element_type=jnp.float32)
    input_result = from_experts(
        input_terms.reshape(source_count, expert_local * capacity, D), dp_count, tensor_count
    )
    grad_routed = jnp.sum(
        jnp.take(input_result, slot_index, axis=0, mode="fill", fill_value=0.0).reshape(
            shard_rows, TOPK, D
        ),
        axis=1,
    )
    grad_hidden_shared = jnp.einsum(
        "rd,fd->rf", out_cotangent, down_common, preferred_element_type=jnp.float32
    )
    grad_gate_common = (grad_hidden_shared * up_shared * slope_shared).astype(jnp.bfloat16)
    grad_up_common = (grad_hidden_shared * silu_shared).astype(jnp.bfloat16)
    grad_down_shared = jnp.einsum(
        "rf,rd->fd", hidden_shared, out_cotangent, preferred_element_type=jnp.float32
    )
    grad_gate_shared = jnp.einsum(
        "rd,rf->df", normed_second, grad_gate_common, preferred_element_type=jnp.float32
    )
    grad_up_shared = jnp.einsum(
        "rd,rf->df", normed_second, grad_up_common, preferred_element_type=jnp.float32
    )
    shared_back_partial = jnp.einsum(
        "rf,df->rd", grad_gate_common, gate_common, preferred_element_type=jnp.float32
    ) + jnp.einsum("rf,df->rd", grad_up_common, up_common, preferred_element_type=jnp.float32)
    layer_output = (hidden_state + routed_out + shared_partial).astype(jnp.bfloat16)
    grad_normed_second = grad_routed + shared_back_partial
    unused_second, second_back = jax.vjp(root_norm, hidden_state, experts_scale)
    grad_from_experts, grad_experts_part = second_back(grad_normed_second)
    grad_hidden_state = cotangent + grad_from_experts
    grad_mixer_full = lax.all_gather(
        grad_hidden_state.astype(jnp.bfloat16), "tensor", axis=0, tiled=True
    )
    grad_output_local = jnp.einsum(
        "sk,sd->kd", heads_out, grad_mixer_full, preferred_element_type=jnp.float32
    )
    grad_heads = (
        jnp.einsum("sd,kd->sk", grad_mixer_full, weight_out, preferred_element_type=jnp.float32)
        .astype(jnp.bfloat16)
        .reshape(seq_len, local_heads, V_DIM)
    )

    def back_block(carried, block_index):
        grad_keys, grad_values = carried
        block_start, query_block, raw_scores, allowed = block_scores(block_index)
        block_totals = log_totals[block_index]
        prob_rows = jnp.where(allowed[None], jnp.exp(raw_scores - block_totals[..., None]), 0.0)
        grad_probs = jnp.einsum(
            "qhd,khd->hqk", grad_heads, values, preferred_element_type=jnp.float32
        )
        row_dot = jnp.sum(prob_rows * grad_probs, axis=-1, keepdims=True)
        grad_scores = (prob_rows * (grad_probs - row_dot)).astype(jnp.bfloat16)
        grad_query_block = (
            jnp.einsum("hqk,khd->qhd", grad_scores, key_rows, preferred_element_type=jnp.float32)
            * scaling
        )
        grad_keys = (
            grad_keys
            + jnp.einsum(
                "hqk,qhd->khd", grad_scores, query_block, preferred_element_type=jnp.float32
            )
            * scaling
        )
        grad_values = grad_values + jnp.einsum(
            "hqk,qhd->khd",
            prob_rows.astype(jnp.bfloat16),
            grad_heads,
            preferred_element_type=jnp.float32,
        )
        return ((grad_keys, grad_values), grad_query_block)

    zero_keys = jnp.zeros((seq_len, local_heads, head_dim), jnp.float32)
    zero_values = jnp.zeros((seq_len, local_heads, V_DIM), jnp.float32)
    (grad_keys, grad_values), grad_query_blocks = lax.scan(
        back_block, (zero_keys, zero_values), jnp.arange(block_count, dtype=jnp.int32)
    )
    grad_query = grad_query_blocks.reshape(seq_len, local_heads, head_dim)
    grad_query_raw = (
        jnp.concatenate(
            [
                grad_query[..., :QK_NOPE],
                rotate(grad_query[..., QK_NOPE:], seq_cos[:, None, :], -seq_sin[:, None, :]),
            ],
            axis=-1,
        )
        .reshape(seq_len, local_heads * head_dim)
        .astype(jnp.bfloat16)
    )
    grad_query_local = jnp.einsum(
        "sd,sk->dk", normed_full, grad_query_raw, preferred_element_type=jnp.float32
    )
    grad_normed_full = jnp.einsum(
        "sk,dk->sd", grad_query_raw, weight_query, preferred_element_type=jnp.float32
    )
    grad_key_value = (
        jnp.concatenate([grad_keys[..., :QK_NOPE], grad_values], axis=-1)
        .reshape(seq_len, local_heads * (QK_NOPE + V_DIM))
        .astype(jnp.bfloat16)
    )
    grad_up_local = jnp.einsum(
        "sr,sk->rk", latent_full, grad_key_value, preferred_element_type=jnp.float32
    )
    grad_latent_full = jnp.concatenate(
        [
            jnp.einsum("sk,rk->sr", grad_key_value, weight_up, preferred_element_type=jnp.float32),
            jnp.sum(grad_keys[..., QK_NOPE:], axis=1),
        ],
        axis=-1,
    )
    grad_normed_shard, grad_latent_shard = (
        lax.psum_scatter(
            grad_normed_full.astype(jnp.bfloat16), "tensor", scatter_dimension=0, tiled=True
        ).astype(jnp.float32),
        lax.psum_scatter(
            grad_latent_full.astype(jnp.bfloat16), "tensor", scatter_dimension=0, tiled=True
        ).astype(jnp.float32),
    )
    unused_latent, latent_back = jax.vjp(root_norm, latent_raw, latent_scale)
    grad_latent_raw, grad_latent_part = latent_back(grad_latent_shard[:, :KV_RANK])
    grad_rope = rotate(grad_latent_shard[:, KV_RANK:], shard_cos, -shard_sin)
    grad_latent_all = jnp.concatenate([grad_latent_raw, grad_rope], axis=-1).astype(jnp.bfloat16)
    grad_latent_local = jnp.einsum(
        "sd,sk->dk", normed_first, grad_latent_all, preferred_element_type=jnp.float32
    )
    grad_normed_first = grad_normed_shard + jnp.einsum(
        "sk,dk->sd", grad_latent_all, weight_latent, preferred_element_type=jnp.float32
    )
    unused_first, first_back = jax.vjp(root_norm, input_float, mixer_scale)
    grad_from_mixer, grad_mixer_part = first_back(grad_normed_first)
    grad_input = grad_hidden_state + grad_from_mixer
    grad_query_weight, grad_latent_up, grad_output_weight = (
        lax.psum_scatter(
            grad_query_local.astype(jnp.bfloat16), "dp", scatter_dimension=0, tiled=True
        ).astype(jnp.float32),
        lax.psum_scatter(
            grad_up_local.astype(jnp.bfloat16), "dp", scatter_dimension=0, tiled=True
        ).astype(jnp.float32),
        lax.psum_scatter(
            grad_output_local.astype(jnp.bfloat16), "dp", scatter_dimension=1, tiled=True
        ).astype(jnp.float32),
    )
    model_width = grad_gate_shared.shape[0]
    hidden_total = grad_gate_shared.shape[1]
    row_block = model_width // dp_count
    unit_block = hidden_total // tensor_count
    group_count = dp_count * tensor_count
    gate_blocks = jnp.transpose(
        grad_gate_shared.reshape(dp_count, row_block, tensor_count, unit_block), (0, 2, 1, 3)
    ).reshape(group_count, row_block, unit_block)
    up_blocks = jnp.transpose(
        grad_up_shared.reshape(dp_count, row_block, tensor_count, unit_block), (0, 2, 1, 3)
    ).reshape(group_count, row_block, unit_block)
    down_blocks = jnp.transpose(
        grad_down_shared.reshape(tensor_count, unit_block, dp_count, row_block), (2, 0, 1, 3)
    ).reshape(group_count, unit_block, row_block)
    reduced = (
        lax.psum_scatter(grad_mixer_part, ("dp", "tensor"), scatter_dimension=0, tiled=True),
        lax.psum_scatter(grad_latent_local, ("dp", "tensor"), scatter_dimension=0, tiled=True),
        lax.psum_scatter(grad_latent_part, ("dp", "tensor"), scatter_dimension=0, tiled=True),
        lax.psum_scatter(grad_experts_part, ("dp", "tensor"), scatter_dimension=0, tiled=True),
        lax.psum_scatter(gate_blocks, ("dp", "tensor"), scatter_dimension=0, tiled=True),
        lax.psum_scatter(up_blocks, ("dp", "tensor"), scatter_dimension=0, tiled=True),
        lax.psum_scatter(down_blocks, ("dp", "tensor"), scatter_dimension=0, tiled=True),
    )
    (
        grad_attention_gain,
        grad_latent_weight,
        grad_latent_gain,
        grad_experts_gain,
        gate_mine,
        up_mine,
        down_mine,
    ) = reduced
    grad_shared_gate = gate_mine[0]
    grad_shared_up = up_mine[0]
    grad_shared_down = down_mine[0]
    return (
        layer_output,
        grad_input,
        grad_attention_gain,
        grad_query_weight,
        grad_latent_weight,
        grad_latent_gain,
        grad_latent_up,
        grad_output_weight,
        grad_experts_gain,
        grad_expert_gate,
        grad_expert_up,
        grad_expert_down,
        grad_shared_gate,
        grad_shared_up,
        grad_shared_down,
    )


def solution(mesh):
    return jax.shard_map(
        local,
        mesh=mesh,
        in_specs=(
            P(("dp", "tensor"), None),
            P("dp", None),
            P(("dp", "tensor"), None),
            P(("dp", "tensor"), None),
            P(("dp", "tensor"), None),
            P("dp"),
            P("dp", "tensor"),
            P("dp", None),
            P("dp"),
            P("dp", "tensor"),
            P("tensor", "dp"),
            P("dp"),
            P("dp", None, "tensor"),
            P("dp", None, "tensor"),
            P("dp", "tensor", None),
            P("dp", None),
            P("dp", None),
            P(None, "dp"),
            P(("dp", "tensor"), None),
        ),
        out_specs=(
            P(("dp", "tensor"), None),
            P(("dp", "tensor"), None),
            P(("dp", "tensor")),
            P("dp", "tensor"),
            P(("dp", "tensor"), None),
            P(("dp", "tensor")),
            P("dp", "tensor"),
            P("tensor", "dp"),
            P(("dp", "tensor")),
            P("dp", None, "tensor"),
            P("dp", None, "tensor"),
            P("dp", "tensor", None),
            P("dp", "tensor"),
            P("dp", "tensor"),
            P("tensor", "dp"),
        ),
        check_vma=False,
    )
```

profile of v0, /device:TPU:0, one launch (start us, length us, event | category | flops | bytes accessed | tf_op | source)
XLA Modules:
  0.0 3529.2 jit_solution(16455610906695932624)
XLA Ops:
  23.4 30.0 scatter_custom_fusion.2
  53.4 7.1 broadcast_in_dim.175
  60.6 7.4 all-to-all-start.2
  69.6 310.3 %all-gather = bf16[8,1,256]{2,1,0:T(2,128)(2,1)S(1)} all-gather(bf16[1,1,256]{2,1,0:T(2,128)(2,1)S(1)} %reshape.567), channel_id=1, replica_groups=mesh['dp'=8,'tensor'=4] {'dp'}, dimensions={0}, use_global_device_ids=true | all-gather | bytes 4608 | tf_op jit(solution)/shard_map/all_gather | solution.py:117
  384.3 97.6 %all-reduce = bf16[512]{0:T(512)(128)(2,1)S(1)} all-reduce(bf16[512]{0:T(512)(128)(2,1)S(1)} %dynamic-update-slice), channel_id=1, replica_groups=mesh['dp'=8,'tensor'=4] {'dp'}, use_global_device_ids=true, to_apply=%add | all-reduce | flops 512 | bytes 2048
  487.8 7.6 all_gather.45
  503.6 5.7 all_gather.49
  509.3 35.9 %all-gather.18.cloned.1.call-done = bf16[2048,768]{1,0:T(8,128)(2,1)} async-done(((bf16[256,768]{1,0:T(8,128)(2,1)}), bf16[2048,768]{1,0:T(8,128)(2,1)}) %all-gather.18.cloned.1.call-update) | async-done | bytes 3145744 | tf_op jit(solution)/shard_map/all_gather | solution.py:118
  556.6 39.5 %all-gather.20.cloned.1.call-done = bf16[512,2048]{1,0:T(8,128)(2,1)} async-done(((bf16[512,256]{1,0:T(8,128)(2,1)}), bf16[512,2048]{1,0:T(8,128)(2,1)}) %all-gather.20.cloned.1.call-update) | async-done | bytes 2097168 | tf_op jit(solution)/shard_map/all_gather | solution.py:122
  596.1 5.1 fusion.110
  601.2 27.8 all-gather.1
  632.6 11.5 reduce-scatter.13.cloned.1.call-done
  646.7 5.9 gather_fusion.2
  656.9 7.1 broadcast_in_dim.169
  664.0 4.7 all-to-all-start
  669.5 18.2 copy.114
  687.7 463.7 %all-to-all-done = bf16[32,120,2048]{2,1,0:T(8,128)(2,1)} async-done(((bf16[32,120,2048]{2,1,0:T(8,128)(2,1)}), bf16[32,120,2048]{2,1,0:T(8,128)(2,1)}, u32[]{:S(2)}, u32[]{:S(2)}) %all-to-all-start) | async-done | bytes 15728672 | tf_op jit(solution)/shard_map/all_to_all | solution.py:69
  1151.5 14.5 copy.107
  1166.0 13.2 fusion.20
  1179.2 10.7 fusion.23
  1189.9 17.8 fusion.3
  1207.7 18.2 fusion.13
  1225.9 19.0 fusion
  1244.9 14.2 copy.117
  1259.1 19.9 copy.118
  1283.6 14.8 convert_bitcast_fusion
  1298.4 14.2 copy.109
  1312.6 19.7 copy.110
  1332.3 433.2 %all-to-all-done.3 = bf16[32,120,2048]{2,1,0:T(8,128)(2,1)} async-done(((bf16[32,120,2048]{2,1,0:T(8,128)(2,1)}), bf16[32,120,2048]{2,1,0:T(8,128)(2,1)}, u32[]{:S(2)}, u32[]{:S(2)}) %all-to-all-start.3) | async-done | bytes 15728672 | tf_op jit(solution)/shard_map/all_to_all | solution.py:81
  1770.5 7.0 fusion.111
  1777.5 7.8 fusion.112
  1785.4 398.5 %all-gather.26.cloned.1.call-done = bf16[2816,2048]{1,0:T(8,128)(2,1)} async-done(((bf16[2816,256]{1,0:T(8,128)(2,1)}), bf16[2816,2048]{1,0:T(8,128)(2,1)}) %all-gather.26.cloned.1.call-update) | async-done | bytes 11534352 | tf_op jit(solution)/shard_map/all_gather | solution.py:126
  2183.8 10.3 multiply_convert_fusion.3
  2194.1 9.3 fusion.113
  2203.4 12.7 convert_reduce_fusion
  2216.1 10.4 gather_fusion.4
  2226.5 26.8 all-to-all-done.1
  2253.3 12.4 convert_reduce_fusion.1
  2265.7 10.5 gather_fusion.3
  2276.1 8.5 broadcast_select_fusion.1
  2284.6 7.8 reshape.478
  2292.4 7.1 reduce_sum.169
  2299.6 9.6 multiply_reduce_fusion.1
  2310.7 18.6 all-gather.28.cloned.1.call-done
  2354.1 5.2 convolution_convert_fusion
  2359.4 9.4 fusion.116
  2368.8 14.6 copy.154
  2383.5 8.1 bitcast_bitcast_fusion
  2391.6 21.5 copy.130
  2417.5 15.0 copy.152
  2432.5 21.8 copy.127
  2458.6 15.1 copy.153
  2473.7 21.6 copy.129
  2501.2 12.2 convolution_bitcast_fusion
  2513.3 12.6 convolution_bitcast_fusion.1
  2525.9 12.4 convolution_bitcast_fusion.2
  2538.4 8.0 reshape.474
  2546.4 6.1 reduce_sum.164
  2552.6 6.9 fusion.29
  2565.6 40.0 %all-reduce.4 = (f32[2048]{0:T(1024)S(1)}, f32[512]{0:T(512)S(1)}, f32[2048]{0:T(1024)S(1)}) all-reduce(f32[2048]{0:T(1024)} %get-tuple-element.64, f32[512]{0:T(512)} %get-tuple-element.77, f32[2048]{0:T(1024)} %get-tuple-element.62), channel_id=5, replica_groups=mesh['dp'=8,'tensor'=4] {'dp','tensor'}, use_global_device_ids=true, to_apply=%region_24.26.clone | all-reduce | flops 4608 | bytes 36864
  2615.5 246.0 %reduce-scatter.29.cloned.1.call-done = f32[1,704,256]{2,1,0:T(8,128)} async-done(((f32[32,704,256]{2,1,0:T(8,128)}), f32[1,704,256]{2,1,0:T(8,128)}) %reduce-scatter.29.cloned.1.call-update) | async-done | bytes 720912 | tf_op jit(solution)/shard_map/reduce_scatter | solution.py:451
  2861.5 254.2 %reduce-scatter.25.cloned.1.call-done = f32[1,256,704]{1,2,0:T(8,128)} async-done(((f32[32,256,704]{1,2,0:T(8,128)}), f32[1,256,704]{1,2,0:T(8,128)}) %reduce-scatter.25.cloned.1.call-update) | async-done | bytes 720912 | tf_op jit(solution)/shard_map/reduce_scatter | solution.py:449
  3115.7 254.2 %reduce-scatter.27.cloned.1.call-done = f32[1,256,704]{1,2,0:T(8,128)} async-done(((f32[32,256,704]{1,2,0:T(8,128)}), f32[1,256,704]{1,2,0:T(8,128)}) %reduce-scatter.27.cloned.1.call-update) | async-done | bytes 720912 | tf_op jit(solution)/shard_map/reduce_scatter | solution.py:450
  3369.9 152.5 %reduce-scatter.19.cloned.1.call-done = f32[64,576]{1,0:T(8,128)} async-done(((f32[2048,576]{1,0:T(8,128)}), f32[64,576]{1,0:T(8,128)}) %reduce-scatter.19.cloned.1.call-update) | async-done | bytes 147472 | tf_op jit(solution)/shard_map/reduce_scatter | solution.py:446
  (341 shorter events, 123.6 us)
Async XLA Ops:
  7.2 1182.7 %copy-start = (bf16[2,352,2048]{2,1,0:T(8,128)(2,1)S(1)}, bf16[2,352,2048]{2,1,0:T(8,128)(2,1)}, u32[]{:S(2)}) copy-start(bf16[2,352,2048]{2,1,0:T(8,128)(2,1)} %param.35) | copy-start | bytes 8650756
  7.2 11.6 copy-start.76
  7.2 11.9 copy-start.17
  9.1 14.3 copy-start.2
  19.1 34.3 copy-start.60
  23.4 37.1 %copy-start.58 = (s32[768]{0:T(1024)}, s32[768]{0:T(1024)S(1)}, u32[]{:S(2)}) copy-start(s32[768]{0:T(1024)S(1)} %gather_fusion.1) | copy-start | bytes 9220
  60.5 9.0 copy-start.86
  60.5 319.4 %copy-start.13 = (bf16[128,2048]{1,0:T(8,128)(2,1)S(1)}, bf16[128,2048]{1,0:T(8,128)(2,1)}, u32[]{:S(2)}) copy-start(bf16[128,2048]{1,0:T(8,128)(2,1)} %param.21) | copy-start | bytes 1572868
  60.5 322.2 %copy-start.89 = (u32[32]{0:T(128)S(1)}, u32[32]{0:T(128)}, u32[]{:S(2)}) copy-start(u32[32]{0:T(128)} %constant.146) | copy-start | bytes 388
  60.5 323.5 %copy-start.87 = (bf16[64]{0:T(256)(128)(2,1)S(1)}, bf16[64]{0:T(256)(128)(2,1)}, u32[]{:S(2)}) copy-start(bf16[64]{0:T(256)(128)(2,1)} %param.29) | copy-start | bytes 388
  60.5 422.8 %copy-start.70 = (s32[1,512]{1,0:T(1,128)S(1)}, s32[1,512]{1,0:T(1,128)}, u32[]{:S(2)}) copy-start(s32[1,512]{1,0:T(1,128)} %param.22) | copy-start | bytes 6148
  60.6 596.4 %all-to-all-start.2 = ((bf16[32,120,2048]{2,1,0:T(8,128)(2,1)}), bf16[32,120,2048]{2,1,0:T(8,128)(2,1)}, u32[]{:S(2)}, u32[]{:S(2)}) async-start(bf16[32,120,2048]{2,1,0:T(8,128)(2,1)} %bitcast.223), calls=%async_computation.3 | async-start | bytes 31457280 | tf_op jit(solution)/shard_map/all_to_all | solution.py:69
  68.0 416.3 %all-gather.12.cloned.1.call-start = ((), (), s32[]{:S(2)}) async-start(), calls=%async_computation.14 | async-start | bytes 2654208 | tf_op jit(solution)/shard_map/all_gather | solution.py:119
  68.7 426.7 %all-gather.14.cloned.1.call-start = ((), (), s32[]{:S(2)}) async-start(), calls=%async_computation.15 | async-start | bytes 1179648 | tf_op jit(solution)/shard_map/all_gather | solution.py:121
  69.5 439.8 %all-gather.16.cloned.1.call-start = ((), (), s32[]{:S(2)}) async-start(), calls=%async_computation.16 | async-start | bytes 2621440 | tf_op jit(solution)/shard_map/all_gather | solution.py:154
  380.1 102.3 %copy-start.71 = (f32[128]{0:T(128)}, f32[128]{0:T(128)S(1)}, u32[]{:S(2)}) copy-start(f32[128]{0:T(128)S(1)} %fusion.94) | copy-start | bytes 1540
  381.5 163.6 %all-gather.18.cloned.1.call-start = ((), (), s32[]{:S(2)}) async-start(), calls=%async_computation.17 | async-start | bytes 3538944 | tf_op jit(solution)/shard_map/all_gather | solution.py:118
  382.1 214.0 %all-gather.20.cloned.1.call-start = ((), (), s32[]{:S(2)}) async-start(), calls=%async_computation.18 | async-start | bytes 2359296 | tf_op jit(solution)/shard_map/all_gather | solution.py:122
  382.7 261.4 %reduce-scatter.13.cloned.1.call-start = ((), (), s32[]{:S(2)}) async-start(), calls=%async_computation.19 | async-start | bytes 5242880 | tf_op jit(solution)/shard_map/reduce_scatter | solution.py:217
  481.9 18.9 copy-start.62
  481.9 20.8 copy-start.72
  483.4 66.3 %copy-start.40 = (f32[512,32]{0,1:T(8,128)}, f32[512,32]{0,1:T(8,128)S(1)}, u32[]{:S(2)}) copy-start(f32[512,32]{0,1:T(8,128)S(1)} %get-tuple-element.102) | copy-start | bytes 196612
  487.6 62.0 %copy-start.74 = (f32[128]{0:T(128)}, f32[128]{0:T(128)S(1)}, u32[]{:S(2)}) copy-start(f32[128]{0:T(128)S(1)} %fusion.95) | copy-start | bytes 1540
  629.0 23.5 copy-start.47
  664.0 487.4 %all-to-all-start = ((bf16[32,120,2048]{2,1,0:T(8,128)(2,1)}), bf16[32,120,2048]{2,1,0:T(8,128)(2,1)}, u32[]{:S(2)}, u32[]{:S(2)}) async-start(bf16[32,120,2048]{2,1,0:T(8,128)(2,1)} %bitcast.224), calls=%async_computation.1 | async-start | bytes 31457280 | tf_op jit(solution)/shard_map/all_to_all | solution.py:69
  668.8 1101.7 %all-gather.22.cloned.1.call-start = ((), (), s32[]{:S(2)}) async-start(), calls=%async_computation.20 | async-start | bytes 12976128 | tf_op jit(solution)/shard_map/all_gather | solution.py:124
  1165.9 13.3 copy-start.12
  1165.9 13.3 copy-start.30
  1207.7 18.2 copy-start.19
  1207.7 18.2 copy-start.21
  1207.7 18.2 copy-start.31
  1279.0 486.5 %all-to-all-start.3 = ((bf16[32,120,2048]{2,1,0:T(8,128)(2,1)}), bf16[32,120,2048]{2,1,0:T(8,128)(2,1)}, u32[]{:S(2)}, u32[]{:S(2)}) async-start(bf16[32,120,2048]{2,1,0:T(8,128)(2,1)} %copy.118), calls=%async_computation.4 | async-start | bytes 31457280 | tf_op jit(solution)/shard_map/all_to_all | solution.py:81
  1282.9 494.7 %all-gather.24.cloned.1.call-start = ((), (), s32[]{:S(2)}) async-start(), calls=%async_computation.21 | async-start | bytes 12976128 | tf_op jit(solution)/shard_map/all_gather | solution.py:125
  1332.3 438.1 %copy-start.3 = (s32[768]{0:T(1024)S(1)}, s32[768]{0:T(1024)}, u32[]{:S(2)}) copy-start(s32[768]{0:T(1024)} %copy-done.2) | copy-start | bytes 9220
  1332.3 438.1 %copy-start.59 = (s32[768]{0:T(1024)S(1)}, s32[768]{0:T(1024)}, u32[]{:S(2)}) copy-start(s32[768]{0:T(1024)} %copy-done.58) | copy-start | bytes 9220
  1332.3 438.2 %copy-start.5 = (bf16[128,2048]{1,0:T(8,128)(2,1)S(1)}, bf16[128,2048]{1,0:T(8,128)(2,1)}, u32[]{:S(2)}) copy-start(bf16[128,2048]{1,0:T(8,128)(2,1)} %copy-done.4) | copy-start | bytes 1572868
  1765.5 487.8 %all-to-all-start.1 = ((bf16[32,120,2048]{2,1,0:T(8,128)(2,1)}), bf16[32,120,2048]{2,1,0:T(8,128)(2,1)}, u32[]{:S(2)}, u32[]{:S(2)}) async-start(bf16[32,120,2048]{2,1,0:T(8,128)(2,1)} %copy.110), calls=%async_computation.2 | async-start | bytes 31457280 | tf_op jit(solution)/shard_map/all_to_all | solution.py:81
  1769.4 414.4 %all-gather.26.cloned.1.call-start = ((), (), s32[]{:S(2)}) async-start(), calls=%async_computation.22 | async-start | bytes 12976128 | tf_op jit(solution)/shard_map/all_gather | solution.py:126
  1770.1 559.2 %all-gather.28.cloned.1.call-start = ((), (), s32[]{:S(2)}) async-start(), calls=%async_computation.23 | async-start | bytes 2621440 | tf_op jit(solution)/shard_map/all_gather | solution.py:319
  1777.5 406.3 %copy-start.18 = (bf16[128,2048]{1,0:T(8,128)(2,1)S(1)}, bf16[128,2048]{1,0:T(8,128)(2,1)}, u32[]{:S(2)}) copy-start(bf16[128,2048]{1,0:T(8,128)(2,1)} %param.39) | copy-start | bytes 1572868
  2194.1 9.3 copy-start.33
  2265.7 10.5 copy-start.61
  2292.4 7.1 copy-start.48
  2292.4 7.1 copy-start.69
  2299.5 9.6 copy-start.83
  2299.5 11.1 copy-start.65
  2299.6 11.1 copy-start.67
  2309.1 23.8 copy-start.16
  2310.4 22.6 copy-start.29
  2310.4 185.2 %reduce-scatter.31.cloned.1.call-start = ((), (), s32[]{:S(2)}) async-start(), calls=%async_computation.32 | async-start | bytes 819200
  2341.1 218.4 %reduce-scatter.21.cloned.1.call-start = ((), (), s32[]{:S(2)}) async-start(), calls=%async_computation.27 | async-start | bytes 1179648 | tf_op jit(solution)/shard_map/reduce_scatter | solution.py:423
  2344.4 216.8 %reduce-scatter.15.cloned.1.call-start = ((), (), s32[]{:S(2)}) async-start(), calls=%async_computation.24 | async-start | bytes 2621440 | tf_op jit(solution)/shard_map/reduce_scatter | solution.py:399
  2349.5 257.8 %reduce-scatter.23.cloned.1.call-start = ((), (), s32[]{:S(2)}) async-start(), calls=%async_computation.28 | async-start | bytes 2359296 | tf_op jit(solution)/shard_map/reduce_scatter | solution.py:426
  2353.8 259.7 %reduce-scatter.17.cloned.1.call-start = ((), (), s32[]{:S(2)}) async-start(), calls=%async_computation.25 | async-start | bytes 3538944 | tf_op jit(solution)/shard_map/reduce_scatter | solution.py:420
  2359.3 502.1 %reduce-scatter.29.cloned.1.call-start = ((), (), s32[]{:S(2)}) async-start(), calls=%async_computation.31 | async-start | bytes 23789568 | tf_op jit(solution)/shard_map/reduce_scatter | solution.py:451
  2413.1 702.6 %reduce-scatter.25.cloned.1.call-start = ((), (), s32[]{:S(2)}) async-start(), calls=%async_computation.29 | async-start | bytes 23789568 | tf_op jit(solution)/shard_map/reduce_scatter | solution.py:449
  2454.3 915.6 %reduce-scatter.27.cloned.1.call-start = ((), (), s32[]{:S(2)}) async-start(), calls=%async_computation.30 | async-start | bytes 23789568 | tf_op jit(solution)/shard_map/reduce_scatter | solution.py:450
  2495.4 1027.1 %reduce-scatter.19.cloned.1.call-start = ((), (), s32[]{:S(2)}) async-start(), calls=%async_computation.26 | async-start | bytes 5406720 | tf_op jit(solution)/shard_map/reduce_scatter | solution.py:446
  2501.2 12.2 copy-start.20
  2513.3 12.6 copy-start.90
  2552.6 8.6 copy-start.14
  2552.6 8.6 copy-start.51
  2559.5 50.3 %copy-start.49 = (f32[8,1,256]{2,1,0:T(1,128)S(1)}, f32[8,1,256]{2,1,0:T(1,128)}, u32[]{:S(2)}) copy-start(f32[8,1,256]{2,1,0:T(1,128)} %copy-done.47) | copy-start | bytes 24580
  2561.2 961.3 %copy-start.1 = (bf16[2,352,2048]{2,1,0:T(8,128)(2,1)S(1)}, bf16[2,352,2048]{2,1,0:T(8,128)(2,1)}, u32[]{:S(2)}) copy-start(bf16[2,352,2048]{2,1,0:T(8,128)(2,1)} %param.35) | copy-start | bytes 8650756
  (50 other events, 130.3 us)
Sparse Core Ops, SparseCore 0:
  70.9 151.0 all-gather.11
  224.1 79.0 all-gather.13
  381.6 101.4 all-gather.15
  485.1 59.9 all-gather.17
  547.0 48.9 all-gather.19
  601.3 42.7 reduce-scatter.12
  671.8 397.1 all-gather.21
  1285.9 397.0 all-gather.23
  1772.2 411.5 all-gather.25
  2310.5 18.7 all-gather.27
  2341.2 22.4 reduce-scatter.30
  2366.9 64.1 reduce-scatter.20
  2433.7 30.1 reduce-scatter.14
  2467.3 68.9 reduce-scatter.22
  2539.7 73.8 reduce-scatter.16
  2616.3 245.1 reduce-scatter.28
  2864.2 251.4 reduce-scatter.24
  3118.4 251.4 reduce-scatter.26
  3372.8 149.5 reduce-scatter.18
where the time goes:
time: 3540 us; the launch traced here: 3530 us
  waiting for transfers between devices  2340 us (66%)
  blocking collectives  489 us (14%)
  local copies, waits for them, and re-layouts  308 us (9%)
  matrix products  248 us (7%)
  other arithmetic  106 us (3%)
    all_to_all x2, waiting for transfers between devices, to_experts(): lax.all_to_all(copies.reshape(dp_count * tensor_count, slot_rows, feature...  464 us
    all_to_all x2, waiting for transfers between devices, from_experts(): lax.all_to_all(partial_rows.astype(jnp.bfloat16), ('dp', 'tensor'), split...  460 us
    all_gather x1, waiting for transfers between devices, local(): lax.all_gather(shared_down, 'dp', axis=1, tiled=True)  398 us
    all_gather x1, blocking collectives, local(): lax.all_gather(attention_gain, 'dp', axis=0, tiled=True)  310 us
    reduce_scatter x1, waiting for transfers between devices, local(): lax.psum_scatter(up_blocks, ('dp', 'tensor'), scatter_dimension=0, tiled=...  254 us
    reduce_scatter x1, waiting for transfers between devices, local(): lax.psum_scatter(gate_blocks, ('dp', 'tensor'), scatter_dimension=0, tile...  254 us
    reduce_scatter x1, waiting for transfers between devices, local(): lax.psum_scatter(down_blocks, ('dp', 'tensor'), scatter_dimension=0, tile...  246 us
    reduce_scatter x1, waiting for transfers between devices, local(): lax.psum_scatter(grad_latent_local, ('dp', 'tensor'), scatter_dimension=0...  152 us
  transfers between devices with their start and end apart: 23, of which 13 were waited for; matrix products, arithmetic and copies ran while one was open for 15% of the time, Pallas kernels for 0%

commit v1 on v0

v1 whole, which is shorter than its diff:
```python
import functools

import jax
import jax.numpy as jnp
from jax import lax
from jax.experimental import pallas as pl
from jax.experimental.pallas import tpu as pltpu
from jax.sharding import PartitionSpec as P

D = 2048
QK_NOPE = 128
QK_ROPE = 64
V_DIM = 128
KV_RANK = 512
TOPK = 6
NORM_EPS = 1e-06

BF = jnp.bfloat16
F32 = jnp.float32
BOTH = ("dp", "tensor")
CORE = 1
GB = 4
LANES = 128
VMEM_CAP = 60 * 1024 * 1024


def round_up(value, step):
    return (value + step - 1) // step * step


def root_norm(values, gain_row):
    factor = lax.rsqrt(jnp.mean(values * values, axis=-1, keepdims=True) + NORM_EPS)
    return values * factor * gain_row


def turn_tables(positions, half_width):
    frequency = 10000.0 ** (-jnp.arange(half_width, dtype=F32) / half_width)
    angles = positions.astype(F32)[:, None] * frequency[None, :]
    return (jnp.cos(angles), jnp.sin(angles))


def rotate(values, cosine, sine_table):
    half_width = values.shape[-1] // 2
    first_half = values[..., :half_width]
    second_half = values[..., half_width:]
    return jnp.concatenate(
        [
            first_half * cosine - second_half * sine_table,
            first_half * sine_table + second_half * cosine,
        ],
        axis=-1,
    )


def dot(left, right, dims=((1,), (0,))):
    return lax.dot_general(left, right, (dims, ((), ())), preferred_element_type=F32)


def swap_with(values, mask, count):
    return lax.ppermute(values, BOTH, [(i, i ^ mask) for i in range(count)])


def cube_gather(block, masks, count):
    for mask in masks:
        block = jnp.concatenate([block, swap_with(block, mask, count)], axis=0)
    return block


def tie(first, second):
    return lax.optimization_barrier((first, second))


def halve_stage(keeps, receiveds, masks, count):
    half = keeps[0].shape[0] // 2
    sent = [
        swap_with((k[half:].astype(F32) + r[half:].astype(F32)).astype(BF), mask, count)
        for k, r, mask in zip(keeps, receiveds, masks)
    ]
    lower = [k[:half].astype(F32) + r[:half].astype(F32) for k, r in zip(keeps, receiveds)]
    return lower, sent


def scatter_rows(partial, masks, count):
    for mask in masks:
        half = partial.shape[0] // 2
        received = swap_with(partial[half:].astype(BF), mask, count)
        partial = partial[:half].astype(F32) + received.astype(F32)
    return partial


def block_order(block, blocks, swapped):
    if not swapped:
        return block
    top, low = block // (blocks // 2), (block // (blocks // 4)) % 2
    return low * (blocks // 2) + top * (blocks // 4) + block % (blocks // 4)


def one_hot(slot_row, rows):
    tokens = lax.broadcasted_iota(jnp.int32, (rows, slot_row.shape[1]), 0)
    return jnp.where(tokens == slot_row, 1.0, 0.0).astype(BF)


def resident(shape):
    return pl.BlockSpec(shape, lambda *_: (0,) * len(shape), pipeline_mode=pl.Buffered(1))


def cotangent_rows(ids, slot_rows, slot_weights, cotangents, down_t, common_down_t):
    groups, _, slots = slot_rows.shape
    experts, _, width = down_t.shape
    cap = slots // experts
    rows = cotangents.shape[0] // groups
    units = common_down_t.shape[1]

    def body(ids_ref, slot_ref, weight_ref, g0, g1, g2, g3, down_ref, common_ref, rows_ref, dh_ref, dhs_ref):
        for k, g_ref in enumerate((g0, g1, g2, g3)):
            value = g_ref[...]
            picked = dot(one_hot(slot_ref[k], rows), value, ((0,), (0,))).astype(BF)
            for j in range(experts):
                rows_ref[j, k * cap : (k + 1) * cap, :] = picked[j * cap : (j + 1) * cap]
            dhs_ref[k * rows : (k + 1) * rows, :] = dot(value, common_ref[...])
        for j in range(experts):
            dh_ref[j] = dot(rows_ref[j], down_ref[j]) * weight_ref[j][:, :1]

    def row_block(k):
        return pl.BlockSpec((rows, D), lambda i, ids: (ids[GB * i + k], 0))

    return pl.pallas_call(
        body,
        grid_spec=pltpu.PrefetchScalarGridSpec(
            num_scalar_prefetch=1,
            grid=(groups // GB,),
            in_specs=[
                pl.BlockSpec((GB, 1, slots), lambda i, ids: (i, 0, 0)),
                pl.BlockSpec((experts, GB * cap, LANES), lambda i, ids: (0, i, 0)),
                *[row_block(k) for k in range(GB)],
                resident(down_t.shape),
                resident(common_down_t.shape),
            ],
            out_specs=[
                pl.BlockSpec((experts, GB * cap, D), lambda i, ids: (0, i, 0)),
                pl.BlockSpec((experts, GB * cap, width), lambda i, ids: (0, i, 0)),
                pl.BlockSpec((GB * rows, units), lambda i, ids: (i, 0)),
            ],
        ),
        out_shape=[
            jax.ShapeDtypeStruct((experts, groups * cap, D), BF),
            jax.ShapeDtypeStruct((experts, groups * cap, width), F32),
            jax.ShapeDtypeStruct((groups * rows, units), F32),
        ],
        compiler_params=pltpu.CompilerParams(vmem_limit_bytes=VMEM_CAP),
        name="cotangent_rows",
    )(ids, slot_rows, slot_weights, *([cotangents] * GB), down_t, common_down_t)


def expert_block(half, streams, order_flags, slot_rows, slot_weights, dh, dhs, weights, previous):
    gate_up, gate_up_t, common_t, common = weights
    groups, _, slots = slot_rows.shape
    experts, _, double = gate_up.shape
    width = double // 2
    cap = slots // experts
    blocks = groups // (2 * GB)
    rows = streams[0].shape[0] // (groups // 2)
    part = streams[0].shape[1]
    units = dhs.shape[1]
    count = len(streams)

    def body(*refs):
        slot_ref, weight_ref, dh_ref, dhs_ref = refs[:4]
        token_refs = refs[4 : 4 + count]
        gu_ref, gut_ref, common_t_ref, common_ref = refs[4 + count : 8 + count]
        x_ref, hidden_ref, dgu_ref, hs_ref, dgs_ref = refs[-(5 + count) : -count]
        out_refs = refs[-count:]
        for k in range(GB):
            picks = one_hot(slot_ref[k], rows)
            for s in range(count):
                picked = dot(
                    picks, token_refs[s][k * rows : (k + 1) * rows, :], ((0,), (0,))
                ).astype(BF)
                for j in range(experts):
                    x_ref[j, k * cap : (k + 1) * cap, s * part : (s + 1) * part] = picked[
                        j * cap : (j + 1) * cap
                    ]
        common_gu = dot(token_refs[0][...], common_t_ref[:part, :])
        for s in range(1, count):
            common_gu += dot(token_refs[s][...], common_t_ref[s * part : (s + 1) * part, :])
        gate, up = common_gu[:, :units], common_gu[:, units:]
        logistic = jax.nn.sigmoid(gate)
        silu = gate * logistic
        hs_ref[...] = (silu * up).astype(BF)
        grad_hidden = dhs_ref[...]
        slope = logistic * (1.0 + gate * (1.0 - logistic))
        dgs_ref[:, :units] = (grad_hidden * up * slope).astype(BF)
        dgs_ref[:, units:] = (grad_hidden * silu).astype(BF)
        grads = []
        for j in range(experts):
            both = dot(x_ref[j], gu_ref[j])
            gate, up = both[:, :width], both[:, width:]
            logistic = jax.nn.sigmoid(gate)
            silu = gate * logistic
            hidden_ref[j] = (silu * up * weight_ref[j][:, :1]).astype(BF)
            grad_hidden = dh_ref[j]
            slope = logistic * (1.0 + gate * (1.0 - logistic))
            dgu_ref[j, :, :width] = (grad_hidden * up * slope).astype(BF)
            dgu_ref[j, :, width:] = (grad_hidden * silu).astype(BF)
            grads.append(dot(dgu_ref[j], gut_ref[j]).astype(BF))
        for k in range(GB):
            picks = one_hot(slot_ref[k], rows)
            stacked = jnp.concatenate([g[k * cap : (k + 1) * cap] for g in grads], axis=0)
            total = dot(picks, stacked) + dot(
                dgs_ref[k * rows : (k + 1) * rows, :], common_ref[...]
            )
            for s in range(count):
                out_refs[s][k * rows : (k + 1) * rows, :] = total[
                    :, s * part : (s + 1) * part
                ].astype(BF)

    shift = half * blocks
    token_specs = [
        pl.BlockSpec((GB * rows, part), functools.partial(lambda f, i: (block_order(i, blocks, f), 0), flag))
        for flag in order_flags
    ]
    in_specs = [
        pl.BlockSpec((GB, 1, slots), lambda i: (shift + i, 0, 0)),
        pl.BlockSpec((experts, GB * cap, LANES), lambda i: (0, shift + i, 0)),
        pl.BlockSpec((experts, GB * cap, width), lambda i: (0, shift + i, 0)),
        pl.BlockSpec((GB * rows, units), lambda i: (shift + i, 0)),
        *token_specs,
        resident(gate_up.shape),
        resident(gate_up_t.shape),
        resident(common_t.shape),
        resident(common.shape),
    ]
    operands = [slot_rows, slot_weights, dh, dhs, *streams, gate_up, gate_up_t, common_t, common]
    aliases = {}
    if previous is not None:
        for at, value in enumerate(previous):
            aliases[len(operands)] = at
            in_specs.append(pl.BlockSpec(memory_space=pl.ANY))
            operands.append(value)
    outs = pl.pallas_call(
        body,
        grid=(blocks,),
        in_specs=in_specs,
        out_specs=[
            pl.BlockSpec((experts, GB * cap, D), lambda i: (0, shift + i, 0)),
            pl.BlockSpec((experts, GB * cap, width), lambda i: (0, shift + i, 0)),
            pl.BlockSpec((experts, GB * cap, double), lambda i: (0, shift + i, 0)),
            pl.BlockSpec((GB * rows, units), lambda i: (shift + i, 0)),
            pl.BlockSpec((GB * rows, 2 * units), lambda i: (shift + i, 0)),
            *token_specs,
        ],
        out_shape=[
            jax.ShapeDtypeStruct((experts, groups * cap, D), BF),
            jax.ShapeDtypeStruct((experts, groups * cap, width), BF),
            jax.ShapeDtypeStruct((experts, groups * cap, double), BF),
            jax.ShapeDtypeStruct((groups * rows, units), BF),
            jax.ShapeDtypeStruct((groups * rows, 2 * units), BF),
            *[jax.ShapeDtypeStruct(s.shape, BF) for s in streams],
        ],
        input_output_aliases=aliases,
        compiler_params=pltpu.CompilerParams(vmem_limit_bytes=VMEM_CAP),
        name="expert_block",
    )(*operands)
    return outs[:5], outs[5:]


def combine_rows(ids, slot_rows, expert_rows, hidden_common, common_down):
    groups, _, slots = slot_rows.shape
    experts = len(expert_rows)
    cap = slots // experts
    rows = hidden_common.shape[0] // groups

    def body(ids_ref, slot_ref, *refs):
        row_refs = refs[:experts]
        hs_ref, down_ref, out_ref = refs[experts:]
        stacked = jnp.concatenate([r[...] for r in row_refs], axis=0)
        total = dot(one_hot(slot_ref[0], rows), stacked) + dot(hs_ref[...], down_ref[...])
        out_ref[...] = total.astype(BF)

    return pl.pallas_call(
        body,
        grid_spec=pltpu.PrefetchScalarGridSpec(
            num_scalar_prefetch=1,
            grid=(groups,),
            in_specs=[
                pl.BlockSpec((1, 1, slots), lambda i, ids: (i, 0, 0)),
                *[pl.BlockSpec((cap, D), lambda i, ids: (i, 0)) for _ in range(experts)],
                pl.BlockSpec((rows, hidden_common.shape[1]), lambda i, ids: (i, 0)),
                resident(common_down.shape),
            ],
            out_specs=pl.BlockSpec((rows, D), lambda i, ids: (ids[i], 0)),
        ),
        out_shape=jax.ShapeDtypeStruct((groups * rows, D), BF),
        compiler_params=pltpu.CompilerParams(vmem_limit_bytes=VMEM_CAP),
        name="combine_rows",
    )(ids, slot_rows, *expert_rows, hidden_common, common_down)


def slot_tables(routes, route_weight, place_order, expert_total, capacity, padded):
    shard_rows = routes.shape[0]
    pair_count = shard_rows * TOPK
    expert_ids = routes.reshape(pair_count)
    ranks = place_order[0]
    earlier = (expert_ids[:, None] == expert_ids[None, :]) & (ranks[None, :] < ranks[:, None])
    places = jnp.sum(earlier.astype(jnp.int32), axis=1)
    slots = jnp.where(places < capacity, expert_ids * padded + places, -1)
    chosen = slots[:, None] == jnp.arange(expert_total * padded, dtype=jnp.int32)[None, :]
    pair_tokens = (jnp.arange(pair_count, dtype=jnp.int32) // TOPK).astype(F32)
    tokens = shard_rows + jnp.sum(
        jnp.where(chosen, pair_tokens[:, None] - shard_rows, 0.0), axis=0
    )
    weights = jnp.sum(jnp.where(chosen, route_weight.reshape(pair_count)[:, None], 0.0), axis=0)
    return jnp.stack([tokens, weights])


def norm_back(values, gain_row, grads):
    factor = lax.rsqrt(jnp.mean(values * values, axis=-1, keepdims=True) + NORM_EPS)
    scaled = gain_row * grads
    inner = jnp.mean(values * scaled, axis=-1, keepdims=True)
    grad_values = factor * scaled - values * (factor * factor * factor) * inner
    grad_gain = jnp.sum(grads * values * factor, axis=0)
    return grad_values, grad_gain


def local(
    layer_input,
    segment_ids,
    routes,
    route_weight,
    place_order,
    attention_gain,
    query_weight,
    latent_weight,
    latent_gain,
    latent_up,
    output_weight,
    experts_gain,
    expert_gate,
    expert_up,
    expert_down,
    shared_gate,
    shared_up,
    shared_down,
    out_cotangent,
):
    tensor_count = lax.axis_size("tensor")
    dp_count = lax.axis_size("dp")
    count = tensor_count * dp_count
    dp_at = lax.axis_index("dp")
    tensor_at = lax.axis_index("tensor")
    me = dp_at * tensor_count + tensor_at
    shard_rows = layer_input.shape[0]
    seq_len = segment_ids.shape[1]
    row_block = D // dp_count
    outer = [1 << b for b in range(count.bit_length() - 2, 0, -1)]
    order_a = tuple(outer)
    order_b = tuple(outer[:-2] + [outer[-1], outer[-2]])
    stream_orders = (order_a, order_b, order_a, order_b)
    order_flags = (False, True, False, True)
    part = D // len(stream_orders)
    tensor_masks = tuple(1 << b for b in range(tensor_count.bit_length() - 2, -1, -1))

    up_split = row_block // latent_up.shape[0]
    latent_pad = round_up(KV_RANK + QK_ROPE + 3, LANES)
    extras = jnp.concatenate(
        [
            latent_weight,
            attention_gain[:, None],
            experts_gain[:, None],
            jnp.broadcast_to(latent_gain[:, None], (latent_gain.shape[0], up_split)).reshape(-1, 1),
            jnp.zeros((row_block, latent_pad - KV_RANK - QK_ROPE - 3), BF),
        ],
        axis=1,
    )
    query_cols = query_weight.shape[1]
    out_cols = output_weight.shape[0]
    up_cols = latent_up.shape[1] // up_split
    packed = jnp.concatenate(
        [query_weight, output_weight.T, latent_up.reshape(row_block, up_cols), extras], axis=1
    )
    packed_full = lax.all_gather(packed, "dp", axis=0, tiled=True)
    hidden_total = shared_gate.shape[1]
    unit_block = hidden_total // tensor_count
    units = unit_block // dp_count
    unit_pad = round_up(units, LANES)
    column = tensor_at * unit_block
    common_send = jnp.stack(
        [
            lax.dynamic_slice_in_dim(shared_gate, column, unit_block, 1).T,
            lax.dynamic_slice_in_dim(shared_up, column, unit_block, 1).T,
            lax.dynamic_slice_in_dim(shared_down, column, unit_block, 0),
        ]
    ).reshape(3, dp_count, units, row_block)
    common_here = lax.all_to_all(
        jnp.transpose(common_send, (1, 0, 2, 3)), "dp", split_axis=0, concat_axis=0, tiled=True
    )
    common_here = jnp.transpose(common_here, (1, 2, 0, 3)).reshape(3, units, D)
    common_here = jnp.pad(common_here, ((0, 0), (0, unit_pad - units), (0, 0)))
    common_gu = common_here[:2].reshape(2 * unit_pad, D)
    common_down = common_here[2]
    common_gu_t = common_gu.T
    common_down_t = common_down.T

    expert_local = expert_gate.shape[0]
    expert_total = expert_local * dp_count
    capacity = max(2, 5 * shard_rows * TOPK // (4 * expert_total))
    padded = round_up(capacity, 16)
    slots = expert_local * padded
    tables = slot_tables(routes, route_weight, place_order, expert_total, capacity, padded)
    tables_all = cube_gather(tables[None], order_a + (CORE,), count)
    tables_mine = lax.dynamic_slice_in_dim(tables_all, dp_at * slots, slots, 2)
    relative = jnp.zeros((count,), jnp.int32)
    canon = jnp.arange(count, dtype=jnp.int32)
    for bit, mask in enumerate(order_a + (CORE,)):
        relative = relative + mask * ((canon >> bit) & 1)
    group_ids = me ^ relative
    slot_rows = tables_mine[:, :1, :].astype(jnp.int32)
    slot_weights = jnp.transpose(
        tables_mine[:, 1, :].reshape(count, expert_local, padded), (1, 0, 2)
    ).reshape(expert_local, count * padded, 1)
    slot_weights = jnp.broadcast_to(slot_weights, (expert_local, count * padded, LANES))

    width = expert_gate.shape[2]
    width_pad = round_up(width, LANES)
    pad_columns = ((0, 0), (0, 0), (0, width_pad - width))
    gate_up = jnp.concatenate(
        [jnp.pad(expert_gate, pad_columns), jnp.pad(expert_up, pad_columns)], axis=2
    )
    gate_up_t = jnp.transpose(gate_up, (0, 2, 1))
    down_pad = jnp.pad(expert_down, ((0, 0), (0, width_pad - width), (0, 0)))
    down_t = jnp.transpose(down_pad, (0, 2, 1))

    input_seq = cube_gather(layer_input, tensor_masks, count)
    ready = (gate_up, gate_up_t, down_pad, down_t, common_gu, common_gu_t, common_down, common_down_t)
    packed_full, (ready, slot_rows, slot_weights, input_seq) = tie(
        packed_full, (ready, slot_rows, slot_weights, input_seq)
    )
    gate_up, gate_up_t, down_pad, down_t, common_gu, common_gu_t, common_down, common_down_t = ready
    at = query_cols
    weight_query = packed_full[:, :at]
    weight_out_t = packed_full[:, at : at + out_cols]
    at += out_cols
    weight_up = packed_full[:, at : at + up_cols].reshape(KV_RANK, up_split * up_cols)
    at += up_cols
    weight_latent = packed_full[:, at : at + KV_RANK + QK_ROPE]
    at += KV_RANK + QK_ROPE
    mixer_scale = packed_full[:, at].astype(F32)
    experts_scale = packed_full[:, at + 1].astype(F32)
    latent_scale = packed_full[:, at + 2].reshape(KV_RANK, up_split)[:, 0].astype(F32)

    input_float = layer_input.astype(F32)
    hops = jnp.zeros((tensor_count,), jnp.int32)
    seq_blocks = jnp.arange(tensor_count, dtype=jnp.int32)
    for bit, mask in enumerate(tensor_masks):
        hops = hops + mask * ((seq_blocks >> bit) & 1)
    block_ids = tensor_at ^ hops
    positions = (
        block_ids[:, None] * shard_rows + jnp.arange(shard_rows, dtype=jnp.int32)[None, :]
    ).reshape(seq_len)
    doc_ids = jnp.take(segment_ids[0].reshape(tensor_count, shard_rows), block_ids, axis=0)
    doc_ids = doc_ids.reshape(seq_len)
    seq_cos, seq_sin = turn_tables(positions, QK_ROPE // 2)
    normed_full = root_norm(input_seq.astype(F32), mixer_scale).astype(BF)
    normed_first = normed_full[:shard_rows]
    latent_all = dot(normed_full, weight_latent)
    latent_full = root_norm(latent_all[:, :KV_RANK], latent_scale).astype(BF)
    rope_full = rotate(latent_all[:, KV_RANK:], seq_cos, seq_sin).astype(BF)
    latent_raw = latent_all[:shard_rows, :KV_RANK]
    head_dim = QK_NOPE + QK_ROPE
    local_heads = query_cols // head_dim
    query_raw = dot(normed_full, weight_query).reshape(seq_len, local_heads, head_dim)
    query_cat = jnp.concatenate(
        [
            query_raw[..., :QK_NOPE],
            rotate(query_raw[..., QK_NOPE:], seq_cos[:, None, :], seq_sin[:, None, :]),
        ],
        axis=-1,
    ).astype(BF)
    key_value = dot(latent_full, weight_up).astype(BF)
    key_value = key_value.reshape(seq_len, local_heads, QK_NOPE + V_DIM)
    key_rows = jnp.concatenate(
        [
            key_value[..., :QK_NOPE],
            jnp.broadcast_to(rope_full[:, None, :], (seq_len, local_heads, QK_ROPE)),
        ],
        axis=-1,
    )
    values = key_value[..., QK_NOPE:]
    scaling = head_dim ** (-0.5)
    raw_scores = jnp.einsum("qhd,khd->hqk", query_cat, key_rows, preferred_element_type=F32)
    raw_scores = raw_scores * scaling
    allowed = (doc_ids[:, None] == doc_ids[None, :]) & (positions[None, :] <= positions[:, None])
    masked = jnp.where(allowed[None], raw_scores, -1e30)
    row_max = jnp.max(masked, axis=-1, keepdims=True)
    exp_terms = jnp.exp(masked - row_max)
    row_total = jnp.sum(exp_terms, axis=-1, keepdims=True)
    prob_rows = exp_terms / row_total
    heads_out = jnp.einsum("hqk,khd->qhd", prob_rows.astype(BF), values, preferred_element_type=F32)
    heads_out = heads_out.astype(BF).reshape(seq_len, local_heads * V_DIM)
    mixer_terms = dot(heads_out, weight_out_t, ((1,), (1,)))
    mixer_out = scatter_rows(mixer_terms, tensor_masks[::-1], count)
    hidden_state = input_float + mixer_out
    normed_second = root_norm(hidden_state, experts_scale).astype(BF)

    cotangent_all = lax.all_gather(out_cotangent, BOTH, axis=0, tiled=True)
    grad_rows, grad_hidden, grad_hidden_common = cotangent_rows(
        group_ids, slot_rows, slot_weights, cotangent_all, down_t, common_down_t
    )

    near = [
        cube_gather(normed_second[:, s * part : (s + 1) * part], order[:-1], count)
        for s, order in enumerate(stream_orders)
    ]
    last = [swap_with(block, order[-1], count) for block, order in zip(near, stream_orders)]
    last, (grad_rows, grad_hidden, grad_hidden_common) = tie(
        last, (grad_rows, grad_hidden, grad_hidden_common)
    )
    near = [jnp.concatenate(pair, axis=0) for pair in zip(near, last)]
    far = [swap_with(block, CORE, count) for block in near]
    expert_weights = (gate_up, gate_up_t, common_gu_t, common_gu)
    kept, far_terms = expert_block(
        1, far, order_flags, slot_rows, slot_weights, grad_hidden, grad_hidden_common,
        expert_weights, None,
    )
    far_received = [swap_with(term, CORE, count) for term in far_terms]
    kept, near_terms = expert_block(
        0, near, order_flags, slot_rows, slot_weights, grad_hidden, grad_hidden_common,
        expert_weights, kept,
    )
    rows_in, hidden_rows, grad_gu, hidden_common, grad_common = kept
    half_rows = count // 2 * shard_rows
    parts = []
    for s, flag in enumerate(order_flags):
        total = 0.0
        for h, tokens in ((0, near[s]), (1, far[s])):
            grads = grad_common[h * half_rows : (h + 1) * half_rows]
            if flag:
                shape = (2, 2, half_rows // 4, 2 * unit_pad)
                grads = jnp.swapaxes(grads.reshape(shape), 0, 1).reshape(half_rows, 2 * unit_pad)
            total = total + dot(grads, tokens, ((0,), (0,)))
        parts.append(total)
    grad_common_gu = jnp.concatenate(parts, axis=1)
    if count > 32:
        near_terms, grad_common_gu = tie(near_terms, grad_common_gu)
    turns = [order[::-1] for order in stream_orders]

    lower, sent = halve_stage(near_terms, far_received, [turn[0] for turn in turns], count)
    expert_rows = [dot(hidden_rows[j], down_pad[j]).astype(BF) for j in range(expert_local)]
    result_terms = combine_rows(group_ids, slot_rows, expert_rows, hidden_common, common_down)
    sent, result_terms = tie(sent, result_terms)

    lower, sent = halve_stage(lower, sent, [turn[1] for turn in turns], count)
    grad_expert_gate = jnp.stack(
        [dot(rows_in[j], grad_gu[j, :, :width], ((0,), (0,))) for j in range(expert_local)]
    )
    sent, grad_expert_gate = tie(sent, grad_expert_gate)
    lower, sent = halve_stage(lower, sent, [turn[2] for turn in turns], count)
    grad_expert_up = jnp.stack(
        [
            dot(rows_in[j], grad_gu[j, :, width_pad : width_pad + width], ((0,), (0,)))
            for j in range(expert_local)
        ]
    )
    sent, grad_expert_up = tie(sent, grad_expert_up)
    for k in range(3, len(order_a)):
        lower, sent = halve_stage(lower, sent, [turn[k] for turn in turns], count)
    grad_normed_second = jnp.concatenate(
        [a + b.astype(F32) for a, b in zip(lower, sent)], axis=1
    )
    grad_expert_down = jnp.stack(
        [dot(hidden_rows[j][:, :width], grad_rows[j], ((0,), (0,))) for j in range(expert_local)]
    )

    canon_ids = jnp.zeros((count,), jnp.int32)
    offset = me ^ canon
    for bit, mask in enumerate(order_a + (CORE,)):
        canon_ids = canon_ids + (1 << bit) * ((offset // mask) & 1)
    hidden_global = jnp.take(
        hidden_common.reshape(count, shard_rows, unit_pad), canon_ids, axis=0
    ).reshape(count * shard_rows, unit_pad)
    if count > 32:
        again, _ = tie(out_cotangent, grad_normed_second)
        cotangent_all = lax.all_gather(again, BOTH, axis=0, tiled=True)
    grad_common_down = dot(hidden_global, cotangent_all, ((0,), (0,)))
    common_grads = jnp.stack(
        [grad_common_gu[:units], grad_common_gu[unit_pad : unit_pad + units], grad_common_down[:units]]
    ).astype(BF)
    common_grads = jnp.transpose(
        common_grads.reshape(3, units, dp_count, row_block), (2, 0, 1, 3)
    )
    common_grads = lax.all_to_all(common_grads, "dp", split_axis=0, concat_axis=0, tiled=True)
    common_grads = jnp.transpose(common_grads, (1, 0, 2, 3)).reshape(3, unit_block, row_block)
    grad_shared_gate = common_grads[0].T.astype(F32)
    grad_shared_up = common_grads[1].T.astype(F32)
    grad_shared_down = common_grads[2].astype(F32)

    if count > 32:
        result_terms, _ = tie(
            result_terms, (grad_normed_second, common_grads, grad_expert_down)
        )
    result = lax.psum_scatter(result_terms, BOTH, scatter_dimension=0, tiled=True)
    cotangent = out_cotangent.astype(F32)
    grad_from_experts, grad_experts_part = norm_back(hidden_state, experts_scale, grad_normed_second)
    grad_hidden_state = cotangent + grad_from_experts
    grad_mixer_full = cube_gather(grad_hidden_state.astype(BF), tensor_masks, count)
    grad_output_t = dot(grad_mixer_full, heads_out, ((0,), (0,)))
    grad_heads = dot(grad_mixer_full, weight_out_t).astype(BF)
    grad_heads = grad_heads.reshape(seq_len, local_heads, V_DIM)
    grad_probs = jnp.einsum("qhd,khd->hqk", grad_heads, values, preferred_element_type=F32)
    row_dot = jnp.sum(prob_rows * grad_probs, axis=-1, keepdims=True)
    grad_scores = (prob_rows * (grad_probs - row_dot)).astype(BF)
    grad_query = scaling * jnp.einsum(
        "hqk,khd->qhd", grad_scores, key_rows, preferred_element_type=F32
    )
    grad_keys = scaling * jnp.einsum(
        "hqk,qhd->khd", grad_scores, query_cat, preferred_element_type=F32
    )
    grad_values = jnp.einsum(
        "hqk,qhd->khd", prob_rows.astype(BF), grad_heads, preferred_element_type=F32
    )
    grad_query_raw = (
        jnp.concatenate(
            [
                grad_query[..., :QK_NOPE],
                rotate(grad_query[..., QK_NOPE:], seq_cos[:, None, :], -seq_sin[:, None, :]),
            ],
            axis=-1,
        )
        .reshape(seq_len, local_heads * head_dim)
        .astype(BF)
    )
    grad_key_value = (
        jnp.concatenate([grad_keys[..., :QK_NOPE], grad_values], axis=-1)
        .reshape(seq_len, local_heads * (QK_NOPE + V_DIM))
        .astype(BF)
    )
    grad_terms = jnp.concatenate(
        [
            dot(grad_query_raw, weight_query, ((1,), (1,))).astype(BF),
            dot(grad_key_value, weight_up, ((1,), (1,))).astype(BF),
            jnp.sum(grad_keys[..., QK_NOPE:], axis=1).astype(BF),
            jnp.zeros((seq_len, QK_ROPE), BF),
        ],
        axis=1,
    )
    grad_shard = scatter_rows(grad_terms, tensor_masks[::-1], count)
    grad_query_local = dot(normed_full, grad_query_raw, ((0,), (0,)))
    grad_up_local = dot(latent_full, grad_key_value, ((0,), (0,)))
    weight_terms = jnp.concatenate(
        [
            grad_query_local.astype(BF),
            grad_output_t.astype(BF),
            grad_up_local.astype(BF).reshape(D, up_cols),
        ],
        axis=1,
    )
    weight_grads = lax.psum_scatter(weight_terms, "dp", scatter_dimension=0, tiled=True)
    weight_grads = weight_grads.astype(F32)
    grad_query_weight = weight_grads[:, :query_cols]
    grad_output_weight = weight_grads[:, query_cols : query_cols + out_cols].T
    grad_latent_up = weight_grads[:, query_cols + out_cols :].reshape(latent_up.shape)

    grad_latent_raw, grad_latent_part = norm_back(
        latent_raw, latent_scale, grad_shard[:, D : D + KV_RANK]
    )
    grad_rope = rotate(
        grad_shard[:, D + KV_RANK : D + KV_RANK + QK_ROPE],
        seq_cos[:shard_rows],
        -seq_sin[:shard_rows],
    )
    grad_latent_all = jnp.concatenate([grad_latent_raw, grad_rope], axis=-1).astype(BF)
    grad_latent_local = dot(normed_first, grad_latent_all, ((0,), (0,)))
    grad_normed_first = grad_shard[:, :D] + dot(grad_latent_all, weight_latent, ((1,), (1,)))
    grad_from_mixer, grad_mixer_part = norm_back(input_float, mixer_scale, grad_normed_first)
    grad_input = grad_hidden_state + grad_from_mixer
    gain_rows = D // KV_RANK
    latent_part = jnp.pad(
        grad_latent_part.reshape(count, KV_RANK // count),
        ((0, 0), (0, (gain_rows - 1) * KV_RANK // count)),
    ).reshape(D, 1)
    small_terms = jnp.concatenate(
        [
            grad_latent_local,
            grad_mixer_part[:, None],
            grad_experts_part[:, None],
            latent_part,
            jnp.zeros((D, latent_pad - KV_RANK - QK_ROPE - 3), F32),
        ],
        axis=1,
    ).astype(BF)
    small_terms = jnp.take(small_terms.reshape(count, D // count, latent_pad), group_ids, axis=0)
    small_grads = scatter_rows(
        small_terms.reshape(D, latent_pad), (CORE,) + order_a[::-1], count
    )
    at = KV_RANK + QK_ROPE
    grad_latent_weight = small_grads[:, :at]
    grad_attention_gain = small_grads[:, at]
    grad_experts_gain = small_grads[:, at + 1]
    grad_latent_gain = small_grads[: KV_RANK // count, at + 2]
    result, grad_input = tie(result, grad_input)
    layer_output = (hidden_state + result.astype(F32)).astype(BF)
    return (
        layer_output,
        grad_input,
        grad_attention_gain,
        grad_query_weight,
        grad_latent_weight,
        grad_latent_gain,
        grad_latent_up,
        grad_output_weight,
        grad_experts_gain,
        grad_expert_gate,
        grad_expert_up,
        grad_expert_down,
        grad_shared_gate,
        grad_shared_up,
        grad_shared_down,
    )


def solution(mesh):
    return jax.shard_map(
        local,
        mesh=mesh,
        in_specs=(
            P(("dp", "tensor"), None),
            P("dp", None),
            P(("dp", "tensor"), None),
            P(("dp", "tensor"), None),
            P(("dp", "tensor"), None),
            P("dp"),
            P("dp", "tensor"),
            P("dp", None),
            P("dp"),
            P("dp", "tensor"),
            P("tensor", "dp"),
            P("dp"),
            P("dp", None, "tensor"),
            P("dp", None, "tensor"),
            P("dp", "tensor", None),
            P("dp", None),
            P("dp", None),
            P(None, "dp"),
            P(("dp", "tensor"), None),
        ),
        out_specs=(
            P(("dp", "tensor"), None),
            P(("dp", "tensor"), None),
            P(("dp", "tensor")),
            P("dp", "tensor"),
            P(("dp", "tensor"), None),
            P(("dp", "tensor")),
            P("dp", "tensor"),
            P("tensor", "dp"),
            P(("dp", "tensor")),
            P("dp", None, "tensor"),
            P("dp", None, "tensor"),
            P("dp", "tensor", None),
            P("dp", "tensor"),
            P("dp", "tensor"),
            P("tensor", "dp"),
        ),
        check_vma=False,
    )
```

time: 3540 us -> 1030 us (0.29)
  waiting for transfers between devices: 2340 us -> 441 us
  blocking collectives: 489 us -> 0 us
  local copies, waits for them, and re-layouts: 308 us -> 142 us
  Pallas kernels: 0 us -> 127 us
  matrix products: 248 us -> 123 us
  starting transfers between devices: 22.1 us -> 71.7 us
    all_to_all x4 -> x2, waiting for transfers between devices: 924 us -> 7.13 us  [the longest x1 7.13 us: local(): lax.all_to_all(jnp.transpose(common_send, (1, 0, 2, 3)), 'dp', split_axis...]
    reduce_scatter x9 -> x2, waiting for transfers between devices: 919 us -> 128 us  [the longest x1 128 us: local(): lax.psum_scatter(result_terms, BOTH, scatter_dimension=0, tiled=True)]
    all_gather x9 -> x2, waiting for transfers between devices: 493 us -> 84.4 us  [the longest x1 84.4 us: local(): packed_full = lax.all_gather(packed, 'dp', axis=0, tiled=True)]
    all_gather x4 -> x0, blocking collectives: 351 us -> none  [the longest x1 310 us: local(): lax.all_gather(attention_gain, 'dp', axis=0, tiled=True)]
    ppermute x0 -> x58, waiting for transfers between devices: none -> 220 us  [swap_with(): return lax.ppermute(values, BOTH, [(i, i ^ mask) for i in range(count)])]
    unnamed x2 -> x0, blocking collectives: 138 us -> none
    pallas_call x0 -> x4, Pallas kernels: none -> 127 us  [the longest x2 72.3 us: expert_block(): pl.pallas_call(body, grid=(blocks,), in_specs=in_specs, out_specs=[pl.Blo...]
    dot_general x36 -> x35, matrix products: 248 us -> 123 us  [the longest x29 117 us: dot(): lax.dot_general(left, right, (dims, ((), ())), preferred_element_type=F32)]
  transfers between devices with their start and end apart: 23 -> 64, of which waited for: 13 -> 38; matrix products, arithmetic and copies ran while one was open for 15% -> 30% of each run, Pallas kernels for 0% -> 9%
where the time goes in v1:
time: 1030 us; the launch traced here: 1020 us
  waiting for transfers between devices  441 us (43%)
  local copies, waits for them, and re-layouts  142 us (14%)
  Pallas kernels  127 us (12%)
  matrix products  123 us (12%)
  other arithmetic  103 us (10%)
  starting transfers between devices  71.7 us (7%)
  between operations  16.6 us (2%)
    ppermute x58, waiting for transfers between devices, swap_with(): return lax.ppermute(values, BOTH, [(i, i ^ mask) for i in range(count)])  220 us
    reduce_scatter x1, waiting for transfers between devices, local(): lax.psum_scatter(result_terms, BOTH, scatter_dimension=0, tiled=True)  128 us
    dot_general x29, matrix products, dot(): lax.dot_general(left, right, (dims, ((), ())), preferred_element_type=F32)  117 us
    all_gather x1, waiting for transfers between devices, local(): packed_full = lax.all_gather(packed, 'dp', axis=0, tiled=True)  84.4 us
    pallas_call x2, Pallas kernels, expert_block(): pl.pallas_call(body, grid=(blocks,), in_specs=in_specs, out_specs=[pl.Blo...  72.3 us
    ppermute x58, starting transfers between devices, swap_with(): return lax.ppermute(values, BOTH, [(i, i ^ mask) for i in range(count)])  61 us
    unnamed x271, local copies, waits for them, and re-layouts  36 us
    pallas_call x1, Pallas kernels, combine_rows(): pl.pallas_call(body, grid_spec=pltpu.PrefetchScalarGridSpec(num_scalar_pr...  29.3 us
  transfers between devices with their start and end apart: 64, of which 38 were waited for; matrix products, arithmetic and copies ran while one was open for 30% of the time, Pallas kernels for 9%

profile of v1, /device:TPU:0, one launch (start us, length us, event | category | flops | bytes accessed | tf_op | source)
XLA Modules:
  0.0 1024.4 jit_solution(3971071648363439318)
XLA Ops:
  18.5 4.1 collective-permute-start
  25.9 4.3 all-to-all-start
  32.2 4.6 copy.264
  37.5 5.3 pad_bitcast_fusion.1
  42.7 7.7 fusion.179
  52.6 13.8 %collective-permute-done.1 = f32[2,2,1024]{2,1,0:T(2,128)S(1)} collective-permute-done((f32[2,2,1024]{2,1,0:T(2,128)S(1)}, f32[2,2,1024]{2,1,0:T(2,128)S(1)}, u32[]{:S(2)}, u32[]{:S(2)}) %collective-permute-start.1) | collective-permute-done | bytes 16416 | tf_op jit(solution)/shard_map/ppermute | solution.py:60
  78.6 7.1 all-to-all-done
  88.3 84.4 %all-gather.3.cloned.1.call-done = bf16[2048,2176]{1,0:T(8,128)(2,1)} async-done(((bf16[256,2176]{1,0:T(8,128)(2,1)}), bf16[2048,2176]{1,0:T(8,128)(2,1)}) %all-gather.3.cloned.1.call-update) | async-done | bytes 8912912 | tf_op jit(solution)/shard_map/all_gather | solution.py:381
  198.8 3.1 convolution_convert_fusion.7
  219.4 12.5 %collective-permute-done.8 = bf16[128,2048]{1,0:T(8,128)(2,1)S(1)} collective-permute-done((bf16[128,2048]{1,0:T(8,128)(2,1)S(1)}, bf16[128,2048]{1,0:T(8,128)(2,1)S(1)}, u32[]{:S(2)}, u32[]{:S(2)}) %collective-permute-start.8) | collective-permute-done | bytes 524320 | tf_op jit(solution)/shard_map/ppermute | solution.py:60
  241.7 19.2 %collective-permute-done.21 = bf16[128,512]{1,0:T(8,128)(2,1)S(1)} collective-permute-done((bf16[128,512]{1,0:T(8,128)(2,1)}, bf16[128,512]{1,0:T(8,128)(2,1)S(1)}, u32[]{:S(2)}, u32[]{:S(2)}) %collective-permute-start.21) | collective-permute-done | bytes 131104 | tf_op jit(solution)/shard_map/ppermute | solution.py:60
  262.0 8.3 collective-permute-done.17
  271.0 6.7 collective-permute-done.13
  277.8 6.3 collective-permute-done.9
  285.8 15.7 %collective-permute-done.22 = bf16[256,512]{1,0:T(8,128)(2,1)S(1)} collective-permute-done((bf16[256,512]{1,0:T(8,128)(2,1)S(1)}, bf16[256,512]{1,0:T(8,128)(2,1)S(1)}, u32[]{:S(2)}, u32[]{:S(2)}) %collective-permute-start.22) | collective-permute-done | bytes 262176 | tf_op jit(solution)/shard_map/ppermute | solution.py:60
  303.1 8.1 collective-permute-done.18
  312.5 4.3 collective-permute-done.14
  317.9 3.7 collective-permute-done.10
  331.7 4.8 collective-permute-done.11
  345.5 25.5 %cotangent_rows.1 = (bf16[2,2048,2048]{2,1,0:T(8,128)(2,1)}, f32[2,2048,384]{2,1,0:T(8,128)}, f32[4096,128]{1,0:T(8,128)}) custom-call(s32[32]{0:T(128)} %fusion.145.ids_ref, s32[32,1,128]{2,1,0:T(1,128)} %get-tuple-element.74.slot_ref.refs_0_, f32[2,2048,128]{2,1,0:T(8,128)} %broadcast_in_dim.150.weight_ref.refs_1_, ...), custom_call_target="tpu_custom_call" | custom-call | tf_op jit(solution)/shard_map/cotangent_rows/pallas_call | solution.py:127
  371.0 9.0 collective-permute-done.16
  390.1 8.6 copy.285.refs_8_
  400.5 36.2 %expert_block.2 = (bf16[2,2048,2048]{2,1,0:T(8,128)(2,1)}, bf16[2,2048,384]{2,1,0:T(8,128)(2,1)}, bf16[2,2048,768]{2,1,0:T(8,128)(2,1)}, bf16[4096,128]{1,0:T(8,...) custom-call(s32[32,1,128]{2,1,0:T(1,128)} %get-tuple-element.74.slot, ...), custom_call_target="tpu_custom_call" | custom-call | tf_op jit(solution)/shard_map/expert_block/pallas_call | solution.py:240
  437.8 36.1 %expert_block.3 = (bf16[2,2048,2048]{2,1,0:T(8,128)(2,1)}, bf16[2,2048,384]{2,1,0:T(8,128)(2,1)}, bf16[2,2048,768]{2,1,0:T(8,128)(2,1)}, bf16[4096,128]{1,0:T(8,...) custom-call(s32[32,1,128]{2,1,0:T(1,128)} %get-tuple-element.74.slot, ...), custom_call_target="tpu_custom_call", output_to_operand_aliasing={{0}: (12, {}), {1}: (13, {}), {2}: (14, {}), {3}: (15, {}),... | custom-call | tf_op jit(solution)/shard_map/expert_block/pallas_call | solution.py:240
  473.9 8.7 fusion.29
  482.7 8.3 convolution_convert_fusion.refs_1_
  491.0 6.6 fusion.35
  497.6 3.6 convert_add_fusion.2
  502.4 3.6 convert_add_fusion.3
  506.9 4.0 convert_add_fusion.4
  512.6 3.9 convert_add_fusion.5
  516.7 6.8 convolution_convert_fusion.1.refs_0_
  523.5 29.3 %combine_rows.1 = bf16[4096,2048]{1,0:T(8,128)(2,1)} custom-call(s32[32]{0:T(128)} %fusion.145.ids_ref, s32[32,1,128]{2,1,0:T(1,128)} %get-tuple-element.74.slot_ref.refs_0_, bf16[2048,2048]{1,0:T(8,128)(2,1)} %convolution_convert_fusion.1.refs_0_, bf16[2048,2048]{1,0:T(8,128)(2,1)} %convolution_convert_fusion.refs_1_, ...), custom_call_target="tpu_custom_call" | custom-call | tf_op jit(solution)/shard_map/combine_rows/pallas_call | solution.py:280
  552.9 6.5 fusion.26
  571.0 4.8 fusion.32
  579.4 6.2 collective-permute-done.37
  597.8 5.6 collective-permute-done.42
  603.4 5.3 collective-permute-done.41
  611.5 3.4 collective-permute-start.45
  618.2 10.6 %collective-permute-done.45 = bf16[128,512]{1,0:T(8,128)(2,1)S(1)} collective-permute-done((bf16[128,512]{1,0:T(8,128)(2,1)S(1)}, bf16[128,512]{1,0:T(8,128)(2,1)S(1)}, u32[]{:S(2)}, u32[]{:S(2)}) %collective-permute-start.45) | collective-permute-done | bytes 131104 | tf_op jit(solution)/shard_map/ppermute | solution.py:60
  637.1 11.0 %collective-permute-done.49 = bf16[128,2048]{1,0:T(8,128)(2,1)S(1)} collective-permute-done((bf16[128,2048]{1,0:T(8,128)(2,1)S(1)}, bf16[128,2048]{1,0:T(8,128)(2,1)S(1)}, u32[]{:S(2)}, u32[]{:S(2)}) %collective-permute-start.49) | collective-permute-done | bytes 524320 | tf_op jit(solution)/shard_map/ppermute | solution.py:60
  652.3 3.5 fusion.72
  678.3 11.3 %pad_maximum_fusion = bf16[2048,1536]{0,1:T(8,128)(2,1)} fusion(bf16[2048,256]{0,1:T(8,128)(2,1)S(1)} %copy-done.24, bf16[2048,512]{0,1:T(8,128)(2,1)S(1)} %convolution_convert_fusion.4, bf16[2048,768]{0,1:T(8,128)(2,1)S(1)} %convolution_convert_fusion.2), kind=kLoop, calls=%fused_computation.29 | loop fusion | flops 18874368 | bytes 12582912 | tf_op jit(solution)/shard_map/concatenate | solution.py:649
  707.0 3.2 fusion.187
  716.3 3.1 convolution_add_fusion.1
  724.3 3.2 convolution_convert_fusion.9
  727.5 5.3 convolution_convert_fusion.5
  733.4 5.2 concatenate.186
  743.2 8.4 fusion.188
  757.3 5.7 all-to-all-start.1
  763.0 3.9 slice_bitcast_fusion.1
  767.9 4.8 collective-permute-done.52
  776.7 3.3 convolution_convert_fusion.3
  780.0 4.4 copy.296
  784.5 4.6 fusion.81
  792.9 6.6 concatenate.192
  799.5 4.1 gather_fusion.1
  807.1 5.8 fusion.38
  813.0 5.7 fusion.41
  828.6 23.5 %collective-permute-done.54 = bf16[512,640]{1,0:T(8,128)(2,1)} collective-permute-done((bf16[512,640]{1,0:T(8,128)(2,1)}, bf16[512,640]{1,0:T(8,128)(2,1)}, u32[]{:S(2)}, u32[]{:S(2)}) %collective-permute-start.54) | collective-permute-done | bytes 655392 | tf_op jit(solution)/shard_map/ppermute | solution.py:60
  855.3 9.7 collective-permute-done.55
  868.1 5.0 collective-permute-done.56
  873.2 5.8 collective-permute-start.57
  887.8 127.9 %reduce-scatter.3.cloned.1.call-done = bf16[128,2048]{1,0:T(8,128)(2,1)} async-done(((bf16[4096,2048]{1,0:T(8,128)(2,1)}), bf16[128,2048]{1,0:T(8,128)(2,1)}) %reduce-scatter.3.cloned.1.call-update) | async-done | bytes 524304 | tf_op jit(solution)/shard_map/reduce_scatter | solution.py:601
  (583 shorter events, 276.3 us)
Async XLA Ops:
  7.2 165.5 %all-gather.3.cloned.1.call-start = ((), (), s32[]{:S(2)}) async-start(), calls=%async_computation.4 | async-start | bytes 10027008 | tf_op jit(solution)/shard_map/all_gather | solution.py:381
  15.9 329.6 %all-gather.5.cloned.1.call-start = ((), (), s32[]{:S(2)}) async-start(), calls=%async_computation.5 | async-start | bytes 17301504 | tf_op jit(solution)/shard_map/all_gather | solution.py:505
  18.5 32.0 %collective-permute-start = (f32[1,2,1024]{2,1,0:T(2,128)S(1)}, f32[1,2,1024]{2,1,0:T(2,128)S(1)}, u32[]{:S(2)}, u32[]{:S(2)}) collective-permute-start(f32[1,2,1024]{2,1,0:T(2,128)S(1)} %maximum_bitcast_fusion.2), channel_id=1, source_target_pairs={{0,16},{1,17},{2,18},{3,19},{4,20},{5,21},{6,22},{7,23},{8,24},{9,... | collective-permute-start | bytes 24584 | tf_op jit(solution)/shard_map/ppermute | solution.py:60
  25.9 59.9 %all-to-all-start = ((bf16[8,3,88,256]{3,2,1,0:T(8,128)(2,1)}), bf16[8,3,88,256]{3,2,1,0:T(8,128)(2,1)}, u32[]{:S(2)}, u32[]{:S(2)}) async-start(bf16[8,3,88,256]{3,2,1,0:T(8,128)(2,1)} %copy.267), calls=%async_computation | async-start | bytes 2162688 | tf_op jit(solution)/shard_map/all_to_all | solution.py:394
  30.2 853.4 %reduce-scatter.5.cloned.1.call-start = ((), (), s32[]{:S(2)}) async-start(), calls=%async_computation.7 | async-start | bytes 7077888 | tf_op jit(solution)/shard_map/reduce_scatter | solution.py:657
  30.7 21.8 %collective-permute-start.5 = (bf16[128,2048]{1,0:T(8,128)(2,1)S(1)}, bf16[128,2048]{1,0:T(8,128)(2,1)S(1)}, u32[]{:S(2)}, u32[]{:S(2)}) collective-permute-start(bf16[128,2048]{1,0:T(8,128)(2,1)S(1)} %copy-done.12), channel_id=1, source_target_pairs={{0,2},{1,3},{2,0},{3,1},{4,6},{5,7},{6,4},{7,5},{8,10},{9,11},{10,... | collective-permute-start | bytes 1572872 | tf_op jit(solution)/shard_map/ppermute | solution.py:60
  50.6 15.9 %collective-permute-start.1 = (f32[2,2,1024]{2,1,0:T(2,128)S(1)}, f32[2,2,1024]{2,1,0:T(2,128)S(1)}, u32[]{:S(2)}, u32[]{:S(2)}) collective-permute-start(f32[2,2,1024]{2,1,0:T(2,128)S(1)} %pad_maximum_fusion.41), channel_id=1, source_target_pairs={{0,8},{1,9},{2,10},{3,11},{4,12},{5,13},{6,14},{7,15},{8,0},{9,1},... | collective-permute-start | bytes 49160 | tf_op jit(solution)/shard_map/ppermute | solution.py:60
  52.6 24.6 %collective-permute-start.6 = (bf16[256,2048]{1,0:T(8,128)(2,1)S(1)}, bf16[256,2048]{1,0:T(8,128)(2,1)}, u32[]{:S(2)}, u32[]{:S(2)}) collective-permute-start(bf16[256,2048]{1,0:T(8,128)(2,1)S(1)} %pad_maximum_fusion.6), channel_id=1, source_target_pairs={{0,1},{1,0},{2,3},{3,2},{4,5},{5,4},{6,7},{7,6},{8,9},{9,8},{10,11... | collective-permute-start | bytes 3145736 | tf_op jit(solution)/shard_map/ppermute | solution.py:60
  66.5 4.0 collective-permute-start.2
  70.5 4.3 collective-permute-start.3
  74.9 1.4 collective-permute-start.4
  214.7 2.7 collective-permute-start.7
  217.9 14.0 %collective-permute-start.8 = (bf16[128,2048]{1,0:T(8,128)(2,1)S(1)}, bf16[128,2048]{1,0:T(8,128)(2,1)S(1)}, u32[]{:S(2)}, u32[]{:S(2)}) collective-permute-start(bf16[128,2048]{1,0:T(8,128)(2,1)S(1)} %slice.996), channel_id=1, source_target_pairs={{0,2},{1,3},{2,0},{3,1},{4,6},{5,7},{6,4},{7,5},{8,10},{9,11},{10,... | collective-permute-start | bytes 1572872 | tf_op jit(solution)/shard_map/ppermute | solution.py:60
  234.3 26.6 %collective-permute-start.21 = (bf16[128,512]{1,0:T(8,128)(2,1)}, bf16[128,512]{1,0:T(8,128)(2,1)S(1)}, u32[]{:S(2)}, u32[]{:S(2)}) collective-permute-start(bf16[128,512]{1,0:T(8,128)(2,1)} %get-tuple-element.291), channel_id=1, source_target_pairs={{0,16},{1,17},{2,18},{3,19},{4,20},{5,21},{6,22},{7,23},{8,24},{9,... | collective-permute-start | bytes 393224 | tf_op jit(solution)/shard_map/ppermute | solution.py:60
  236.0 34.2 %collective-permute-start.17 = (bf16[128,512]{1,0:T(8,128)(2,1)S(1)}, bf16[128,512]{1,0:T(8,128)(2,1)S(1)}, u32[]{:S(2)}, u32[]{:S(2)}) collective-permute-start(bf16[128,512]{1,0:T(8,128)(2,1)S(1)} %get-tuple-element.292), channel_id=1, source_target_pairs={{0,16},{1,17},{2,18},{3,19},{4,20},{5,21},{6,22},{7,23},{8,24},{9,... | collective-permute-start | bytes 393224 | tf_op jit(solution)/shard_map/ppermute | solution.py:60
  238.7 39.0 %collective-permute-start.13 = (bf16[128,512]{1,0:T(8,128)(2,1)S(1)}, bf16[128,512]{1,0:T(8,128)(2,1)S(1)}, u32[]{:S(2)}, u32[]{:S(2)}) collective-permute-start(bf16[128,512]{1,0:T(8,128)(2,1)S(1)} %get-tuple-element.293), channel_id=1, source_target_pairs={{0,16},{1,17},{2,18},{3,19},{4,20},{5,21},{6,22},{7,23},{8,24},{9,... | collective-permute-start | bytes 393224 | tf_op jit(solution)/shard_map/ppermute | solution.py:60
  240.5 43.7 %collective-permute-start.9 = (bf16[128,512]{1,0:T(8,128)(2,1)S(1)}, bf16[128,512]{1,0:T(8,128)(2,1)S(1)}, u32[]{:S(2)}, u32[]{:S(2)}) collective-permute-start(bf16[128,512]{1,0:T(8,128)(2,1)S(1)} %get-tuple-element.294), channel_id=1, source_target_pairs={{0,16},{1,17},{2,18},{3,19},{4,20},{5,21},{6,22},{7,23},{8,24},{9,... | collective-permute-start | bytes 393224 | tf_op jit(solution)/shard_map/ppermute | solution.py:60
  261.9 39.7 %collective-permute-start.22 = (bf16[256,512]{1,0:T(8,128)(2,1)S(1)}, bf16[256,512]{1,0:T(8,128)(2,1)S(1)}, u32[]{:S(2)}, u32[]{:S(2)}) collective-permute-start(bf16[256,512]{1,0:T(8,128)(2,1)S(1)} %pad_maximum_fusion.32), channel_id=1, source_target_pairs={{0,8},{1,9},{2,10},{3,11},{4,12},{5,13},{6,14},{7,15},{8,0},{9,1},... | collective-permute-start | bytes 786440 | tf_op jit(solution)/shard_map/ppermute | solution.py:60
  270.9 40.3 %collective-permute-start.18 = (bf16[256,512]{1,0:T(8,128)(2,1)S(1)}, bf16[256,512]{1,0:T(8,128)(2,1)S(1)}, u32[]{:S(2)}, u32[]{:S(2)}) collective-permute-start(bf16[256,512]{1,0:T(8,128)(2,1)S(1)} %pad_maximum_fusion.31), channel_id=1, source_target_pairs={{0,8},{1,9},{2,10},{3,11},{4,12},{5,13},{6,14},{7,15},{8,0},{9,1},... | collective-permute-start | bytes 786440 | tf_op jit(solution)/shard_map/ppermute | solution.py:60
  277.8 39.1 %collective-permute-start.14 = (bf16[256,512]{1,0:T(8,128)(2,1)S(1)}, bf16[256,512]{1,0:T(8,128)(2,1)S(1)}, u32[]{:S(2)}, u32[]{:S(2)}) collective-permute-start(bf16[256,512]{1,0:T(8,128)(2,1)S(1)} %pad_maximum_fusion.30), channel_id=1, source_target_pairs={{0,8},{1,9},{2,10},{3,11},{4,12},{5,13},{6,14},{7,15},{8,0},{9,1},... | collective-permute-start | bytes 786440 | tf_op jit(solution)/shard_map/ppermute | solution.py:60
  284.2 37.4 %collective-permute-start.10 = (bf16[256,512]{1,0:T(8,128)(2,1)S(1)}, bf16[256,512]{1,0:T(8,128)(2,1)S(1)}, u32[]{:S(2)}, u32[]{:S(2)}) collective-permute-start(bf16[256,512]{1,0:T(8,128)(2,1)S(1)} %pad_maximum_fusion.29), channel_id=1, source_target_pairs={{0,8},{1,9},{2,10},{3,11},{4,12},{5,13},{6,14},{7,15},{8,0},{9,1},... | collective-permute-start | bytes 786440 | tf_op jit(solution)/shard_map/ppermute | solution.py:60
  302.6 21.0 %collective-permute-start.23 = (bf16[512,512]{1,0:T(8,128)(2,1)S(1)}, bf16[512,512]{1,0:T(8,128)(2,1)S(1)}, u32[]{:S(2)}, u32[]{:S(2)}) collective-permute-start(bf16[512,512]{1,0:T(8,128)(2,1)S(1)} %pad_maximum_fusion.26), channel_id=1, source_target_pairs={{0,2},{1,3},{2,0},{3,1},{4,6},{5,7},{6,4},{7,5},{8,10},{9,11},{10,... | collective-permute-start | bytes 1572872 | tf_op jit(solution)/shard_map/ppermute | solution.py:60
  311.2 15.1 %collective-permute-start.19 = (bf16[512,512]{1,0:T(8,128)(2,1)S(1)}, bf16[512,512]{1,0:T(8,128)(2,1)S(1)}, u32[]{:S(2)}, u32[]{:S(2)}) collective-permute-start(bf16[512,512]{1,0:T(8,128)(2,1)S(1)} %pad_maximum_fusion.25), channel_id=1, source_target_pairs={{0,4},{1,5},{2,6},{3,7},{4,0},{5,1},{6,2},{7,3},{8,12},{9,13},{10,... | collective-permute-start | bytes 1572872 | tf_op jit(solution)/shard_map/ppermute | solution.py:60
  316.9 12.7 %collective-permute-start.15 = (bf16[512,512]{1,0:T(8,128)(2,1)S(1)}, bf16[512,512]{1,0:T(8,128)(2,1)S(1)}, u32[]{:S(2)}, u32[]{:S(2)}) collective-permute-start(bf16[512,512]{1,0:T(8,128)(2,1)S(1)} %pad_maximum_fusion.24), channel_id=1, source_target_pairs={{0,2},{1,3},{2,0},{3,1},{4,6},{5,7},{6,4},{7,5},{8,10},{9,11},{10,... | collective-permute-start | bytes 1572872 | tf_op jit(solution)/shard_map/ppermute | solution.py:60
  321.7 14.9 %collective-permute-start.11 = (bf16[512,512]{1,0:T(8,128)(2,1)S(1)}, bf16[512,512]{1,0:T(8,128)(2,1)S(1)}, u32[]{:S(2)}, u32[]{:S(2)}) collective-permute-start(bf16[512,512]{1,0:T(8,128)(2,1)S(1)} %pad_maximum_fusion.23), channel_id=1, source_target_pairs={{0,4},{1,5},{2,6},{3,7},{4,0},{5,1},{6,2},{7,3},{8,12},{9,13},{10,... | collective-permute-start | bytes 1572872 | tf_op jit(solution)/shard_map/ppermute | solution.py:60
  325.5 45.4 %collective-permute-start.24 = (bf16[1024,512]{1,0:T(8,128)(2,1)}, bf16[1024,512]{1,0:T(8,128)(2,1)}, u32[]{:S(2)}, u32[]{:S(2)}) collective-permute-start(bf16[1024,512]{1,0:T(8,128)(2,1)} %pad_maximum_fusion.10), channel_id=1, source_target_pairs={{0,4},{1,5},{2,6},{3,7},{4,0},{5,1},{6,2},{7,3},{8,12},{9,13},{10,... | collective-permute-start | bytes 3145736 | tf_op jit(solution)/shard_map/ppermute | solution.py:60
  327.4 43.5 %collective-permute-start.20 = (bf16[1024,512]{1,0:T(8,128)(2,1)}, bf16[1024,512]{1,0:T(8,128)(2,1)}, u32[]{:S(2)}, u32[]{:S(2)}) collective-permute-start(bf16[1024,512]{1,0:T(8,128)(2,1)} %pad_maximum_fusion.9), channel_id=1, source_target_pairs={{0,2},{1,3},{2,0},{3,1},{4,6},{5,7},{6,4},{7,5},{8,10},{9,11},{10,... | collective-permute-start | bytes 3145736 | tf_op jit(solution)/shard_map/ppermute | solution.py:60
  330.6 49.4 %collective-permute-start.16 = (bf16[1024,512]{1,0:T(8,128)(2,1)}, bf16[1024,512]{1,0:T(8,128)(2,1)}, u32[]{:S(2)}, u32[]{:S(2)}) collective-permute-start(bf16[1024,512]{1,0:T(8,128)(2,1)} %pad_maximum_fusion.8), channel_id=1, source_target_pairs={{0,4},{1,5},{2,6},{3,7},{4,0},{5,1},{6,2},{7,3},{8,12},{9,13},{10,... | collective-permute-start | bytes 3145736 | tf_op jit(solution)/shard_map/ppermute | solution.py:60
  337.6 42.4 %collective-permute-start.12 = (bf16[1024,512]{1,0:T(8,128)(2,1)}, bf16[1024,512]{1,0:T(8,128)(2,1)}, u32[]{:S(2)}, u32[]{:S(2)}) collective-permute-start(bf16[1024,512]{1,0:T(8,128)(2,1)} %pad_maximum_fusion.7), channel_id=1, source_target_pairs={{0,2},{1,3},{2,0},{3,1},{4,6},{5,7},{6,4},{7,5},{8,10},{9,11},{10,... | collective-permute-start | bytes 3145736 | tf_op jit(solution)/shard_map/ppermute | solution.py:60
  382.3 18.2 %collective-permute-start.28 = (bf16[2048,512]{1,0:T(8,128)(2,1)}, bf16[2048,512]{1,0:T(8,128)(2,1)}, u32[]{:S(2)}, u32[]{:S(2)}) collective-permute-start(bf16[2048,512]{1,0:T(8,128)(2,1)} %constant_dynamic-update-slice_fusion.26.refs_7_), channel_id=1, source_target_pairs={{0,1},{1,0},{2,3},{3,2},{4,5},{5,4},{6,7},{7,6},{8,9},{9,8},{10,11... | collective-permute-start | bytes 6291464 | tf_op jit(solution)/shard_map/ppermute | solution.py:60
  384.5 15.9 %collective-permute-start.27 = (bf16[2048,512]{1,0:T(8,128)(2,1)}, bf16[2048,512]{1,0:T(8,128)(2,1)}, u32[]{:S(2)}, u32[]{:S(2)}) collective-permute-start(bf16[2048,512]{1,0:T(8,128)(2,1)} %constant_dynamic-update-slice_fusion.21.refs_6_), channel_id=1, source_target_pairs={{0,1},{1,0},{2,3},{3,2},{4,5},{5,4},{6,7},{7,6},{8,9},{9,8},{10,11... | collective-permute-start | bytes 6291464 | tf_op jit(solution)/shard_map/ppermute | solution.py:60
  387.3 13.1 %collective-permute-start.26 = (bf16[2048,512]{1,0:T(8,128)(2,1)}, bf16[2048,512]{1,0:T(8,128)(2,1)}, u32[]{:S(2)}, u32[]{:S(2)}) collective-permute-start(bf16[2048,512]{1,0:T(8,128)(2,1)} %constant_dynamic-update-slice_fusion.16.refs_5_), channel_id=1, source_target_pairs={{0,1},{1,0},{2,3},{3,2},{4,5},{5,4},{6,7},{7,6},{8,9},{9,8},{10,11... | collective-permute-start | bytes 6291464 | tf_op jit(solution)/shard_map/ppermute | solution.py:60
  389.6 10.9 %collective-permute-start.25 = (bf16[2048,512]{1,0:T(8,128)(2,1)}, bf16[2048,512]{1,0:T(8,128)(2,1)}, u32[]{:S(2)}, u32[]{:S(2)}) collective-permute-start(bf16[2048,512]{1,0:T(8,128)(2,1)} %constant_dynamic-update-slice_fusion.11.refs_4_), channel_id=1, source_target_pairs={{0,1},{1,0},{2,3},{3,2},{4,5},{5,4},{6,7},{7,6},{8,9},{9,8},{10,11... | collective-permute-start | bytes 6291464 | tf_op jit(solution)/shard_map/ppermute | solution.py:60
  436.7 60.9 %collective-permute-start.35 = (bf16[2048,512]{1,0:T(8,128)(2,1)}, bf16[2048,512]{1,0:T(8,128)(2,1)}, u32[]{:S(2)}, u32[]{:S(2)}) collective-permute-start(bf16[2048,512]{1,0:T(8,128)(2,1)} %get-tuple-element.103), channel_id=1, source_target_pairs={{0,1},{1,0},{2,3},{3,2},{4,5},{5,4},{6,7},{7,6},{8,9},{9,8},{10,11... | collective-permute-start | bytes 6291464 | tf_op jit(solution)/shard_map/ppermute | solution.py:60
  436.8 65.7 %collective-permute-start.33 = (bf16[2048,512]{1,0:T(8,128)(2,1)}, bf16[2048,512]{1,0:T(8,128)(2,1)}, u32[]{:S(2)}, u32[]{:S(2)}) collective-permute-start(bf16[2048,512]{1,0:T(8,128)(2,1)} %get-tuple-element.101), channel_id=1, source_target_pairs={{0,1},{1,0},{2,3},{3,2},{4,5},{5,4},{6,7},{7,6},{8,9},{9,8},{10,11... | collective-permute-start | bytes 6291464 | tf_op jit(solution)/shard_map/ppermute | solution.py:60
  437.3 69.6 %collective-permute-start.31 = (bf16[2048,512]{1,0:T(8,128)(2,1)}, bf16[2048,512]{1,0:T(8,128)(2,1)}, u32[]{:S(2)}, u32[]{:S(2)}) collective-permute-start(bf16[2048,512]{1,0:T(8,128)(2,1)} %get-tuple-element.99), channel_id=1, source_target_pairs={{0,1},{1,0},{2,3},{3,2},{4,5},{5,4},{6,7},{7,6},{8,9},{9,8},{10,11... | collective-permute-start | bytes 6291464 | tf_op jit(solution)/shard_map/ppermute | solution.py:60
  437.3 75.2 %collective-permute-start.29 = (bf16[2048,512]{1,0:T(8,128)(2,1)}, bf16[2048,512]{1,0:T(8,128)(2,1)}, u32[]{:S(2)}, u32[]{:S(2)}) collective-permute-start(bf16[2048,512]{1,0:T(8,128)(2,1)} %get-tuple-element.97), channel_id=1, source_target_pairs={{0,1},{1,0},{2,3},{3,2},{4,5},{5,4},{6,7},{7,6},{8,9},{9,8},{10,11... | collective-permute-start | bytes 6291464 | tf_op jit(solution)/shard_map/ppermute | solution.py:60
  501.2 58.1 %collective-permute-start.36 = (bf16[1024,512]{1,0:T(8,128)(2,1)S(1)}, bf16[1024,512]{1,0:T(8,128)(2,1)}, u32[]{:S(2)}, u32[]{:S(2)}) collective-permute-start(bf16[1024,512]{1,0:T(8,128)(2,1)S(1)} %get-tuple-element.244), channel_id=1, source_target_pairs={{0,4},{1,5},{2,6},{3,7},{4,0},{5,1},{6,2},{7,3},{8,12},{9,13},{10,... | collective-permute-start | bytes 3145736 | tf_op jit(solution)/shard_map/ppermute | solution.py:60
  506.0 53.3 %collective-permute-start.34 = (bf16[1024,512]{1,0:T(8,128)(2,1)S(1)}, bf16[1024,512]{1,0:T(8,128)(2,1)}, u32[]{:S(2)}, u32[]{:S(2)}) collective-permute-start(bf16[1024,512]{1,0:T(8,128)(2,1)S(1)} %get-tuple-element.238), channel_id=1, source_target_pairs={{0,2},{1,3},{2,0},{3,1},{4,6},{5,7},{6,4},{7,5},{8,10},{9,11},{10,... | collective-permute-start | bytes 3145736 | tf_op jit(solution)/shard_map/ppermute | solution.py:60
  510.8 48.5 %collective-permute-start.32 = (bf16[1024,512]{1,0:T(8,128)(2,1)}, bf16[1024,512]{1,0:T(8,128)(2,1)}, u32[]{:S(2)}, u32[]{:S(2)}) collective-permute-start(bf16[1024,512]{1,0:T(8,128)(2,1)} %get-tuple-element.240), channel_id=1, source_target_pairs={{0,4},{1,5},{2,6},{3,7},{4,0},{5,1},{6,2},{7,3},{8,12},{9,13},{10,... | collective-permute-start | bytes 3145736 | tf_op jit(solution)/shard_map/ppermute | solution.py:60
  516.5 42.9 %collective-permute-start.30 = (bf16[1024,512]{1,0:T(8,128)(2,1)}, bf16[1024,512]{1,0:T(8,128)(2,1)}, u32[]{:S(2)}, u32[]{:S(2)}) collective-permute-start(bf16[1024,512]{1,0:T(8,128)(2,1)} %get-tuple-element.242), channel_id=1, source_target_pairs={{0,2},{1,3},{2,0},{3,1},{4,6},{5,7},{6,4},{7,5},{8,10},{9,11},{10,... | collective-permute-start | bytes 3145736 | tf_op jit(solution)/shard_map/ppermute | solution.py:60
  561.5 17.2 %collective-permute-start.39 = (bf16[512,512]{1,0:T(8,128)(2,1)S(1)}, bf16[512,512]{1,0:T(8,128)(2,1)S(1)}, u32[]{:S(2)}, u32[]{:S(2)}) collective-permute-start(bf16[512,512]{1,0:T(8,128)(2,1)S(1)} %get-tuple-element.248), channel_id=1, source_target_pairs={{0,4},{1,5},{2,6},{3,7},{4,0},{5,1},{6,2},{7,3},{8,12},{9,13},{10,... | collective-permute-start | bytes 1572872 | tf_op jit(solution)/shard_map/ppermute | solution.py:60
  564.5 14.9 %collective-permute-start.38 = (bf16[512,512]{1,0:T(8,128)(2,1)S(1)}, bf16[512,512]{1,0:T(8,128)(2,1)S(1)}, u32[]{:S(2)}, u32[]{:S(2)}) collective-permute-start(bf16[512,512]{1,0:T(8,128)(2,1)S(1)} %get-tuple-element.250), channel_id=1, source_target_pairs={{0,2},{1,3},{2,0},{3,1},{4,6},{5,7},{6,4},{7,5},{8,10},{9,11},{10,... | collective-permute-start | bytes 1572872 | tf_op jit(solution)/shard_map/ppermute | solution.py:60
  567.2 18.3 %collective-permute-start.37 = (bf16[512,512]{1,0:T(8,128)(2,1)S(1)}, bf16[512,512]{1,0:T(8,128)(2,1)S(1)}, u32[]{:S(2)}, u32[]{:S(2)}) collective-permute-start(bf16[512,512]{1,0:T(8,128)(2,1)S(1)} %get-tuple-element.252), channel_id=1, source_target_pairs={{0,4},{1,5},{2,6},{3,7},{4,0},{5,1},{6,2},{7,3},{8,12},{9,13},{10,... | collective-permute-start | bytes 1572872 | tf_op jit(solution)/shard_map/ppermute | solution.py:60
  570.6 17.8 %collective-permute-start.40 = (bf16[512,512]{1,0:T(8,128)(2,1)S(1)}, bf16[512,512]{1,0:T(8,128)(2,1)}, u32[]{:S(2)}, u32[]{:S(2)}) collective-permute-start(bf16[512,512]{1,0:T(8,128)(2,1)S(1)} %get-tuple-element.253), channel_id=1, source_target_pairs={{0,2},{1,3},{2,0},{3,1},{4,6},{5,7},{6,4},{7,5},{8,10},{9,11},{10,... | collective-permute-start | bytes 1572872 | tf_op jit(solution)/shard_map/ppermute | solution.py:60
  588.6 9.2 collective-permute-start.43
  588.8 14.6 %collective-permute-start.42 = (bf16[256,512]{1,0:T(8,128)(2,1)S(1)}, bf16[256,512]{1,0:T(8,128)(2,1)S(1)}, u32[]{:S(2)}, u32[]{:S(2)}) collective-permute-start(bf16[256,512]{1,0:T(8,128)(2,1)S(1)} %get-tuple-element.270), channel_id=1, source_target_pairs={{0,8},{1,9},{2,10},{3,11},{4,12},{5,13},{6,14},{7,15},{8,0},{9,1},... | collective-permute-start | bytes 786440 | tf_op jit(solution)/shard_map/ppermute | solution.py:60
  591.0 17.7 %collective-permute-start.41 = (bf16[256,512]{1,0:T(8,128)(2,1)S(1)}, bf16[256,512]{1,0:T(8,128)(2,1)S(1)}, u32[]{:S(2)}, u32[]{:S(2)}) collective-permute-start(bf16[256,512]{1,0:T(8,128)(2,1)S(1)} %get-tuple-element.268), channel_id=1, source_target_pairs={{0,8},{1,9},{2,10},{3,11},{4,12},{5,13},{6,14},{7,15},{8,0},{9,1},... | collective-permute-start | bytes 786440 | tf_op jit(solution)/shard_map/ppermute | solution.py:60
  592.5 19.0 %collective-permute-start.44 = (bf16[256,512]{1,0:T(8,128)(2,1)S(1)}, bf16[256,512]{1,0:T(8,128)(2,1)S(1)}, u32[]{:S(2)}, u32[]{:S(2)}) collective-permute-start(bf16[256,512]{1,0:T(8,128)(2,1)S(1)} %get-tuple-element.273), channel_id=1, source_target_pairs={{0,8},{1,9},{2,10},{3,11},{4,12},{5,13},{6,14},{7,15},{8,0},{9,1},... | collective-permute-start | bytes 786440 | tf_op jit(solution)/shard_map/ppermute | solution.py:60
  611.5 17.2 %collective-permute-start.45 = (bf16[128,512]{1,0:T(8,128)(2,1)S(1)}, bf16[128,512]{1,0:T(8,128)(2,1)S(1)}, u32[]{:S(2)}, u32[]{:S(2)}) collective-permute-start(bf16[128,512]{1,0:T(8,128)(2,1)S(1)} %fusion.113), channel_id=1, source_target_pairs={{0,16},{1,17},{2,18},{3,19},{4,20},{5,21},{6,22},{7,23},{8,24},{9,... | collective-permute-start | bytes 393224 | tf_op jit(solution)/shard_map/ppermute | solution.py:60
  615.0 16.6 %collective-permute-start.46 = (bf16[128,512]{1,0:T(8,128)(2,1)S(1)}, bf16[128,512]{1,0:T(8,128)(2,1)S(1)}, u32[]{:S(2)}, u32[]{:S(2)}) collective-permute-start(bf16[128,512]{1,0:T(8,128)(2,1)S(1)} %fusion.111), channel_id=1, source_target_pairs={{0,16},{1,17},{2,18},{3,19},{4,20},{5,21},{6,22},{7,23},{8,24},{9,... | collective-permute-start | bytes 393224 | tf_op jit(solution)/shard_map/ppermute | solution.py:60
  615.1 18.6 %collective-permute-start.47 = (bf16[128,512]{1,0:T(8,128)(2,1)S(1)}, bf16[128,512]{1,0:T(8,128)(2,1)S(1)}, u32[]{:S(2)}, u32[]{:S(2)}) collective-permute-start(bf16[128,512]{1,0:T(8,128)(2,1)S(1)} %fusion.109), channel_id=1, source_target_pairs={{0,16},{1,17},{2,18},{3,19},{4,20},{5,21},{6,22},{7,23},{8,24},{9,... | collective-permute-start | bytes 393224 | tf_op jit(solution)/shard_map/ppermute | solution.py:60
  618.1 17.0 %collective-permute-start.48 = (bf16[128,512]{1,0:T(8,128)(2,1)S(1)}, bf16[128,512]{1,0:T(8,128)(2,1)S(1)}, u32[]{:S(2)}, u32[]{:S(2)}) collective-permute-start(bf16[128,512]{1,0:T(8,128)(2,1)S(1)} %fusion.107), channel_id=1, source_target_pairs={{0,16},{1,17},{2,18},{3,19},{4,20},{5,21},{6,22},{7,23},{8,24},{9,... | collective-permute-start | bytes 393224 | tf_op jit(solution)/shard_map/ppermute | solution.py:60
  635.9 12.2 %collective-permute-start.49 = (bf16[128,2048]{1,0:T(8,128)(2,1)S(1)}, bf16[128,2048]{1,0:T(8,128)(2,1)S(1)}, u32[]{:S(2)}, u32[]{:S(2)}) collective-permute-start(bf16[128,2048]{1,0:T(8,128)(2,1)S(1)} %get-tuple-element.231), channel_id=1, source_target_pairs={{0,2},{1,3},{2,0},{3,1},{4,6},{5,7},{6,4},{7,5},{8,10},{9,11},{10,... | collective-permute-start | bytes 1572872 | tf_op jit(solution)/shard_map/ppermute | solution.py:60
  649.3 3.0 collective-permute-start.50
  689.6 326.1 %reduce-scatter.3.cloned.1.call-start = ((), (), s32[]{:S(2)}) async-start(), calls=%async_computation.6 | async-start | bytes 17301504 | tf_op jit(solution)/shard_map/reduce_scatter | solution.py:601
  740.2 11.6 %collective-permute-start.51 = (bf16[256,2688]{1,0:T(8,128)(2,1)S(1)}, bf16[256,2688]{1,0:T(8,128)(2,1)S(1)}, u32[]{:S(2)}, u32[]{:S(2)}) collective-permute-start(bf16[256,2688]{1,0:T(8,128)(2,1)S(1)} %slice.695), channel_id=1, source_target_pairs={{0,1},{1,0},{2,3},{3,2},{4,5},{5,4},{6,7},{7,6},{8,9},{9,8},{10,11... | collective-permute-start | bytes 4128776 | tf_op jit(solution)/shard_map/ppermute | solution.py:60
  754.6 18.1 %collective-permute-start.52 = (bf16[128,2688]{1,0:T(8,128)(2,1)}, bf16[128,2688]{1,0:T(8,128)(2,1)}, u32[]{:S(2)}, u32[]{:S(2)}) collective-permute-start(bf16[128,2688]{1,0:T(8,128)(2,1)} %slice.993), channel_id=1, source_target_pairs={{0,2},{1,3},{2,0},{3,1},{4,6},{5,7},{6,4},{7,5},{8,10},{9,11},{10,... | collective-permute-start | bytes 2064392 | tf_op jit(solution)/shard_map/ppermute | solution.py:60
  757.3 68.7 %all-to-all-start.1 = ((bf16[8,3,88,256]{3,2,1,0:T(8,128)(2,1)}), bf16[8,3,88,256]{3,2,1,0:T(8,128)(2,1)}, u32[]{:S(2)}, u32[]{:S(2)}) async-start(bf16[8,3,88,256]{3,2,1,0:T(8,128)(2,1)} %maximum_bitcast_fusion.1), calls=%async_computation.3 | async-start | bytes 2162688 | tf_op jit(solution)/shard_map/all_to_all | solution.py:591
  806.0 12.7 %collective-permute-start.53 = (bf16[1024,640]{1,0:T(8,128)(2,1)S(1)}, bf16[1024,640]{1,0:T(8,128)(2,1)S(1)}, u32[]{:S(2)}, u32[]{:S(2)}) collective-permute-start(bf16[1024,640]{1,0:T(8,128)(2,1)S(1)} %bitcast.233), channel_id=1, source_target_pairs={{0,1},{1,0},{2,3},{3,2},{4,5},{5,4},{6,7},{7,6},{8,9},{9,8},{10,11... | collective-permute-start | bytes 3932168 | tf_op jit(solution)/shard_map/ppermute | solution.py:60
  821.5 30.5 %collective-permute-start.54 = (bf16[512,640]{1,0:T(8,128)(2,1)}, bf16[512,640]{1,0:T(8,128)(2,1)}, u32[]{:S(2)}, u32[]{:S(2)}) collective-permute-start(bf16[512,640]{1,0:T(8,128)(2,1)} %slice.994), channel_id=1, source_target_pairs={{0,2},{1,3},{2,0},{3,1},{4,6},{5,7},{6,4},{7,5},{8,10},{9,11},{10,... | collective-permute-start | bytes 1966088 | tf_op jit(solution)/shard_map/ppermute | solution.py:60
  853.3 11.7 %collective-permute-start.55 = (bf16[256,640]{1,0:T(8,128)(2,1)S(1)}, bf16[256,640]{1,0:T(8,128)(2,1)S(1)}, u32[]{:S(2)}, u32[]{:S(2)}) collective-permute-start(bf16[256,640]{1,0:T(8,128)(2,1)S(1)} %slice.999), channel_id=1, source_target_pairs={{0,4},{1,5},{2,6},{3,7},{4,0},{5,1},{6,2},{7,3},{8,12},{9,13},{10,... | collective-permute-start | bytes 983048 | tf_op jit(solution)/shard_map/ppermute | solution.py:60
  865.1 8.0 collective-permute-start.56
  873.2 8.9 collective-permute-start.57
  (122 other events, 1173.4 us)
Sparse Core Ops, SparseCore 0:
  16.1 156.6 all-gather.2
  175.6 139.3 all-gather.4
  689.7 130.1 reduce-scatter.4
  822.1 193.5 reduce-scatter.2

commit v2 on v1

--- a/solution.py
+++ b/solution.py
@@ -70,14 +70,16 @@
     return lax.optimization_barrier((first, second))
 
 
-def halve_stage(keeps, receiveds, masks, count):
+def halve_stage(keeps, receiveds, masks, count, follow=()):
     half = keeps[0].shape[0] // 2
-    sent = [
-        swap_with((k[half:].astype(F32) + r[half:].astype(F32)).astype(BF), mask, count)
-        for k, r, mask in zip(keeps, receiveds, masks)
+    upper = [
+        (k[half:].astype(F32) + r[half:].astype(F32)).astype(BF)
+        for k, r in zip(keeps, receiveds)
     ]
+    upper, follow = tie(upper, follow)
+    sent = [swap_with(value, mask, count) for value, mask in zip(upper, masks)]
     lower = [k[:half].astype(F32) + r[:half].astype(F32) for k, r in zip(keeps, receiveds)]
-    return lower, sent
+    return lower, sent, follow
 
 
 def scatter_rows(partial, masks, count):
@@ -152,8 +154,8 @@
     )(ids, slot_rows, slot_weights, *([cotangents] * GB), down_t, common_down_t)
 
 
-def expert_block(half, streams, order_flags, slot_rows, slot_weights, dh, dhs, weights, previous):
-    gate_up, gate_up_t, common_t, common = weights
+def expert_hidden(half, streams, order_flags, slot_rows, slot_weights, dh, dhs, weights, previous):
+    gate_up, common_t = weights
     groups, _, slots = slot_rows.shape
     experts, _, double = gate_up.shape
     width = double // 2
@@ -167,9 +169,8 @@
     def body(*refs):
         slot_ref, weight_ref, dh_ref, dhs_ref = refs[:4]
         token_refs = refs[4 : 4 + count]
-        gu_ref, gut_ref, common_t_ref, common_ref = refs[4 + count : 8 + count]
-        x_ref, hidden_ref, dgu_ref, hs_ref, dgs_ref = refs[-(5 + count) : -count]
-        out_refs = refs[-count:]
+        gu_ref, common_t_ref = refs[4 + count : 6 + count]
+        x_ref, hidden_ref, dgu_ref, hs_ref, dgs_ref = refs[-5:]
         for k in range(GB):
             picks = one_hot(slot_ref[k], rows)
             for s in range(count):
@@ -191,7 +192,6 @@
         slope = logistic * (1.0 + gate * (1.0 - logistic))
         dgs_ref[:, :units] = (grad_hidden * up * slope).astype(BF)
         dgs_ref[:, units:] = (grad_hidden * silu).astype(BF)
-        grads = []
         for j in range(experts):
             both = dot(x_ref[j], gu_ref[j])
             gate, up = both[:, :width], both[:, width:]
@@ -202,17 +202,6 @@
             slope = logistic * (1.0 + gate * (1.0 - logistic))
             dgu_ref[j, :, :width] = (grad_hidden * up * slope).astype(BF)
             dgu_ref[j, :, width:] = (grad_hidden * silu).astype(BF)
-            grads.append(dot(dgu_ref[j], gut_ref[j]).astype(BF))
-        for k in range(GB):
-            picks = one_hot(slot_ref[k], rows)
-            stacked = jnp.concatenate([g[k * cap : (k + 1) * cap] for g in grads], axis=0)
-            total = dot(picks, stacked) + dot(
-                dgs_ref[k * rows : (k + 1) * rows, :], common_ref[...]
-            )
-            for s in range(count):
-                out_refs[s][k * rows : (k + 1) * rows, :] = total[
-                    :, s * part : (s + 1) * part
-                ].astype(BF)
 
     shift = half * blocks
     token_specs = [
@@ -226,18 +215,16 @@
         pl.BlockSpec((GB * rows, units), lambda i: (shift + i, 0)),
         *token_specs,
         resident(gate_up.shape),
-        resident(gate_up_t.shape),
         resident(common_t.shape),
-        resident(common.shape),
     ]
-    operands = [slot_rows, slot_weights, dh, dhs, *streams, gate_up, gate_up_t, common_t, common]
+    operands = [slot_rows, slot_weights, dh, dhs, *streams, gate_up, common_t]
     aliases = {}
     if previous is not None:
         for at, value in enumerate(previous):
             aliases[len(operands)] = at
             in_specs.append(pl.BlockSpec(memory_space=pl.ANY))
             operands.append(value)
-    outs = pl.pallas_call(
+    return pl.pallas_call(
         body,
         grid=(blocks,),
         in_specs=in_specs,
@@ -247,7 +234,6 @@
             pl.BlockSpec((experts, GB * cap, double), lambda i: (0, shift + i, 0)),
             pl.BlockSpec((GB * rows, units), lambda i: (shift + i, 0)),
             pl.BlockSpec((GB * rows, 2 * units), lambda i: (shift + i, 0)),
-            *token_specs,
         ],
         out_shape=[
             jax.ShapeDtypeStruct((experts, groups * cap, D), BF),
@@ -255,45 +241,59 @@
             jax.ShapeDtypeStruct((experts, groups * cap, double), BF),
             jax.ShapeDtypeStruct((groups * rows, units), BF),
             jax.ShapeDtypeStruct((groups * rows, 2 * units), BF),
-            *[jax.ShapeDtypeStruct(s.shape, BF) for s in streams],
         ],
         input_output_aliases=aliases,
         compiler_params=pltpu.CompilerParams(vmem_limit_bytes=VMEM_CAP),
-        name="expert_block",
+        name="expert_hidden",
     )(*operands)
-    return outs[:5], outs[5:]
-
-
-def combine_rows(ids, slot_rows, expert_rows, hidden_common, common_down):
+
+
+def token_terms(half, order_flags, slot_rows, slot_values, weights, extra, extra_weights):
     groups, _, slots = slot_rows.shape
-    experts = len(expert_rows)
+    experts, _, width = slot_values.shape
     cap = slots // experts
-    rows = hidden_common.shape[0] // groups
-
-    def body(ids_ref, slot_ref, *refs):
-        row_refs = refs[:experts]
-        hs_ref, down_ref, out_ref = refs[experts:]
-        stacked = jnp.concatenate([r[...] for r in row_refs], axis=0)
-        total = dot(one_hot(slot_ref[0], rows), stacked) + dot(hs_ref[...], down_ref[...])
-        out_ref[...] = total.astype(BF)
+    rows = extra.shape[0] // groups
+    units = extra.shape[1]
+    blocks = groups // (2 * GB)
+    shift = half * blocks
+    count = len(order_flags)
+    part = D // count
+
+    def body(slot_ref, value_ref, weight_ref, extra_ref, extra_weight_ref, *out_refs):
+        results = [dot(value_ref[j], weight_ref[j]).astype(BF) for j in range(experts)]
+        for k in range(GB):
+            stacked = jnp.concatenate([r[k * cap : (k + 1) * cap] for r in results], axis=0)
+            total = dot(one_hot(slot_ref[k], rows), stacked) + dot(
+                extra_ref[k * rows : (k + 1) * rows, :], extra_weight_ref[...]
+            )
+            for s in range(count):
+                out_refs[s][k * rows : (k + 1) * rows, :] = total[
+                    :, s * part : (s + 1) * part
+                ].astype(BF)
 
     return pl.pallas_call(
         body,
-        grid_spec=pltpu.PrefetchScalarGridSpec(
-            num_scalar_prefetch=1,
-            grid=(groups,),
-            in_specs=[
-                pl.BlockSpec((1, 1, slots), lambda i, ids: (i, 0, 0)),
-                *[pl.BlockSpec((cap, D), lambda i, ids: (i, 0)) for _ in range(experts)],
-                pl.BlockSpec((rows, hidden_common.shape[1]), lambda i, ids: (i, 0)),
-                resident(common_down.shape),
-            ],
-            out_specs=pl.BlockSpec((rows, D), lambda i, ids: (ids[i], 0)),
-        ),
-        out_shape=jax.ShapeDtypeStruct((groups * rows, D), BF),
+        grid=(blocks,),
+        in_specs=[
+            pl.BlockSpec((GB, 1, slots), lambda i: (shift + i, 0, 0)),
+            pl.BlockSpec((experts, GB * cap, width), lambda i: (0, shift + i, 0)),
+            resident(weights.shape),
+            pl.BlockSpec((GB * rows, units), lambda i: (shift + i, 0)),
+            resident(extra_weights.shape),
+        ],
+        out_specs=[
+            pl.BlockSpec(
+                (GB * rows, part),
+                functools.partial(lambda f, i: (block_order(i, blocks, f), 0), flag),
+            )
+            for flag in order_flags
+        ],
+        out_shape=[
+            jax.ShapeDtypeStruct((groups // 2 * rows, part), BF) for _ in order_flags
+        ],
         compiler_params=pltpu.CompilerParams(vmem_limit_bytes=VMEM_CAP),
-        name="combine_rows",
-    )(ids, slot_rows, *expert_rows, hidden_common, common_down)
+        name="token_terms",
+    )(slot_rows, slot_values, weights, extra, extra_weights)
 
 
 def slot_tables(routes, route_weight, place_order, expert_total, capacity, padded):
@@ -517,58 +517,92 @@
     )
     near = [jnp.concatenate(pair, axis=0) for pair in zip(near, last)]
     far = [swap_with(block, CORE, count) for block in near]
-    expert_weights = (gate_up, gate_up_t, common_gu_t, common_gu)
-    kept, far_terms = expert_block(
-        1, far, order_flags, slot_rows, slot_weights, grad_hidden, grad_hidden_common,
-        expert_weights, None,
+    hidden_weights = (gate_up, common_gu_t)
+    kept = None
+    for half, streams in ((0, near), (1, far)):
+        kept = expert_hidden(
+            half, streams, order_flags, slot_rows, slot_weights, grad_hidden,
+            grad_hidden_common, hidden_weights, kept,
+        )
+    rows_in, hidden_rows, grad_gu, hidden_common, grad_common = kept
+    far_terms = token_terms(
+        1, order_flags, slot_rows, grad_gu, gate_up_t, grad_common, common_gu
     )
     far_received = [swap_with(term, CORE, count) for term in far_terms]
-    kept, near_terms = expert_block(
-        0, near, order_flags, slot_rows, slot_weights, grad_hidden, grad_hidden_common,
-        expert_weights, kept,
-    )
-    rows_in, hidden_rows, grad_gu, hidden_common, grad_common = kept
-    half_rows = count // 2 * shard_rows
-    parts = []
-    for s, flag in enumerate(order_flags):
-        total = 0.0
-        for h, tokens in ((0, near[s]), (1, far[s])):
-            grads = grad_common[h * half_rows : (h + 1) * half_rows]
-            if flag:
-                shape = (2, 2, half_rows // 4, 2 * unit_pad)
-                grads = jnp.swapaxes(grads.reshape(shape), 0, 1).reshape(half_rows, 2 * unit_pad)
-            total = total + dot(grads, tokens, ((0,), (0,)))
-        parts.append(total)
-    grad_common_gu = jnp.concatenate(parts, axis=1)
+    slot_rows_after, _ = tie(slot_rows, far_terms)
+    near_terms = token_terms(
+        0, order_flags, slot_rows_after, grad_gu, gate_up_t, grad_common, common_gu
+    )
+
+    def common_gradients(cotangents):
+        half_rows = count // 2 * shard_rows
+        parts = []
+        for s, flag in enumerate(order_flags):
+            total = 0.0
+            for h, tokens in ((0, near[s]), (1, far[s])):
+                grads = cotangents[h * half_rows : (h + 1) * half_rows]
+                if flag:
+                    shape = (2, 2, half_rows // 4, 2 * unit_pad)
+                    grads = jnp.swapaxes(grads.reshape(shape), 0, 1).reshape(half_rows, 2 * unit_pad)
+                total = total + dot(grads, tokens, ((0,), (0,)))
+            parts.append(total)
+        grad_common_gu = jnp.concatenate(parts, axis=1)
+        return grad_common_gu
+
     if count > 32:
+        grad_common_gu = common_gradients(grad_common)
         near_terms, grad_common_gu = tie(near_terms, grad_common_gu)
     turns = [order[::-1] for order in stream_orders]
 
-    lower, sent = halve_stage(near_terms, far_received, [turn[0] for turn in turns], count)
-    expert_rows = [dot(hidden_rows[j], down_pad[j]).astype(BF) for j in range(expert_local)]
-    result_terms = combine_rows(group_ids, slot_rows, expert_rows, hidden_common, common_down)
-    sent, result_terms = tie(sent, result_terms)
-
-    lower, sent = halve_stage(lower, sent, [turn[1] for turn in turns], count)
+    lower, sent, (slot_rows_late, rows_late, grad_gu_late, hidden_late) = halve_stage(
+        near_terms, far_received, [turn[0] for turn in turns], count,
+        (slot_rows, rows_in, grad_gu, hidden_rows),
+    )
+
+    def result_exchange(slot_rows_late):
+        far_results = token_terms(
+            1, order_flags, slot_rows_late, hidden_late, down_pad, hidden_common, common_down
+        )
+        far_results, slot_rows_late = tie(far_results, slot_rows_late)
+        far_results_received = [swap_with(term, CORE, count) for term in far_results]
+        near_results = token_terms(
+            0, order_flags, slot_rows_late, hidden_late, down_pad, hidden_common, common_down
+        )
+        return near_results, far_results_received
+
     grad_expert_gate = jnp.stack(
-        [dot(rows_in[j], grad_gu[j, :, :width], ((0,), (0,))) for j in range(expert_local)]
-    )
-    sent, grad_expert_gate = tie(sent, grad_expert_gate)
-    lower, sent = halve_stage(lower, sent, [turn[2] for turn in turns], count)
+        [dot(rows_late[j], grad_gu_late[j, :, :width], ((0,), (0,))) for j in range(expert_local)]
+    )
+    if count <= 32:
+        near_results, far_results_received = result_exchange(slot_rows_late)
+    lower, sent, (rows_late, grad_gu_late, hidden_late, grad_common_late) = halve_stage(
+        lower, sent, [turn[1] for turn in turns], count,
+        (rows_late, grad_gu_late, hidden_late, grad_common),
+    )
     grad_expert_up = jnp.stack(
         [
-            dot(rows_in[j], grad_gu[j, :, width_pad : width_pad + width], ((0,), (0,)))
+            dot(rows_late[j], grad_gu_late[j, :, width_pad : width_pad + width], ((0,), (0,)))
             for j in range(expert_local)
         ]
     )
-    sent, grad_expert_up = tie(sent, grad_expert_up)
+    if count <= 32:
+        lower, sent, (near_results, hidden_late, grad_common_late) = halve_stage(
+            lower, sent, [turn[2] for turn in turns], count,
+            (near_results, hidden_late, grad_common_late),
+        )
+        grad_common_gu = common_gradients(grad_common_late)
+        result_lower, result_sent, _ = halve_stage(
+            near_results, far_results_received, [turn[0] for turn in turns], count
+        )
+    else:
+        lower, sent, _ = halve_stage(lower, sent, [turn[2] for turn in turns], count)
     for k in range(3, len(order_a)):
-        lower, sent = halve_stage(lower, sent, [turn[k] for turn in turns], count)
+        lower, sent, _ = halve_stage(lower, sent, [turn[k] for turn in turns], count)
     grad_normed_second = jnp.concatenate(
         [a + b.astype(F32) for a, b in zip(lower, sent)], axis=1
     )
     grad_expert_down = jnp.stack(
-        [dot(hidden_rows[j][:, :width], grad_rows[j], ((0,), (0,))) for j in range(expert_local)]
+        [dot(hidden_late[j][:, :width], grad_rows[j], ((0,), (0,))) for j in range(expert_local)]
     )
 
     canon_ids = jnp.zeros((count,), jnp.int32)
@@ -595,15 +629,22 @@
     grad_shared_down = common_grads[2].astype(F32)
 
     if count > 32:
-        result_terms, _ = tie(
-            result_terms, (grad_normed_second, common_grads, grad_expert_down)
+        slot_rows_late, grad_normed_second = tie(slot_rows_late, grad_normed_second)
+        near_results, far_results_received = result_exchange(slot_rows_late)
+        result_lower, result_sent, _ = halve_stage(
+            near_results, far_results_received, [turn[0] for turn in turns], count
         )
-    result = lax.psum_scatter(result_terms, BOTH, scatter_dimension=0, tiled=True)
     cotangent = out_cotangent.astype(F32)
     grad_from_experts, grad_experts_part = norm_back(hidden_state, experts_scale, grad_normed_second)
     grad_hidden_state = cotangent + grad_from_experts
     grad_mixer_full = cube_gather(grad_hidden_state.astype(BF), tensor_masks, count)
     grad_output_t = dot(grad_mixer_full, heads_out, ((0,), (0,)))
+    result_lower, result_sent, _ = halve_stage(
+        result_lower, result_sent, [turn[1] for turn in turns], count
+    )
+    grad_output_t = lax.psum_scatter(
+        grad_output_t.astype(BF), "dp", scatter_dimension=0, tiled=True
+    )
     grad_heads = dot(grad_mixer_full, weight_out_t).astype(BF)
     grad_heads = grad_heads.reshape(seq_len, local_heads, V_DIM)
     grad_probs = jnp.einsum("qhd,khd->hqk", grad_heads, values, preferred_element_type=F32)
@@ -644,12 +685,15 @@
         axis=1,
     )
     grad_shard = scatter_rows(grad_terms, tensor_masks[::-1], count)
+    grad_shard, hidden_late = tie(grad_shard, hidden_state)
+    result_lower, result_sent, _ = halve_stage(
+        result_lower, result_sent, [turn[2] for turn in turns], count
+    )
     grad_query_local = dot(normed_full, grad_query_raw, ((0,), (0,)))
     grad_up_local = dot(latent_full, grad_key_value, ((0,), (0,)))
     weight_terms = jnp.concatenate(
         [
             grad_query_local.astype(BF),
-            grad_output_t.astype(BF),
             grad_up_local.astype(BF).reshape(D, up_cols),
         ],
         axis=1,
@@ -657,8 +701,8 @@
     weight_grads = lax.psum_scatter(weight_terms, "dp", scatter_dimension=0, tiled=True)
     weight_grads = weight_grads.astype(F32)
     grad_query_weight = weight_grads[:, :query_cols]
-    grad_output_weight = weight_grads[:, query_cols : query_cols + out_cols].T
-    grad_latent_up = weight_grads[:, query_cols + out_cols :].reshape(latent_up.shape)
+    grad_output_weight = grad_output_t.astype(F32).T
+    grad_latent_up = weight_grads[:, query_cols:].reshape(latent_up.shape)
 
     grad_latent_raw, grad_latent_part = norm_back(
         latent_raw, latent_scale, grad_shard[:, D : D + KV_RANK]
@@ -688,17 +732,21 @@
         ],
         axis=1,
     ).astype(BF)
+    for k in range(3, len(order_a)):
+        result_lower, result_sent, _ = halve_stage(
+            result_lower, result_sent, [turn[k] for turn in turns], count
+        )
+    result = jnp.concatenate(
+        [a + b.astype(F32) for a, b in zip(result_lower, result_sent)], axis=1
+    )
     small_terms = jnp.take(small_terms.reshape(count, D // count, latent_pad), group_ids, axis=0)
-    small_grads = scatter_rows(
-        small_terms.reshape(D, latent_pad), (CORE,) + order_a[::-1], count
-    )
+    small_grads = scatter_rows(small_terms.reshape(D, latent_pad), (CORE,) + order_a[::-1], count)
     at = KV_RANK + QK_ROPE
     grad_latent_weight = small_grads[:, :at]
     grad_attention_gain = small_grads[:, at]
     grad_experts_gain = small_grads[:, at + 1]
     grad_latent_gain = small_grads[: KV_RANK // count, at + 2]
-    result, grad_input = tie(result, grad_input)
-    layer_output = (hidden_state + result.astype(F32)).astype(BF)
+    layer_output = (hidden_late + result).astype(BF)
     return (
         layer_output,
         grad_input,

time: 1030 us -> 1000 us (0.971)
  other arithmetic: 103 us -> 141 us
  waiting for transfers between devices: 441 us -> 410 us
  matrix products: 123 us -> 99.2 us
  local copies, waits for them, and re-layouts: 142 us -> 127 us
    reduce_scatter x1, waiting for transfers between devices: 128 us -> 0.02 us  [local(): lax.psum_scatter(grad_output_t.astype(BF), 'dp', scatter_dimension=0, til...]
    ppermute x58 -> x78, waiting for transfers between devices: 220 us -> 305 us  [swap_with(): return lax.ppermute(values, BOTH, [(i, i ^ mask) for i in range(count)])]
    dot_general x29 -> x27, matrix products: 117 us -> 91.1 us  [dot(): lax.dot_general(left, right, (dims, ((), ())), preferred_element_type=F32)]
    add x10 -> x16, other arithmetic: 21.1 us -> 45 us  [halve_stage(): k[:half].astype(F32) + r[:half].astype(F32)]
    convert_element_type x6 -> x16, other arithmetic: 3.04 us -> 18.8 us  [halve_stage(): (k[half:].astype(F32) + r[half:].astype(F32)).astype(BF)]
    reduce_scatter x1, waiting for transfers between devices: 0.01 us -> 14.3 us  [local(): lax.psum_scatter(weight_terms, 'dp', scatter_dimension=0, tiled=True)]
    ppermute x58 -> x78, starting transfers between devices: 61 us -> 69.5 us  [swap_with(): return lax.ppermute(values, BOTH, [(i, i ^ mask) for i in range(count)])]
    pallas_call x3 -> x6, Pallas kernels: 102 us -> 96 us  [the longest x4 59.5 us: token_terms(): pl.pallas_call(body, grid=(blocks,), in_specs=[pl.BlockSpec((GB, 1, slots...]
  transfers between devices with their start and end apart: 64 -> 84, of which waited for: 38 -> 43; matrix products, arithmetic and copies ran while one was open for 30% -> 33% of each run, Pallas kernels for 9% -> 9%
where the time goes in v2:
time: 1000 us; the launch traced here: 994 us
  waiting for transfers between devices  410 us (41%)
  other arithmetic  141 us (14%)
  local copies, waits for them, and re-layouts  127 us (13%)
  Pallas kernels  122 us (12%)
  matrix products  99.2 us (10%)
  starting transfers between devices  78.9 us (8%)
  between operations  16.4 us (2%)
    ppermute x78, waiting for transfers between devices, swap_with(): return lax.ppermute(values, BOTH, [(i, i ^ mask) for i in range(count)])  305 us
    dot_general x27, matrix products, dot(): lax.dot_general(left, right, (dims, ((), ())), preferred_element_type=F32)  91.1 us
    all_gather x1, waiting for transfers between devices, local(): packed_full = lax.all_gather(packed, 'dp', axis=0, tiled=True)  83.1 us
    ppermute x78, starting transfers between devices, swap_with(): return lax.ppermute(values, BOTH, [(i, i ^ mask) for i in range(count)])  69.5 us
    pallas_call x4, Pallas kernels, token_terms(): pl.pallas_call(body, grid=(blocks,), in_specs=[pl.BlockSpec((GB, 1, slots...  59.5 us
    add x16, other arithmetic, halve_stage(): k[:half].astype(F32) + r[:half].astype(F32)  45 us
    pallas_call x2, Pallas kernels, expert_hidden(): pl.pallas_call(body, grid=(blocks,), in_specs=in_specs, out_specs=[pl.Blo...  36.6 us
    unnamed x295, local copies, waits for them, and re-layouts  32.1 us
  transfers between devices with their start and end apart: 84, of which 43 were waited for; matrix products, arithmetic and copies ran while one was open for 33% of the time, Pallas kernels for 9%

profile of v2, /device:TPU:0, one launch (start us, length us, event | category | flops | bytes accessed | tf_op | source)
XLA Modules:
  0.0 994.1 jit_solution(13687793207112101004)
XLA Ops:
  18.5 4.1 collective-permute-start
  25.8 4.8 all-to-all-start
  32.8 5.5 pad_bitcast_fusion.1
  38.4 7.7 fusion.189
  48.4 18.6 %collective-permute-done.1 = f32[2,2,1024]{2,1,0:T(2,128)S(1)} collective-permute-done((f32[2,2,1024]{2,1,0:T(2,128)S(1)}, f32[2,2,1024]{2,1,0:T(2,128)S(1)}, u32[]{:S(2)}, u32[]{:S(2)}) %collective-permute-start.1) | collective-permute-done | bytes 16416 | tf_op jit(solution)/shard_map/ppermute | solution.py:60
  79.0 7.0 all-to-all-done
  89.6 83.1 %all-gather.3.cloned.1.call-done = bf16[2048,2176]{1,0:T(8,128)(2,1)} async-done(((bf16[256,2176]{1,0:T(8,128)(2,1)}), bf16[2048,2176]{1,0:T(8,128)(2,1)}) %all-gather.3.cloned.1.call-update) | async-done | bytes 8912912 | tf_op jit(solution)/shard_map/all_gather | solution.py:381
  211.1 20.2 %collective-permute-done.8 = bf16[128,2048]{1,0:T(8,128)(2,1)S(1)} collective-permute-done((bf16[128,2048]{1,0:T(8,128)(2,1)S(1)}, bf16[128,2048]{1,0:T(8,128)(2,1)S(1)}, u32[]{:S(2)}, u32[]{:S(2)}) %collective-permute-start.8) | collective-permute-done | bytes 524320 | tf_op jit(solution)/shard_map/ppermute | solution.py:60
  237.2 4.7 copy.286.down_ref
  245.8 7.7 collective-permute-done.21
  253.5 6.6 collective-permute-done.17
  260.2 7.4 collective-permute-done.13
  267.7 7.2 collective-permute-done.9
  275.7 12.0 %collective-permute-done.22 = bf16[256,512]{1,0:T(8,128)(2,1)S(1)} collective-permute-done((bf16[256,512]{1,0:T(8,128)(2,1)S(1)}, bf16[256,512]{1,0:T(8,128)(2,1)S(1)}, u32[]{:S(2)}, u32[]{:S(2)}) %collective-permute-start.22) | collective-permute-done | bytes 262176 | tf_op jit(solution)/shard_map/ppermute | solution.py:60
  287.9 16.1 %collective-permute-done.18 = bf16[256,512]{1,0:T(8,128)(2,1)S(1)} collective-permute-done((bf16[256,512]{1,0:T(8,128)(2,1)S(1)}, bf16[256,512]{1,0:T(8,128)(2,1)S(1)}, u32[]{:S(2)}, u32[]{:S(2)}) %collective-permute-start.18) | collective-permute-done | bytes 262176 | tf_op jit(solution)/shard_map/ppermute | solution.py:60
  307.7 11.3 %collective-permute-done.14 = bf16[256,512]{1,0:T(8,128)(2,1)S(1)} collective-permute-done((bf16[256,512]{1,0:T(8,128)(2,1)S(1)}, bf16[256,512]{1,0:T(8,128)(2,1)S(1)}, u32[]{:S(2)}, u32[]{:S(2)}) %collective-permute-start.14) | collective-permute-done | bytes 262176 | tf_op jit(solution)/shard_map/ppermute | solution.py:60
  319.8 9.4 collective-permute-done.10
  337.6 6.9 collective-permute-done.11
  352.4 25.6 %cotangent_rows.1 = (bf16[2,2048,2048]{2,1,0:T(8,128)(2,1)}, f32[2,2048,384]{2,1,0:T(8,128)}, f32[4096,128]{1,0:T(8,128)}) custom-call(s32[32]{0:T(128)} %fusion.155.ids_ref, s32[32,1,128]{2,1,0:T(1,128)} %get-tuple-element.173.slot_ref.refs_0_, f32[2,2048,128]{2,1,0:T(8,128)} %broadcast_in_dim.150.weight_ref.refs_1_, ...), custom_call_target="tpu_custom_call" | custom-call | tf_op jit(solution)/shard_map/cotangent_rows/pallas_call | solution.py:129
  378.1 10.7 %collective-permute-done.16 = bf16[1024,512]{1,0:T(8,128)(2,1)} collective-permute-done((bf16[1024,512]{1,0:T(8,128)(2,1)}, bf16[1024,512]{1,0:T(8,128)(2,1)}, u32[]{:S(2)}, u32[]{:S(2)}) %collective-permute-start.16) | collective-permute-done | bytes 1048608 | tf_op jit(solution)/shard_map/ppermute | solution.py:60
  400.4 8.8 copy.290.refs_8_
  412.1 18.3 %expert_hidden.2 = (bf16[2,2048,2048]{2,1,0:T(8,128)(2,1)}, bf16[2,2048,384]{2,1,0:T(8,128)(2,1)}, bf16[2,2048,768]{2,1,0:T(8,128)(2,1)}, bf16[4096,128]{1,0:T(8,128)(2,1)}, bf16[4096,256]{1,0:T(8,128)(2,1)}) custom-call(s32[32,1,128]{2,1,0:T(1,128)} %get-tuple-element.173.slot_ref.refs_0_, f32[2,2048,128]{2,1,0:T(8,128)} %broadcast_in_dim.150.weight_ref.refs_1_, ...), custom_call_target="tpu_custom_call" | custom-call | tf_op jit(solution)/shard_map/expert_hidden/pallas_call | solution.py:227
  430.4 18.3 %expert_hidden.3 = (bf16[2,2048,2048]{2,1,0:T(8,128)(2,1)}, bf16[2,2048,384]{2,1,0:T(8,128)(2,1)}, bf16[2,2048,768]{2,1,0:T(8,128)(2,1)}, bf16[4096,128]{1,0:T(8,128)(2,1)}, bf16[4096,256]{1,0:T(8,128)(2,1)}) custom-call(s32[32,1,128]{2,1,0:T(1,128)} %get-tuple-element.173.slot_ref.ref, ...), custom_call_target="tpu_custom_call", output_to_operand_aliasing={{0}: (10, {}), {1}: (11, {}), {2}: (12, {}), {3}: (13, {}),... | custom-call | tf_op jit(solution)/shard_map/expert_hidden/pallas_call | solution.py:227
  448.7 16.5 %token_terms.4 = (bf16[2048,512]{1,0:T(8,128)(2,1)}, bf16[2048,512]{1,0:T(8,128)(2,1)}, bf16[2048,512]{1,0:T(8,128)(2,1)}, bf16[2048,512]{1,0:T(8,128)(2,1)}) custom-call(s32[32,1,128]{2,1,0:T(1,128)} %get-tuple-element.173.slot_ref.refs_0_, bf16[2,2048,768]{2,1,0:T(8,128)(2,1)} %get-tuple-element.215.value_ref, ...), custom_call_target="tpu_custom_call" | custom-call | tf_op jit(solution)/shard_map/token_terms/pallas_call | solution.py:274
  469.7 16.7 %token_terms.5 = (bf16[2048,512]{1,0:T(8,128)(2,1)}, bf16[2048,512]{1,0:T(8,128)(2,1)}, bf16[2048,512]{1,0:T(8,128)(2,1)}, bf16[2048,512]{1,0:T(8,128)(2,1)}) custom-call(s32[32,1,128]{2,1,0:T(1,128)} %get-tuple-element.173.slot_ref.refs_0_, bf16[2,2048,768]{2,1,0:T(8,128)(2,1)} %get-tuple-element.215.value_ref, ...), custom_call_target="tpu_custom_call" | custom-call | tf_op jit(solution)/shard_map/token_terms/pallas_call | solution.py:274
  486.5 8.3 fusion.198
  500.0 4.0 convert_add_fusion.8
  515.0 5.0 fusion.26
  520.0 5.0 fusion.29
  525.0 13.2 %token_terms.6 = (bf16[2048,512]{1,0:T(8,128)(2,1)}, bf16[2048,512]{1,0:T(8,128)(2,1)}, bf16[2048,512]{1,0:T(8,128)(2,1)}, bf16[2048,512]{1,0:T(8,128)(2,1)}) custom-call(s32[32,1,128]{2,1,0:T(1,128)} %get-tuple-element.173.slot_ref.refs_0_, bf16[2,2048,384]{2,1,0:T(8,128)(2,1)} %get-tuple-element.216.value_ref, ...), custom_call_target="tpu_custom_call" | custom-call | tf_op jit(solution)/shard_map/token_terms/pallas_call | solution.py:274
  538.2 13.1 %token_terms.7 = (bf16[2048,512]{1,0:T(8,128)(2,1)}, bf16[2048,512]{1,0:T(8,128)(2,1)}, bf16[2048,512]{1,0:T(8,128)(2,1)}, bf16[2048,512]{1,0:T(8,128)(2,1)}) custom-call(s32[32,1,128]{2,1,0:T(1,128)} %get-tuple-element.173.slot_ref.refs_0_, bf16[2,2048,384]{2,1,0:T(8,128)(2,1)} %get-tuple-element.216.value_ref, ...), custom_call_target="tpu_custom_call" | custom-call | tf_op jit(solution)/shard_map/token_terms/pallas_call | solution.py:274
  551.6 6.1 pad_maximum_fusion
  565.0 10.8 %collective-permute-done.36 = bf16[1024,512]{1,0:T(8,128)(2,1)S(1)} collective-permute-done((bf16[1024,512]{1,0:T(8,128)(2,1)}, bf16[1024,512]{1,0:T(8,128)(2,1)S(1)}, u32[]{:S(2)}, u32[]{:S(2)}) %collective-permute-start.36) | collective-permute-done | bytes 1048608 | tf_op jit(solution)/shard_map/ppermute | solution.py:60
  577.3 6.3 fusion.32
  584.5 5.0 fusion.35
  589.8 4.9 pad_maximum_fusion.1
  607.7 5.4 collective-permute-done.40
  634.4 4.4 all-to-all-start.1
  643.1 21.4 %collective-permute-done.44 = bf16[256,512]{1,0:T(8,128)(2,1)S(1)} collective-permute-done((bf16[256,512]{1,0:T(8,128)(2,1)S(1)}, bf16[256,512]{1,0:T(8,128)(2,1)S(1)}, u32[]{:S(2)}, u32[]{:S(2)}) %collective-permute-start.44) | collective-permute-done | bytes 262176 | tf_op jit(solution)/shard_map/ppermute | solution.py:60
  665.6 4.6 collective-permute-done.43
  680.9 5.9 fusion.38
  687.1 8.9 collective-permute-done.46
  696.1 6.4 collective-permute-done.47
  702.9 5.4 collective-permute-done.48
  725.6 4.1 collective-permute-start.58
  729.7 6.1 fusion.41
  744.2 6.8 collective-permute-done.59
  756.9 8.8 collective-permute-done.57
  787.8 4.2 convolution_convert_fusion.2
  792.1 4.6 multiply_convert_fusion
  816.4 4.8 concatenate.189
  848.4 7.0 collective-permute-done.52
  861.4 4.5 copy.301
  865.9 4.3 fusion.76
  871.8 6.7 concatenate.196
  878.5 4.3 gather_fusion.1
  895.6 19.5 %collective-permute-done.69 = bf16[128,512]{1,0:T(8,128)(2,1)S(1)} collective-permute-done((bf16[128,512]{1,0:T(8,128)(2,1)S(1)}, bf16[128,512]{1,0:T(8,128)(2,1)S(1)}, u32[]{:S(2)}, u32[]{:S(2)}) %collective-permute-start.69) | collective-permute-done | bytes 131104 | tf_op jit(solution)/shard_map/ppermute | solution.py:60
  916.0 7.5 collective-permute-done.70
  925.6 5.7 collective-permute-done.71
  936.0 5.4 collective-permute-done.74
  944.1 10.3 %collective-permute-done.75 = bf16[256,640]{1,0:T(8,128)(2,1)S(1)} collective-permute-done((bf16[256,640]{1,0:T(8,128)(2,1)S(1)}, bf16[256,640]{1,0:T(8,128)(2,1)S(1)}, u32[]{:S(2)}, u32[]{:S(2)}) %collective-permute-start.75) | collective-permute-done | bytes 327712 | tf_op jit(solution)/shard_map/ppermute | solution.py:60
  955.5 4.5 collective-permute-done.76
  962.2 6.2 collective-permute-done.77
  969.8 14.3 %reduce-scatter.3.cloned.1.call-done = bf16[256,1024]{0,1:T(8,128)(2,1)} async-done(((bf16[2048,1024]{0,1:T(8,128)(2,1)}), bf16[256,1024]{0,1:T(8,128)(2,1)}) %reduce-scatter.3.cloned.1.call-update) | async-done | bytes 524304 | tf_op jit(solution)/shard_map/reduce_scatter | solution.py:701
  (670 shorter events, 338.8 us)
Async XLA Ops:
  7.2 165.5 %all-gather.3.cloned.1.call-start = ((), (), s32[]{:S(2)}) async-start(), calls=%async_computation.4 | async-start | bytes 10027008 | tf_op jit(solution)/shard_map/all_gather | solution.py:381
  15.9 336.5 %all-gather.5.cloned.1.call-start = ((), (), s32[]{:S(2)}) async-start(), calls=%async_computation.5 | async-start | bytes 17301504 | tf_op jit(solution)/shard_map/all_gather | solution.py:505
  18.5 27.6 %collective-permute-start = (f32[1,2,1024]{2,1,0:T(2,128)S(1)}, f32[1,2,1024]{2,1,0:T(2,128)S(1)}, u32[]{:S(2)}, u32[]{:S(2)}) collective-permute-start(f32[1,2,1024]{2,1,0:T(2,128)S(1)} %maximum_bitcast_fusion.2), channel_id=1, source_target_pairs={{0,16},{1,17},{2,18},{3,19},{4,20},{5,21},{6,22},{7,23},{8,24},{9,... | collective-permute-start | bytes 24584 | tf_op jit(solution)/shard_map/ppermute | solution.py:60
  25.8 60.2 %all-to-all-start = ((bf16[8,3,88,256]{3,2,1,0:T(8,128)(2,1)}), bf16[8,3,88,256]{3,2,1,0:T(8,128)(2,1)}, u32[]{:S(2)}, u32[]{:S(2)}) async-start(bf16[8,3,88,256]{3,2,1,0:T(8,128)(2,1)} %copy.271), calls=%async_computation | async-start | bytes 2162688 | tf_op jit(solution)/shard_map/all_to_all | solution.py:394
  30.6 17.6 %collective-permute-start.5 = (bf16[128,2048]{1,0:T(8,128)(2,1)S(1)}, bf16[128,2048]{1,0:T(8,128)(2,1)S(1)}, u32[]{:S(2)}, u32[]{:S(2)}) collective-permute-start(bf16[128,2048]{1,0:T(8,128)(2,1)S(1)} %copy-done.15), channel_id=1, source_target_pairs={{0,2},{1,3},{2,0},{3,1},{4,6},{5,7},{6,4},{7,5},{8,10},{9,11},{10,... | collective-permute-start | bytes 1572872 | tf_op jit(solution)/shard_map/ppermute | solution.py:60
  46.2 20.8 %collective-permute-start.1 = (f32[2,2,1024]{2,1,0:T(2,128)S(1)}, f32[2,2,1024]{2,1,0:T(2,128)S(1)}, u32[]{:S(2)}, u32[]{:S(2)}) collective-permute-start(f32[2,2,1024]{2,1,0:T(2,128)S(1)} %pad_maximum_fusion.39), channel_id=1, source_target_pairs={{0,8},{1,9},{2,10},{3,11},{4,12},{5,13},{6,14},{7,15},{8,0},{9,1},... | collective-permute-start | bytes 49160 | tf_op jit(solution)/shard_map/ppermute | solution.py:60
  48.3 29.4 %collective-permute-start.6 = (bf16[256,2048]{1,0:T(8,128)(2,1)S(1)}, bf16[256,2048]{1,0:T(8,128)(2,1)}, u32[]{:S(2)}, u32[]{:S(2)}) collective-permute-start(bf16[256,2048]{1,0:T(8,128)(2,1)S(1)} %pad_maximum_fusion.6), channel_id=1, source_target_pairs={{0,1},{1,0},{2,3},{3,2},{4,5},{5,4},{6,7},{7,6},{8,9},{9,8},{10,11... | collective-permute-start | bytes 3145736 | tf_op jit(solution)/shard_map/ppermute | solution.py:60
  209.3 21.9 %collective-permute-start.8 = (bf16[128,2048]{1,0:T(8,128)(2,1)S(1)}, bf16[128,2048]{1,0:T(8,128)(2,1)S(1)}, u32[]{:S(2)}, u32[]{:S(2)}) collective-permute-start(bf16[128,2048]{1,0:T(8,128)(2,1)S(1)} %slice.1399), channel_id=1, source_target_pairs={{0,2},{1,3},{2,0},{3,1},{4,6},{5,7},{6,4},{7,5},{8,10},{9,11},{10,... | collective-permute-start | bytes 1572872 | tf_op jit(solution)/shard_map/ppermute | solution.py:60
  233.7 19.7 %collective-permute-start.21 = (bf16[128,512]{1,0:T(8,128)(2,1)S(1)}, bf16[128,512]{1,0:T(8,128)(2,1)S(1)}, u32[]{:S(2)}, u32[]{:S(2)}) collective-permute-start(bf16[128,512]{1,0:T(8,128)(2,1)S(1)} %get-tuple-element.405), channel_id=1, source_target_pairs={{0,16},{1,17},{2,18},{3,19},{4,20},{5,21},{6,22},{7,23},{8,24},{9,... | collective-permute-start | bytes 393224 | tf_op jit(solution)/shard_map/ppermute | solution.py:60
  236.1 24.0 %collective-permute-start.17 = (bf16[128,512]{1,0:T(8,128)(2,1)S(1)}, bf16[128,512]{1,0:T(8,128)(2,1)S(1)}, u32[]{:S(2)}, u32[]{:S(2)}) collective-permute-start(bf16[128,512]{1,0:T(8,128)(2,1)S(1)} %get-tuple-element.406), channel_id=1, source_target_pairs={{0,16},{1,17},{2,18},{3,19},{4,20},{5,21},{6,22},{7,23},{8,24},{9,... | collective-permute-start | bytes 393224 | tf_op jit(solution)/shard_map/ppermute | solution.py:60
  242.8 24.8 %collective-permute-start.13 = (bf16[128,512]{1,0:T(8,128)(2,1)S(1)}, bf16[128,512]{1,0:T(8,128)(2,1)S(1)}, u32[]{:S(2)}, u32[]{:S(2)}) collective-permute-start(bf16[128,512]{1,0:T(8,128)(2,1)S(1)} %get-tuple-element.407), channel_id=1, source_target_pairs={{0,16},{1,17},{2,18},{3,19},{4,20},{5,21},{6,22},{7,23},{8,24},{9,... | collective-permute-start | bytes 393224 | tf_op jit(solution)/shard_map/ppermute | solution.py:60
  245.3 29.7 %collective-permute-start.9 = (bf16[128,512]{1,0:T(8,128)(2,1)S(1)}, bf16[128,512]{1,0:T(8,128)(2,1)S(1)}, u32[]{:S(2)}, u32[]{:S(2)}) collective-permute-start(bf16[128,512]{1,0:T(8,128)(2,1)S(1)} %get-tuple-element.408), channel_id=1, source_target_pairs={{0,16},{1,17},{2,18},{3,19},{4,20},{5,21},{6,22},{7,23},{8,24},{9,... | collective-permute-start | bytes 393224 | tf_op jit(solution)/shard_map/ppermute | solution.py:60
  253.5 34.3 %collective-permute-start.22 = (bf16[256,512]{1,0:T(8,128)(2,1)S(1)}, bf16[256,512]{1,0:T(8,128)(2,1)S(1)}, u32[]{:S(2)}, u32[]{:S(2)}) collective-permute-start(bf16[256,512]{1,0:T(8,128)(2,1)S(1)} %pad_maximum_fusion.32), channel_id=1, source_target_pairs={{0,8},{1,9},{2,10},{3,11},{4,12},{5,13},{6,14},{7,15},{8,0},{9,1},... | collective-permute-start | bytes 786440 | tf_op jit(solution)/shard_map/ppermute | solution.py:60
  260.1 43.9 %collective-permute-start.18 = (bf16[256,512]{1,0:T(8,128)(2,1)S(1)}, bf16[256,512]{1,0:T(8,128)(2,1)S(1)}, u32[]{:S(2)}, u32[]{:S(2)}) collective-permute-start(bf16[256,512]{1,0:T(8,128)(2,1)S(1)} %pad_maximum_fusion.31), channel_id=1, source_target_pairs={{0,8},{1,9},{2,10},{3,11},{4,12},{5,13},{6,14},{7,15},{8,0},{9,1},... | collective-permute-start | bytes 786440 | tf_op jit(solution)/shard_map/ppermute | solution.py:60
  267.6 51.3 %collective-permute-start.14 = (bf16[256,512]{1,0:T(8,128)(2,1)S(1)}, bf16[256,512]{1,0:T(8,128)(2,1)S(1)}, u32[]{:S(2)}, u32[]{:S(2)}) collective-permute-start(bf16[256,512]{1,0:T(8,128)(2,1)S(1)} %pad_maximum_fusion.30), channel_id=1, source_target_pairs={{0,8},{1,9},{2,10},{3,11},{4,12},{5,13},{6,14},{7,15},{8,0},{9,1},... | collective-permute-start | bytes 786440 | tf_op jit(solution)/shard_map/ppermute | solution.py:60
  275.0 54.2 %collective-permute-start.10 = (bf16[256,512]{1,0:T(8,128)(2,1)S(1)}, bf16[256,512]{1,0:T(8,128)(2,1)S(1)}, u32[]{:S(2)}, u32[]{:S(2)}) collective-permute-start(bf16[256,512]{1,0:T(8,128)(2,1)S(1)} %pad_maximum_fusion.29), channel_id=1, source_target_pairs={{0,8},{1,9},{2,10},{3,11},{4,12},{5,13},{6,14},{7,15},{8,0},{9,1},... | collective-permute-start | bytes 786440 | tf_op jit(solution)/shard_map/ppermute | solution.py:60
  287.8 44.6 %collective-permute-start.23 = (bf16[512,512]{1,0:T(8,128)(2,1)S(1)}, bf16[512,512]{1,0:T(8,128)(2,1)S(1)}, u32[]{:S(2)}, u32[]{:S(2)}) collective-permute-start(bf16[512,512]{1,0:T(8,128)(2,1)S(1)} %pad_maximum_fusion.26), channel_id=1, source_target_pairs={{0,2},{1,3},{2,0},{3,1},{4,6},{5,7},{6,4},{7,5},{8,10},{9,11},{10,... | collective-permute-start | bytes 1572872 | tf_op jit(solution)/shard_map/ppermute | solution.py:60
  304.1 29.4 %collective-permute-start.19 = (bf16[512,512]{1,0:T(8,128)(2,1)S(1)}, bf16[512,512]{1,0:T(8,128)(2,1)S(1)}, u32[]{:S(2)}, u32[]{:S(2)}) collective-permute-start(bf16[512,512]{1,0:T(8,128)(2,1)S(1)} %pad_maximum_fusion.25), channel_id=1, source_target_pairs={{0,4},{1,5},{2,6},{3,7},{4,0},{5,1},{6,2},{7,3},{8,12},{9,13},{10,... | collective-permute-start | bytes 1572872 | tf_op jit(solution)/shard_map/ppermute | solution.py:60
  333.4 44.7 %collective-permute-start.24 = (bf16[1024,512]{1,0:T(8,128)(2,1)}, bf16[1024,512]{1,0:T(8,128)(2,1)}, u32[]{:S(2)}, u32[]{:S(2)}) collective-permute-start(bf16[1024,512]{1,0:T(8,128)(2,1)} %pad_maximum_fusion.10), channel_id=1, source_target_pairs={{0,4},{1,5},{2,6},{3,7},{4,0},{5,1},{6,2},{7,3},{8,12},{9,13},{10,... | collective-permute-start | bytes 3145736 | tf_op jit(solution)/shard_map/ppermute | solution.py:60
  334.5 43.6 %collective-permute-start.20 = (bf16[1024,512]{1,0:T(8,128)(2,1)}, bf16[1024,512]{1,0:T(8,128)(2,1)}, u32[]{:S(2)}, u32[]{:S(2)}) collective-permute-start(bf16[1024,512]{1,0:T(8,128)(2,1)} %pad_maximum_fusion.9), channel_id=1, source_target_pairs={{0,2},{1,3},{2,0},{3,1},{4,6},{5,7},{6,4},{7,5},{8,10},{9,11},{10,... | collective-permute-start | bytes 3145736 | tf_op jit(solution)/shard_map/ppermute | solution.py:60
  335.5 53.3 %collective-permute-start.16 = (bf16[1024,512]{1,0:T(8,128)(2,1)}, bf16[1024,512]{1,0:T(8,128)(2,1)}, u32[]{:S(2)}, u32[]{:S(2)}) collective-permute-start(bf16[1024,512]{1,0:T(8,128)(2,1)} %pad_maximum_fusion.8), channel_id=1, source_target_pairs={{0,4},{1,5},{2,6},{3,7},{4,0},{5,1},{6,2},{7,3},{8,12},{9,13},{10,... | collective-permute-start | bytes 3145736 | tf_op jit(solution)/shard_map/ppermute | solution.py:60
  345.5 43.3 %collective-permute-start.12 = (bf16[1024,512]{1,0:T(8,128)(2,1)}, bf16[1024,512]{1,0:T(8,128)(2,1)}, u32[]{:S(2)}, u32[]{:S(2)}) collective-permute-start(bf16[1024,512]{1,0:T(8,128)(2,1)} %pad_maximum_fusion.7), channel_id=1, source_target_pairs={{0,2},{1,3},{2,0},{3,1},{4,6},{5,7},{6,4},{7,5},{8,10},{9,11},{10,... | collective-permute-start | bytes 3145736 | tf_op jit(solution)/shard_map/ppermute | solution.py:60
  391.2 39.2 %collective-permute-start.28 = (bf16[2048,512]{1,0:T(8,128)(2,1)}, bf16[2048,512]{1,0:T(8,128)(2,1)}, u32[]{:S(2)}, u32[]{:S(2)}) collective-permute-start(bf16[2048,512]{1,0:T(8,128)(2,1)} %constant_dynamic-update-slice_fusion.26.refs_7_), channel_id=1, source_target_pairs={{0,1},{1,0},{2,3},{3,2},{4,5},{5,4},{6,7},{7,6},{8,9},{9,8},{10,11... | collective-permute-start | bytes 6291464 | tf_op jit(solution)/shard_map/ppermute | solution.py:60
  393.5 36.9 %collective-permute-start.27 = (bf16[2048,512]{1,0:T(8,128)(2,1)}, bf16[2048,512]{1,0:T(8,128)(2,1)}, u32[]{:S(2)}, u32[]{:S(2)}) collective-permute-start(bf16[2048,512]{1,0:T(8,128)(2,1)} %constant_dynamic-update-slice_fusion.21.refs_6_), channel_id=1, source_target_pairs={{0,1},{1,0},{2,3},{3,2},{4,5},{5,4},{6,7},{7,6},{8,9},{9,8},{10,11... | collective-permute-start | bytes 6291464 | tf_op jit(solution)/shard_map/ppermute | solution.py:60
  396.2 34.1 %collective-permute-start.26 = (bf16[2048,512]{1,0:T(8,128)(2,1)}, bf16[2048,512]{1,0:T(8,128)(2,1)}, u32[]{:S(2)}, u32[]{:S(2)}) collective-permute-start(bf16[2048,512]{1,0:T(8,128)(2,1)} %constant_dynamic-update-slice_fusion.16.refs_5_), channel_id=1, source_target_pairs={{0,1},{1,0},{2,3},{3,2},{4,5},{5,4},{6,7},{7,6},{8,9},{9,8},{10,11... | collective-permute-start | bytes 6291464 | tf_op jit(solution)/shard_map/ppermute | solution.py:60
  398.6 31.8 %collective-permute-start.25 = (bf16[2048,512]{1,0:T(8,128)(2,1)}, bf16[2048,512]{1,0:T(8,128)(2,1)}, u32[]{:S(2)}, u32[]{:S(2)}) collective-permute-start(bf16[2048,512]{1,0:T(8,128)(2,1)} %constant_dynamic-update-slice_fusion.11.refs_4_), channel_id=1, source_target_pairs={{0,1},{1,0},{2,3},{3,2},{4,5},{5,4},{6,7},{7,6},{8,9},{9,8},{10,11... | collective-permute-start | bytes 6291464 | tf_op jit(solution)/shard_map/ppermute | solution.py:60
  465.2 29.8 %collective-permute-start.31 = (bf16[2048,512]{1,0:T(8,128)(2,1)}, bf16[2048,512]{1,0:T(8,128)(2,1)}, u32[]{:S(2)}, u32[]{:S(2)}) collective-permute-start(bf16[2048,512]{1,0:T(8,128)(2,1)} %get-tuple-element.145), channel_id=1, source_target_pairs={{0,1},{1,0},{2,3},{3,2},{4,5},{5,4},{6,7},{7,6},{8,9},{9,8},{10,11... | collective-permute-start | bytes 6291464 | tf_op jit(solution)/shard_map/ppermute | solution.py:60
  465.8 34.2 %collective-permute-start.30 = (bf16[2048,512]{1,0:T(8,128)(2,1)}, bf16[2048,512]{1,0:T(8,128)(2,1)}, u32[]{:S(2)}, u32[]{:S(2)}) collective-permute-start(bf16[2048,512]{1,0:T(8,128)(2,1)} %get-tuple-element.144), channel_id=1, source_target_pairs={{0,1},{1,0},{2,3},{3,2},{4,5},{5,4},{6,7},{7,6},{8,9},{9,8},{10,11... | collective-permute-start | bytes 6291464 | tf_op jit(solution)/shard_map/ppermute | solution.py:60
  466.3 37.7 %collective-permute-start.29 = (bf16[2048,512]{1,0:T(8,128)(2,1)}, bf16[2048,512]{1,0:T(8,128)(2,1)}, u32[]{:S(2)}, u32[]{:S(2)}) collective-permute-start(bf16[2048,512]{1,0:T(8,128)(2,1)} %get-tuple-element.143), channel_id=1, source_target_pairs={{0,1},{1,0},{2,3},{3,2},{4,5},{5,4},{6,7},{7,6},{8,9},{9,8},{10,11... | collective-permute-start | bytes 6291464 | tf_op jit(solution)/shard_map/ppermute | solution.py:60
  466.3 41.0 %collective-permute-start.32 = (bf16[2048,512]{1,0:T(8,128)(2,1)}, bf16[2048,512]{1,0:T(8,128)(2,1)}, u32[]{:S(2)}, u32[]{:S(2)}) collective-permute-start(bf16[2048,512]{1,0:T(8,128)(2,1)} %get-tuple-element.146), channel_id=1, source_target_pairs={{0,1},{1,0},{2,3},{3,2},{4,5},{5,4},{6,7},{7,6},{8,9},{9,8},{10,11... | collective-permute-start | bytes 6291464 | tf_op jit(solution)/shard_map/ppermute | solution.py:60
  511.2 46.6 %collective-permute-start.35 = (bf16[1024,512]{1,0:T(8,128)(2,1)S(1)}, bf16[1024,512]{1,0:T(8,128)(2,1)}, u32[]{:S(2)}, u32[]{:S(2)}) collective-permute-start(bf16[1024,512]{1,0:T(8,128)(2,1)S(1)} %get-tuple-element.156), channel_id=1, source_target_pairs={{0,2},{1,3},{2,0},{3,1},{4,6},{5,7},{6,4},{7,5},{8,10},{9,11},{10,... | collective-permute-start | bytes 3145736 | tf_op jit(solution)/shard_map/ppermute | solution.py:60
  511.2 49.4 %collective-permute-start.34 = (bf16[1024,512]{1,0:T(8,128)(2,1)}, bf16[1024,512]{1,0:T(8,128)(2,1)}, u32[]{:S(2)}, u32[]{:S(2)}) collective-permute-start(bf16[1024,512]{1,0:T(8,128)(2,1)} %get-tuple-element.155), channel_id=1, source_target_pairs={{0,4},{1,5},{2,6},{3,7},{4,0},{5,1},{6,2},{7,3},{8,12},{9,13},{10,... | collective-permute-start | bytes 3145736 | tf_op jit(solution)/shard_map/ppermute | solution.py:60
  512.9 50.4 %collective-permute-start.33 = (bf16[1024,512]{1,0:T(8,128)(2,1)}, bf16[1024,512]{1,0:T(8,128)(2,1)}, u32[]{:S(2)}, u32[]{:S(2)}) collective-permute-start(bf16[1024,512]{1,0:T(8,128)(2,1)} %get-tuple-element.154), channel_id=1, source_target_pairs={{0,2},{1,3},{2,0},{3,1},{4,6},{5,7},{6,4},{7,5},{8,10},{9,11},{10,... | collective-permute-start | bytes 3145736 | tf_op jit(solution)/shard_map/ppermute | solution.py:60
  551.3 24.5 %collective-permute-start.36 = (bf16[1024,512]{1,0:T(8,128)(2,1)}, bf16[1024,512]{1,0:T(8,128)(2,1)S(1)}, u32[]{:S(2)}, u32[]{:S(2)}) collective-permute-start(bf16[1024,512]{1,0:T(8,128)(2,1)} %get-tuple-element.157), channel_id=1, source_target_pairs={{0,4},{1,5},{2,6},{3,7},{4,0},{5,1},{6,2},{7,3},{8,12},{9,13},{10,... | collective-permute-start | bytes 3145736 | tf_op jit(solution)/shard_map/ppermute | solution.py:60
  551.6 159.8 %collective-permute-start.55 = (bf16[2048,512]{1,0:T(8,128)(2,1)}, bf16[2048,512]{1,0:T(8,128)(2,1)}, u32[]{:S(2)}, u32[]{:S(2)}) collective-permute-start(bf16[2048,512]{1,0:T(8,128)(2,1)} %get-tuple-element.194), channel_id=1, source_target_pairs={{0,1},{1,0},{2,3},{3,2},{4,5},{5,4},{6,7},{7,6},{8,9},{9,8},{10,11... | collective-permute-start | bytes 6291464 | tf_op jit(solution)/shard_map/ppermute | solution.py:60
  557.8 157.5 %collective-permute-start.54 = (bf16[2048,512]{1,0:T(8,128)(2,1)}, bf16[2048,512]{1,0:T(8,128)(2,1)}, u32[]{:S(2)}, u32[]{:S(2)}) collective-permute-start(bf16[2048,512]{1,0:T(8,128)(2,1)} %get-tuple-element.192), channel_id=1, source_target_pairs={{0,1},{1,0},{2,3},{3,2},{4,5},{5,4},{6,7},{7,6},{8,9},{9,8},{10,11... | collective-permute-start | bytes 6291464 | tf_op jit(solution)/shard_map/ppermute | solution.py:60
  560.6 158.6 %collective-permute-start.53 = (bf16[2048,512]{1,0:T(8,128)(2,1)}, bf16[2048,512]{1,0:T(8,128)(2,1)}, u32[]{:S(2)}, u32[]{:S(2)}) collective-permute-start(bf16[2048,512]{1,0:T(8,128)(2,1)} %get-tuple-element.190), channel_id=1, source_target_pairs={{0,1},{1,0},{2,3},{3,2},{4,5},{5,4},{6,7},{7,6},{8,9},{9,8},{10,11... | collective-permute-start | bytes 6291464 | tf_op jit(solution)/shard_map/ppermute | solution.py:60
  577.0 17.7 %collective-permute-start.39 = (bf16[512,512]{1,0:T(8,128)(2,1)}, bf16[512,512]{1,0:T(8,128)(2,1)}, u32[]{:S(2)}, u32[]{:S(2)}) collective-permute-start(bf16[512,512]{1,0:T(8,128)(2,1)} %get-tuple-element.163), channel_id=1, source_target_pairs={{0,4},{1,5},{2,6},{3,7},{4,0},{5,1},{6,2},{7,3},{8,12},{9,13},{10,... | collective-permute-start | bytes 1572872 | tf_op jit(solution)/shard_map/ppermute | solution.py:60
  634.4 142.2 %all-to-all-start.1 = ((bf16[8,3,88,256]{3,2,1,0:T(8,128)(2,1)}), bf16[8,3,88,256]{3,2,1,0:T(8,128)(2,1)}, u32[]{:S(2)}, u32[]{:S(2)}) async-start(bf16[8,3,88,256]{3,2,1,0:T(8,128)(2,1)} %maximum_bitcast_fusion.1), calls=%async_computation.3 | async-start | bytes 2162688 | tf_op jit(solution)/shard_map/all_to_all | solution.py:625
  638.8 321.4 %reduce-scatter.5.cloned.1.call-start = ((), (), s32[]{:S(2)}) async-start(), calls=%async_computation.7 | async-start | bytes 2359296 | tf_op jit(solution)/shard_map/reduce_scatter | solution.py:645
  638.8 25.7 %collective-permute-start.44 = (bf16[256,512]{1,0:T(8,128)(2,1)S(1)}, bf16[256,512]{1,0:T(8,128)(2,1)S(1)}, u32[]{:S(2)}, u32[]{:S(2)}) collective-permute-start(bf16[256,512]{1,0:T(8,128)(2,1)S(1)} %copy-done.87), channel_id=1, source_target_pairs={{0,8},{1,9},{2,10},{3,11},{4,12},{5,13},{6,14},{7,15},{8,0},{9,1},... | collective-permute-start | bytes 786440 | tf_op jit(solution)/shard_map/ppermute | solution.py:60
  640.8 29.4 %collective-permute-start.43 = (bf16[256,512]{1,0:T(8,128)(2,1)S(1)}, bf16[256,512]{1,0:T(8,128)(2,1)S(1)}, u32[]{:S(2)}, u32[]{:S(2)}) collective-permute-start(bf16[256,512]{1,0:T(8,128)(2,1)S(1)} %copy-done.84), channel_id=1, source_target_pairs={{0,8},{1,9},{2,10},{3,11},{4,12},{5,13},{6,14},{7,15},{8,0},{9,1},... | collective-permute-start | bytes 786440 | tf_op jit(solution)/shard_map/ppermute | solution.py:60
  675.1 48.0 %collective-permute-start.56 = (bf16[2048,512]{1,0:T(8,128)(2,1)S(1)}, bf16[2048,512]{1,0:T(8,128)(2,1)S(1)}, u32[]{:S(2)}, u32[]{:S(2)}) collective-permute-start(bf16[2048,512]{1,0:T(8,128)(2,1)S(1)} %copy-done.116), channel_id=1, source_target_pairs={{0,1},{1,0},{2,3},{3,2},{4,5},{5,4},{6,7},{7,6},{8,9},{9,8},{10,11... | collective-permute-start | bytes 6291464 | tf_op jit(solution)/shard_map/ppermute | solution.py:60
  710.3 31.5 %collective-permute-start.49 = (bf16[128,2048]{1,0:T(8,128)(2,1)}, bf16[128,2048]{1,0:T(8,128)(2,1)}, u32[]{:S(2)}, u32[]{:S(2)}) collective-permute-start(bf16[128,2048]{1,0:T(8,128)(2,1)} %get-tuple-element.321), channel_id=1, source_target_pairs={{0,2},{1,3},{2,0},{3,1},{4,6},{5,7},{6,4},{7,5},{8,10},{9,11},{10,... | collective-permute-start | bytes 1572872 | tf_op jit(solution)/shard_map/ppermute | solution.py:60
  724.7 26.3 %collective-permute-start.59 = (bf16[1024,512]{1,0:T(8,128)(2,1)}, bf16[1024,512]{1,0:T(8,128)(2,1)}, u32[]{:S(2)}, u32[]{:S(2)}) collective-permute-start(bf16[1024,512]{1,0:T(8,128)(2,1)} %get-tuple-element.199), channel_id=1, source_target_pairs={{0,2},{1,3},{2,0},{3,1},{4,6},{5,7},{6,4},{7,5},{8,10},{9,11},{10,... | collective-permute-start | bytes 3145736 | tf_op jit(solution)/shard_map/ppermute | solution.py:60
  725.6 28.4 %collective-permute-start.58 = (bf16[1024,512]{1,0:T(8,128)(2,1)}, bf16[1024,512]{1,0:T(8,128)(2,1)}, u32[]{:S(2)}, u32[]{:S(2)}) collective-permute-start(bf16[1024,512]{1,0:T(8,128)(2,1)} %get-tuple-element.198), channel_id=1, source_target_pairs={{0,4},{1,5},{2,6},{3,7},{4,0},{5,1},{6,2},{7,3},{8,12},{9,13},{10,... | collective-permute-start | bytes 3145736 | tf_op jit(solution)/shard_map/ppermute | solution.py:60
  735.8 29.9 %collective-permute-start.57 = (bf16[1024,512]{1,0:T(8,128)(2,1)}, bf16[1024,512]{1,0:T(8,128)(2,1)}, u32[]{:S(2)}, u32[]{:S(2)}) collective-permute-start(bf16[1024,512]{1,0:T(8,128)(2,1)} %get-tuple-element.197), channel_id=1, source_target_pairs={{0,2},{1,3},{2,0},{3,1},{4,6},{5,7},{6,4},{7,5},{8,10},{9,11},{10,... | collective-permute-start | bytes 3145736 | tf_op jit(solution)/shard_map/ppermute | solution.py:60
  741.8 27.9 %collective-permute-start.60 = (bf16[1024,512]{1,0:T(8,128)(2,1)}, bf16[1024,512]{1,0:T(8,128)(2,1)S(1)}, u32[]{:S(2)}, u32[]{:S(2)}) collective-permute-start(bf16[1024,512]{1,0:T(8,128)(2,1)} %get-tuple-element.200), channel_id=1, source_target_pairs={{0,4},{1,5},{2,6},{3,7},{4,0},{5,1},{6,2},{7,3},{8,12},{9,13},{10,... | collective-permute-start | bytes 3145736 | tf_op jit(solution)/shard_map/ppermute | solution.py:60
  744.2 35.5 %collective-permute-start.50 = (bf16[256,2048]{1,0:T(8,128)(2,1)}, bf16[256,2048]{1,0:T(8,128)(2,1)}, u32[]{:S(2)}, u32[]{:S(2)}) collective-permute-start(bf16[256,2048]{1,0:T(8,128)(2,1)} %pad_maximum_fusion.12), channel_id=1, source_target_pairs={{0,1},{1,0},{2,3},{3,2},{4,5},{5,4},{6,7},{7,6},{8,9},{9,8},{10,11... | collective-permute-start | bytes 3145736 | tf_op jit(solution)/shard_map/ppermute | solution.py:60
  771.2 54.9 %collective-permute-start.63 = (bf16[512,512]{1,0:T(8,128)(2,1)}, bf16[512,512]{1,0:T(8,128)(2,1)}, u32[]{:S(2)}, u32[]{:S(2)}) collective-permute-start(bf16[512,512]{1,0:T(8,128)(2,1)} %get-tuple-element.203), channel_id=1, source_target_pairs={{0,4},{1,5},{2,6},{3,7},{4,0},{5,1},{6,2},{7,3},{8,12},{9,13},{10,... | collective-permute-start | bytes 1572872 | tf_op jit(solution)/shard_map/ppermute | solution.py:60
  774.6 53.8 %collective-permute-start.62 = (bf16[512,512]{1,0:T(8,128)(2,1)}, bf16[512,512]{1,0:T(8,128)(2,1)}, u32[]{:S(2)}, u32[]{:S(2)}) collective-permute-start(bf16[512,512]{1,0:T(8,128)(2,1)} %get-tuple-element.202), channel_id=1, source_target_pairs={{0,2},{1,3},{2,0},{3,1},{4,6},{5,7},{6,4},{7,5},{8,10},{9,11},{10,... | collective-permute-start | bytes 1572872 | tf_op jit(solution)/shard_map/ppermute | solution.py:60
  775.5 55.1 %collective-permute-start.61 = (bf16[512,512]{1,0:T(8,128)(2,1)}, bf16[512,512]{1,0:T(8,128)(2,1)}, u32[]{:S(2)}, u32[]{:S(2)}) collective-permute-start(bf16[512,512]{1,0:T(8,128)(2,1)} %get-tuple-element.201), channel_id=1, source_target_pairs={{0,4},{1,5},{2,6},{3,7},{4,0},{5,1},{6,2},{7,3},{8,12},{9,13},{10,... | collective-permute-start | bytes 1572872 | tf_op jit(solution)/shard_map/ppermute | solution.py:60
  775.5 57.3 %collective-permute-start.64 = (bf16[512,512]{1,0:T(8,128)(2,1)}, bf16[512,512]{1,0:T(8,128)(2,1)}, u32[]{:S(2)}, u32[]{:S(2)}) collective-permute-start(bf16[512,512]{1,0:T(8,128)(2,1)} %get-tuple-element.204), channel_id=1, source_target_pairs={{0,2},{1,3},{2,0},{3,1},{4,6},{5,7},{6,4},{7,5},{8,10},{9,11},{10,... | collective-permute-start | bytes 1572872 | tf_op jit(solution)/shard_map/ppermute | solution.py:60
  792.0 192.1 %reduce-scatter.3.cloned.1.call-start = ((), (), s32[]{:S(2)}) async-start(), calls=%async_computation.6 | async-start | bytes 4718592 | tf_op jit(solution)/shard_map/reduce_scatter | solution.py:701
  837.7 17.8 %collective-permute-start.52 = (bf16[128,2688]{1,0:T(8,128)(2,1)}, bf16[128,2688]{1,0:T(8,128)(2,1)}, u32[]{:S(2)}, u32[]{:S(2)}) collective-permute-start(bf16[128,2688]{1,0:T(8,128)(2,1)} %slice.1396), channel_id=1, source_target_pairs={{0,2},{1,3},{2,0},{3,1},{4,6},{5,7},{6,4},{7,5},{8,10},{9,11},{10,... | collective-permute-start | bytes 2064392 | tf_op jit(solution)/shard_map/ppermute | solution.py:60
  842.7 42.5 %collective-permute-start.67 = (bf16[256,512]{1,0:T(8,128)(2,1)}, bf16[256,512]{1,0:T(8,128)(2,1)}, u32[]{:S(2)}, u32[]{:S(2)}) collective-permute-start(bf16[256,512]{1,0:T(8,128)(2,1)} %get-tuple-element.207), channel_id=1, source_target_pairs={{0,8},{1,9},{2,10},{3,11},{4,12},{5,13},{6,14},{7,15},{8,0},{9,1},... | collective-permute-start | bytes 786440 | tf_op jit(solution)/shard_map/ppermute | solution.py:60
  844.7 42.1 %collective-permute-start.66 = (bf16[256,512]{1,0:T(8,128)(2,1)}, bf16[256,512]{1,0:T(8,128)(2,1)}, u32[]{:S(2)}, u32[]{:S(2)}) collective-permute-start(bf16[256,512]{1,0:T(8,128)(2,1)} %get-tuple-element.206), channel_id=1, source_target_pairs={{0,8},{1,9},{2,10},{3,11},{4,12},{5,13},{6,14},{7,15},{8,0},{9,1},... | collective-permute-start | bytes 786440 | tf_op jit(solution)/shard_map/ppermute | solution.py:60
  844.8 43.0 %collective-permute-start.65 = (bf16[256,512]{1,0:T(8,128)(2,1)}, bf16[256,512]{1,0:T(8,128)(2,1)}, u32[]{:S(2)}, u32[]{:S(2)}) collective-permute-start(bf16[256,512]{1,0:T(8,128)(2,1)} %get-tuple-element.205), channel_id=1, source_target_pairs={{0,8},{1,9},{2,10},{3,11},{4,12},{5,13},{6,14},{7,15},{8,0},{9,1},... | collective-permute-start | bytes 786440 | tf_op jit(solution)/shard_map/ppermute | solution.py:60
  885.1 39.3 %collective-permute-start.73 = (bf16[1024,640]{1,0:T(8,128)(2,1)S(1)}, bf16[1024,640]{1,0:T(8,128)(2,1)S(1)}, u32[]{:S(2)}, u32[]{:S(2)}) collective-permute-start(bf16[1024,640]{1,0:T(8,128)(2,1)S(1)} %bitcast.231), channel_id=1, source_target_pairs={{0,1},{1,0},{2,3},{3,2},{4,5},{5,4},{6,7},{7,6},{8,9},{9,8},{10,11... | collective-permute-start | bytes 3932168 | tf_op jit(solution)/shard_map/ppermute | solution.py:60
  888.8 26.3 %collective-permute-start.69 = (bf16[128,512]{1,0:T(8,128)(2,1)S(1)}, bf16[128,512]{1,0:T(8,128)(2,1)S(1)}, u32[]{:S(2)}, u32[]{:S(2)}) collective-permute-start(bf16[128,512]{1,0:T(8,128)(2,1)S(1)} %fusion.117), channel_id=1, source_target_pairs={{0,16},{1,17},{2,18},{3,19},{4,20},{5,21},{6,22},{7,23},{8,24},{9,... | collective-permute-start | bytes 393224 | tf_op jit(solution)/shard_map/ppermute | solution.py:60
  891.8 31.8 %collective-permute-start.70 = (bf16[128,512]{1,0:T(8,128)(2,1)S(1)}, bf16[128,512]{1,0:T(8,128)(2,1)S(1)}, u32[]{:S(2)}, u32[]{:S(2)}) collective-permute-start(bf16[128,512]{1,0:T(8,128)(2,1)S(1)} %fusion.116), channel_id=1, source_target_pairs={{0,16},{1,17},{2,18},{3,19},{4,20},{5,21},{6,22},{7,23},{8,24},{9,... | collective-permute-start | bytes 393224 | tf_op jit(solution)/shard_map/ppermute | solution.py:60
  892.7 38.6 %collective-permute-start.71 = (bf16[128,512]{1,0:T(8,128)(2,1)S(1)}, bf16[128,512]{1,0:T(8,128)(2,1)S(1)}, u32[]{:S(2)}, u32[]{:S(2)}) collective-permute-start(bf16[128,512]{1,0:T(8,128)(2,1)S(1)} %fusion.115), channel_id=1, source_target_pairs={{0,16},{1,17},{2,18},{3,19},{4,20},{5,21},{6,22},{7,23},{8,24},{9,... | collective-permute-start | bytes 393224 | tf_op jit(solution)/shard_map/ppermute | solution.py:60
  894.7 40.3 %collective-permute-start.72 = (bf16[128,512]{1,0:T(8,128)(2,1)S(1)}, bf16[128,512]{1,0:T(8,128)(2,1)S(1)}, u32[]{:S(2)}, u32[]{:S(2)}) collective-permute-start(bf16[128,512]{1,0:T(8,128)(2,1)S(1)} %copy-done.96), channel_id=1, source_target_pairs={{0,16},{1,17},{2,18},{3,19},{4,20},{5,21},{6,22},{7,23},{8,24},{9,... | collective-permute-start | bytes 393224 | tf_op jit(solution)/shard_map/ppermute | solution.py:60
  925.0 16.4 %collective-permute-start.74 = (bf16[512,640]{1,0:T(8,128)(2,1)S(1)}, bf16[512,640]{1,0:T(8,128)(2,1)S(1)}, u32[]{:S(2)}, u32[]{:S(2)}) collective-permute-start(bf16[512,640]{1,0:T(8,128)(2,1)S(1)} %slice.1397), channel_id=1, source_target_pairs={{0,2},{1,3},{2,0},{3,1},{4,6},{5,7},{6,4},{7,5},{8,10},{9,11},{10,... | collective-permute-start | bytes 1966088 | tf_op jit(solution)/shard_map/ppermute | solution.py:60
  (154 other events, 1408.3 us)
Sparse Core Ops, SparseCore 0:
  16.1 156.6 all-gather.2
  175.6 155.5 all-gather.4
  792.1 71.8 reduce-scatter.4
  867.5 116.5 reduce-scatter.2

commit v3 on v2

--- a/solution.py
+++ b/solution.py
@@ -76,9 +76,13 @@
         (k[half:].astype(F32) + r[half:].astype(F32)).astype(BF)
         for k, r in zip(keeps, receiveds)
     ]
-    upper, follow = tie(upper, follow)
+    first, follow = tie(upper[:2], follow)
+    upper = [*first, *upper[2:]]
     sent = [swap_with(value, mask, count) for value, mask in zip(upper, masks)]
-    lower = [k[:half].astype(F32) + r[:half].astype(F32) for k, r in zip(keeps, receiveds)]
+    lower = [
+        (k[:half].astype(F32) + r[:half].astype(F32)).astype(BF)
+        for k, r in zip(keeps, receiveds)
+    ]
     return lower, sent, follow
 
 
@@ -106,52 +110,71 @@
     return pl.BlockSpec(shape, lambda *_: (0,) * len(shape), pipeline_mode=pl.Buffered(1))
 
 
-def cotangent_rows(ids, slot_rows, slot_weights, cotangents, down_t, common_down_t):
+def cotangent_rows(half, streams, slot_rows, slot_weights, down_t, common_down_t, previous):
     groups, _, slots = slot_rows.shape
     experts, _, width = down_t.shape
     cap = slots // experts
-    rows = cotangents.shape[0] // groups
+    blocks = groups // (2 * GB)
+    rows = streams[0].shape[0] // (groups // 2)
+    part = streams[0].shape[1]
     units = common_down_t.shape[1]
-
-    def body(ids_ref, slot_ref, weight_ref, g0, g1, g2, g3, down_ref, common_ref, rows_ref, dh_ref, dhs_ref):
-        for k, g_ref in enumerate((g0, g1, g2, g3)):
-            value = g_ref[...]
-            picked = dot(one_hot(slot_ref[k], rows), value, ((0,), (0,))).astype(BF)
-            for j in range(experts):
-                rows_ref[j, k * cap : (k + 1) * cap, :] = picked[j * cap : (j + 1) * cap]
-            dhs_ref[k * rows : (k + 1) * rows, :] = dot(value, common_ref[...])
+    count = len(streams)
+
+    def body(*refs):
+        slot_ref, weight_ref = refs[:2]
+        token_refs = refs[2 : 2 + count]
+        down_ref, common_ref = refs[2 + count : 4 + count]
+        rows_ref, dh_ref, dhs_ref = refs[-3:]
+        for k in range(GB):
+            picks = one_hot(slot_ref[k], rows)
+            for s in range(count):
+                picked = dot(
+                    picks, token_refs[s][k * rows : (k + 1) * rows, :], ((0,), (0,))
+                ).astype(BF)
+                for j in range(experts):
+                    rows_ref[j, k * cap : (k + 1) * cap, s * part : (s + 1) * part] = picked[
+                        j * cap : (j + 1) * cap
+                    ]
+        total = dot(token_refs[0][...], common_ref[:part, :])
+        for s in range(1, count):
+            total += dot(token_refs[s][...], common_ref[s * part : (s + 1) * part, :])
+        dhs_ref[...] = total
         for j in range(experts):
             dh_ref[j] = dot(rows_ref[j], down_ref[j]) * weight_ref[j][:, :1]
 
-    def row_block(k):
-        return pl.BlockSpec((rows, D), lambda i, ids: (ids[GB * i + k], 0))
-
+    shift = half * blocks
+    in_specs = [
+        pl.BlockSpec((GB, 1, slots), lambda i: (shift + i, 0, 0)),
+        pl.BlockSpec((experts, GB * cap, LANES), lambda i: (0, shift + i, 0)),
+        *[pl.BlockSpec((GB * rows, part), lambda i: (i, 0)) for _ in streams],
+        resident(down_t.shape),
+        resident(common_down_t.shape),
+    ]
+    operands = [slot_rows, slot_weights, *streams, down_t, common_down_t]
+    aliases = {}
+    if previous is not None:
+        for at, value in enumerate(previous):
+            aliases[len(operands)] = at
+            in_specs.append(pl.BlockSpec(memory_space=pl.ANY))
+            operands.append(value)
     return pl.pallas_call(
         body,
-        grid_spec=pltpu.PrefetchScalarGridSpec(
-            num_scalar_prefetch=1,
-            grid=(groups // GB,),
-            in_specs=[
-                pl.BlockSpec((GB, 1, slots), lambda i, ids: (i, 0, 0)),
-                pl.BlockSpec((experts, GB * cap, LANES), lambda i, ids: (0, i, 0)),
-                *[row_block(k) for k in range(GB)],
-                resident(down_t.shape),
-                resident(common_down_t.shape),
-            ],
-            out_specs=[
-                pl.BlockSpec((experts, GB * cap, D), lambda i, ids: (0, i, 0)),
-                pl.BlockSpec((experts, GB * cap, width), lambda i, ids: (0, i, 0)),
-                pl.BlockSpec((GB * rows, units), lambda i, ids: (i, 0)),
-            ],
-        ),
+        grid=(blocks,),
+        in_specs=in_specs,
+        out_specs=[
+            pl.BlockSpec((experts, GB * cap, D), lambda i: (0, shift + i, 0)),
+            pl.BlockSpec((experts, GB * cap, width), lambda i: (0, shift + i, 0)),
+            pl.BlockSpec((GB * rows, units), lambda i: (shift + i, 0)),
+        ],
         out_shape=[
             jax.ShapeDtypeStruct((experts, groups * cap, D), BF),
             jax.ShapeDtypeStruct((experts, groups * cap, width), F32),
             jax.ShapeDtypeStruct((groups * rows, units), F32),
         ],
+        input_output_aliases=aliases,
         compiler_params=pltpu.CompilerParams(vmem_limit_bytes=VMEM_CAP),
         name="cotangent_rows",
-    )(ids, slot_rows, slot_weights, *([cotangents] * GB), down_t, common_down_t)
+    )(*operands)
 
 
 def expert_hidden(half, streams, order_flags, slot_rows, slot_weights, dh, dhs, weights, previous):
@@ -401,6 +424,22 @@
     common_gu_t = common_gu.T
     common_down_t = common_down.T
 
+    cotangent_part = D // 2
+
+    def first_cotangents(source):
+        return [
+            cube_gather(
+                source[:, s * cotangent_part : (s + 1) * cotangent_part], order_a[:-1], count
+            )
+            for s in range(2)
+        ]
+
+    def last_cotangents(blocks):
+        near = [cube_gather(block, order_a[-1:], count) for block in blocks]
+        return near, [swap_with(block, CORE, count) for block in near]
+
+    cotangent_blocks = first_cotangents(out_cotangent)
+
     expert_local = expert_gate.shape[0]
     expert_total = expert_local * dp_count
     capacity = max(2, 5 * shard_rows * TOPK // (4 * expert_total))
@@ -435,6 +474,9 @@
     packed_full, (ready, slot_rows, slot_weights, input_seq) = tie(
         packed_full, (ready, slot_rows, slot_weights, input_seq)
     )
+    if count <= 32:
+        packed_full, cotangent_blocks[1] = tie(packed_full, cotangent_blocks[1])
+    cotangents_near, cotangents_far = last_cotangents(cotangent_blocks)
     gate_up, gate_up_t, down_pad, down_t, common_gu, common_gu_t, common_down, common_down_t = ready
     at = query_cols
     weight_query = packed_full[:, :at]
@@ -502,20 +544,17 @@
     hidden_state = input_float + mixer_out
     normed_second = root_norm(hidden_state, experts_scale).astype(BF)
 
-    cotangent_all = lax.all_gather(out_cotangent, BOTH, axis=0, tiled=True)
-    grad_rows, grad_hidden, grad_hidden_common = cotangent_rows(
-        group_ids, slot_rows, slot_weights, cotangent_all, down_t, common_down_t
-    )
+    cotangent_kept = None
+    for half, streams in ((0, cotangents_near), (1, cotangents_far)):
+        cotangent_kept = cotangent_rows(
+            half, streams, slot_rows, slot_weights, down_t, common_down_t, cotangent_kept
+        )
+    grad_rows, grad_hidden, grad_hidden_common = cotangent_kept
 
     near = [
-        cube_gather(normed_second[:, s * part : (s + 1) * part], order[:-1], count)
+        cube_gather(normed_second[:, s * part : (s + 1) * part], order, count)
         for s, order in enumerate(stream_orders)
     ]
-    last = [swap_with(block, order[-1], count) for block, order in zip(near, stream_orders)]
-    last, (grad_rows, grad_hidden, grad_hidden_common) = tie(
-        last, (grad_rows, grad_hidden, grad_hidden_common)
-    )
-    near = [jnp.concatenate(pair, axis=0) for pair in zip(near, last)]
     far = [swap_with(block, CORE, count) for block in near]
     hidden_weights = (gate_up, common_gu_t)
     kept = None
@@ -546,8 +585,18 @@
                     grads = jnp.swapaxes(grads.reshape(shape), 0, 1).reshape(half_rows, 2 * unit_pad)
                 total = total + dot(grads, tokens, ((0,), (0,)))
             parts.append(total)
-        grad_common_gu = jnp.concatenate(parts, axis=1)
-        return grad_common_gu
+        return jnp.concatenate(parts, axis=1)
+
+    def common_down_gradient(hidden):
+        half_rows = count // 2 * shard_rows
+        return jnp.concatenate(
+            [
+                dot(hidden[:half_rows], cotangents_near[s], ((0,), (0,)))
+                + dot(hidden[half_rows:], cotangents_far[s], ((0,), (0,)))
+                for s in range(2)
+            ],
+            axis=1,
+        )
 
     if count > 32:
         grad_common_gu = common_gradients(grad_common)
@@ -591,6 +640,7 @@
             (near_results, hidden_late, grad_common_late),
         )
         grad_common_gu = common_gradients(grad_common_late)
+        grad_common_down = common_down_gradient(hidden_common)
         result_lower, result_sent, _ = halve_stage(
             near_results, far_results_received, [turn[0] for turn in turns], count
         )
@@ -599,23 +649,16 @@
     for k in range(3, len(order_a)):
         lower, sent, _ = halve_stage(lower, sent, [turn[k] for turn in turns], count)
     grad_normed_second = jnp.concatenate(
-        [a + b.astype(F32) for a, b in zip(lower, sent)], axis=1
+        [a.astype(F32) + b.astype(F32) for a, b in zip(lower, sent)], axis=1
     )
     grad_expert_down = jnp.stack(
         [dot(hidden_late[j][:, :width], grad_rows[j], ((0,), (0,))) for j in range(expert_local)]
     )
 
-    canon_ids = jnp.zeros((count,), jnp.int32)
-    offset = me ^ canon
-    for bit, mask in enumerate(order_a + (CORE,)):
-        canon_ids = canon_ids + (1 << bit) * ((offset // mask) & 1)
-    hidden_global = jnp.take(
-        hidden_common.reshape(count, shard_rows, unit_pad), canon_ids, axis=0
-    ).reshape(count * shard_rows, unit_pad)
     if count > 32:
-        again, _ = tie(out_cotangent, grad_normed_second)
-        cotangent_all = lax.all_gather(again, BOTH, axis=0, tiled=True)
-    grad_common_down = dot(hidden_global, cotangent_all, ((0,), (0,)))
+        again, grad_normed_second = tie(out_cotangent, grad_normed_second)
+        cotangents_near, cotangents_far = last_cotangents(first_cotangents(again))
+        grad_common_down = common_down_gradient(hidden_common)
     common_grads = jnp.stack(
         [grad_common_gu[:units], grad_common_gu[unit_pad : unit_pad + units], grad_common_down[:units]]
     ).astype(BF)
@@ -737,7 +780,7 @@
             result_lower, result_sent, [turn[k] for turn in turns], count
         )
     result = jnp.concatenate(
-        [a + b.astype(F32) for a, b in zip(result_lower, result_sent)], axis=1
+        [a.astype(F32) + b.astype(F32) for a, b in zip(result_lower, result_sent)], axis=1
     )
     small_terms = jnp.take(small_terms.reshape(count, D // count, latent_pad), group_ids, axis=0)
     small_grads = scatter_rows(small_terms.reshape(D, latent_pad), (CORE,) + order_a[::-1], count)

time: 1000 us -> 1020 us (1.020)
  starting transfers between devices: 78.9 us -> 91.6 us
    ppermute x78 -> x88, waiting for transfers between devices: 305 us -> 402 us  [swap_with(): return lax.ppermute(values, BOTH, [(i, i ^ mask) for i in range(count)])]
    all_gather x1, waiting for transfers between devices: 83.1 us -> 0.02 us  [local(): packed_full = lax.all_gather(packed, 'dp', axis=0, tiled=True)]
    convert_element_type x0 -> x24, other arithmetic: none -> 54 us  [halve_stage(): (k[:half].astype(F32) + r[:half].astype(F32)).astype(BF)]
    add x24 -> x8, other arithmetic: 48.9 us -> 4 us  [local(): a.astype(F32) + b.astype(F32)]
    convert_element_type x16 -> x8, other arithmetic: 18.8 us -> 3.89 us  [halve_stage(): (k[half:].astype(F32) + r[half:].astype(F32)).astype(BF)]
    ppermute x78 -> x88, starting transfers between devices: 69.5 us -> 82 us  [swap_with(): return lax.ppermute(values, BOTH, [(i, i ^ mask) for i in range(count)])]
    pallas_call x1 -> x2, Pallas kernels: 25.6 us -> 29.2 us  [cotangent_rows(): pl.pallas_call(body, grid=(blocks,), in_specs=in_specs, out_specs=[pl.Blo...]
    dot_general x27 -> x30, matrix products: 91.1 us -> 94.2 us  [dot(): lax.dot_general(left, right, (dims, ((), ())), preferred_element_type=F32)]
  transfers between devices with their start and end apart: 84 -> 93, of which waited for: 43 -> 43; matrix products, arithmetic and copies ran while one was open for 33% -> 34% of each run, Pallas kernels for 9% -> 9%
where the time goes in v3:
time: 1020 us; the launch traced here: 1010 us
  waiting for transfers between devices  419 us (41%)
  other arithmetic  138 us (14%)
  Pallas kernels  125 us (12%)
  local copies, waits for them, and re-layouts  122 us (12%)
  matrix products  102 us (10%)
  starting transfers between devices  91.6 us (9%)
  between operations  16.7 us (2%)
    ppermute x88, waiting for transfers between devices, swap_with(): return lax.ppermute(values, BOTH, [(i, i ^ mask) for i in range(count)])  402 us
    dot_general x30, matrix products, dot(): lax.dot_general(left, right, (dims, ((), ())), preferred_element_type=F32)  94.2 us
    ppermute x88, starting transfers between devices, swap_with(): return lax.ppermute(values, BOTH, [(i, i ^ mask) for i in range(count)])  82 us
    pallas_call x4, Pallas kernels, token_terms(): pl.pallas_call(body, grid=(blocks,), in_specs=[pl.BlockSpec((GB, 1, slots...  59.4 us
    convert_element_type x24, other arithmetic, halve_stage(): (k[:half].astype(F32) + r[:half].astype(F32)).astype(BF)  54 us
    pallas_call x2, Pallas kernels, expert_hidden(): pl.pallas_call(body, grid=(blocks,), in_specs=in_specs, out_specs=[pl.Blo...  36.6 us
    unnamed x294, local copies, waits for them, and re-layouts  29.6 us
    pallas_call x2, Pallas kernels, cotangent_rows(): pl.pallas_call(body, grid=(blocks,), in_specs=in_specs, out_specs=[pl.Blo...  29.2 us
  transfers between devices with their start and end apart: 93, of which 43 were waited for; matrix products, arithmetic and copies ran while one was open for 34% of the time, Pallas kernels for 9%

profile of v3, /device:TPU:0, one launch (start us, length us, event | category | flops | bytes accessed | tf_op | source)
XLA Modules:
  0.0 1014.7 jit_solution(10910323206359501994)
XLA Ops:
  17.8 4.1 collective-permute-start
  25.1 4.9 all-to-all-start
  36.7 5.5 pad_bitcast_fusion.1
  42.3 7.7 fusion.164
  53.2 35.6 %collective-permute-done.1 = f32[2,2,1024]{2,1,0:T(2,128)S(1)} collective-permute-done((f32[2,2,1024]{2,1,0:T(2,128)S(1)}, f32[2,2,1024]{2,1,0:T(2,128)S(1)}, u32[]{:S(2)}, u32[]{:S(2)}) %collective-permute-start.1) | collective-permute-done | bytes 16416 | tf_op jit(solution)/shard_map/ppermute | solution.py:60
  91.4 21.8 %collective-permute-done.12 = bf16[128,1024]{1,0:T(8,128)(2,1)S(1)} collective-permute-done((bf16[128,1024]{1,0:T(8,128)(2,1)S(1)}, bf16[128,1024]{1,0:T(8,128)(2,1)S(1)}, u32[]{:S(2)}, u32[]{:S(2)}) %collective-permute-start.12) | collective-permute-done | bytes 262176 | tf_op jit(solution)/shard_map/ppermute | solution.py:60
  118.8 40.0 %collective-permute-done.13 = bf16[256,1024]{1,0:T(8,128)(2,1)S(1)} collective-permute-done((bf16[256,1024]{1,0:T(8,128)(2,1)S(1)}, bf16[256,1024]{1,0:T(8,128)(2,1)S(1)}, u32[]{:S(2)}, u32[]{:S(2)}) %collective-permute-start.13) | collective-permute-done | bytes 524320 | tf_op jit(solution)/shard_map/ppermute | solution.py:60
  161.4 34.7 %collective-permute-done.8 = bf16[256,1024]{1,0:T(8,128)(2,1)S(1)} collective-permute-done((bf16[256,1024]{1,0:T(8,128)(2,1)S(1)}, bf16[256,1024]{1,0:T(8,128)(2,1)S(1)}, u32[]{:S(2)}, u32[]{:S(2)}) %collective-permute-start.8) | collective-permute-done | bytes 524320 | tf_op jit(solution)/shard_map/ppermute | solution.py:60
  209.9 12.6 %collective-permute-done.9 = bf16[512,1024]{1,0:T(8,128)(2,1)} collective-permute-done((bf16[512,1024]{1,0:T(8,128)(2,1)}, bf16[512,1024]{1,0:T(8,128)(2,1)}, u32[]{:S(2)}, u32[]{:S(2)}) %collective-permute-start.9) | collective-permute-done | bytes 1048608 | tf_op jit(solution)/shard_map/ppermute | solution.py:60
  274.4 9.2 collective-permute-done.11
  290.3 8.8 collective-permute-done.34
  305.4 6.7 collective-permute-done.35
  317.7 5.8 collective-permute-done.25
  325.0 13.9 %collective-permute-done.36 = bf16[512,512]{1,0:T(8,128)(2,1)S(1)} collective-permute-done((bf16[512,512]{1,0:T(8,128)(2,1)S(1)}, bf16[512,512]{1,0:T(8,128)(2,1)S(1)}, u32[]{:S(2)}, u32[]{:S(2)}) %collective-permute-start.36) | collective-permute-done | bytes 524320 | tf_op jit(solution)/shard_map/ppermute | solution.py:60
  346.3 5.7 collective-permute-done.26
  353.5 22.3 %collective-permute-done.21 = bf16[512,512]{1,0:T(8,128)(2,1)S(1)} collective-permute-done((bf16[512,512]{1,0:T(8,128)(2,1)S(1)}, bf16[512,512]{1,0:T(8,128)(2,1)S(1)}, u32[]{:S(2)}, u32[]{:S(2)}) %collective-permute-start.21) | collective-permute-done | bytes 524320 | tf_op jit(solution)/shard_map/ppermute | solution.py:60
  384.9 14.2 %collective-permute-done.27 = bf16[1024,512]{1,0:T(8,128)(2,1)S(1)} collective-permute-done((bf16[1024,512]{1,0:T(8,128)(2,1)S(1)}, bf16[1024,512]{1,0:T(8,128)(2,1)S(1)}, u32[]{:S(2)}, u32[]{:S(2)}) %collective-permute-start.27) | collective-permute-done | bytes 1048608 | tf_op jit(solution)/shard_map/ppermute | solution.py:60
  402.5 4.7 copy.301.refs_4_
  408.2 8.6 copy.305.refs_8_
  419.2 14.8 %cotangent_rows.2 = (bf16[2,2048,2048]{2,1,0:T(8,128)(2,1)}, f32[2,2048,384]{2,1,0:T(8,128)}, f32[4096,128]{1,0:T(8,128)}) custom-call(s32[32,1,128]{2,1,0:T(1,128)} %get-tuple-element.147.refs_0_.slot_ref, f32[2,2048,128]{2,1,0:T(8,128)} %broadcast_in_dim.136.refs_1_, bf16[2048,1024]{1,0:T(8,128)(2,1)} %copy-done.8, ...), custom_call_target="tpu_custom_call" | custom-call | tf_op jit(solution)/shard_map/cotangent_rows/pallas_call | solution.py:160
  434.0 14.4 %cotangent_rows.3 = (bf16[2,2048,2048]{2,1,0:T(8,128)(2,1)}, f32[2,2048,384]{2,1,0:T(8,128)}, f32[4096,128]{1,0:T(8,128)}) custom-call(s32[32,1,128]{2,1,0:T(1,128)} %get-tuple-element.147.refs_0_.slot_ref, f32[2,2048,128]{2,1,0:T(8,128)} %broadcast_in_dim.136.refs_1_, ...), custom_call_target="tpu_custom_call", output_to_operand_aliasing={{0}: (6, {}), {1}: (7, {}), {2}: (8, {})} | custom-call | tf_op jit(solution)/shard_map/cotangent_rows/pallas_call | solution.py:160
  448.4 18.3 %expert_hidden.2 = (bf16[2,2048,2048]{2,1,0:T(8,128)(2,1)}, bf16[2,2048,384]{2,1,0:T(8,128)(2,1)}, bf16[2,2048,768]{2,1,0:T(8,128)(2,1)}, bf16[4096,128]{1,0:T(8,128)(2,1)}, bf16[4096,256]{1,0:T(8,128)(2,1)}) custom-call(s32[32,1,128]{2,1,0:T(1,128)} %get-tuple-element.147.refs_0_.slot_ref, f32[2,2048,128]{2,1,0:T(8,128)} %broadcast_in_dim.136.refs_1_, ...), custom_call_target="tpu_custom_call" | custom-call | tf_op jit(solution)/shard_map/expert_hidden/pallas_call | solution.py:250
  466.8 18.3 %expert_hidden.3 = (bf16[2,2048,2048]{2,1,0:T(8,128)(2,1)}, bf16[2,2048,384]{2,1,0:T(8,128)(2,1)}, bf16[2,2048,768]{2,1,0:T(8,128)(2,1)}, bf16[4096,128]{1,0:T(8,128)(2,1)}, bf16[4096,256]{1,0:T(8,128)(2,1)}) custom-call(s32[32,1,128]{2,1,0:T(1,128)} %get-tuple-element.147.refs_0_.slot, ...), custom_call_target="tpu_custom_call", output_to_operand_aliasing={{0}: (10, {}), {1}: (11, {}), {2}: (12, {}), {3}: (13, {}),... | custom-call | tf_op jit(solution)/shard_map/expert_hidden/pallas_call | solution.py:250
  485.1 16.5 %token_terms.4 = (bf16[2048,512]{1,0:T(8,128)(2,1)}, bf16[2048,512]{1,0:T(8,128)(2,1)}, bf16[2048,512]{1,0:T(8,128)(2,1)}, bf16[2048,512]{1,0:T(8,128)(2,1)}) custom-call(s32[32,1,128]{2,1,0:T(1,128)} %get-tuple-element.147.refs_0_.slot_ref, bf16[2,2048,768]{2,1,0:T(8,128)(2,1)} %get-tuple-element.179.value_ref, ...), custom_call_target="tpu_custom_call" | custom-call | tf_op jit(solution)/shard_map/token_terms/pallas_call | solution.py:297
  503.7 16.6 %token_terms.5 = (bf16[2048,512]{1,0:T(8,128)(2,1)}, bf16[2048,512]{1,0:T(8,128)(2,1)}, bf16[2048,512]{1,0:T(8,128)(2,1)}, bf16[2048,512]{1,0:T(8,128)(2,1)}) custom-call(s32[32,1,128]{2,1,0:T(1,128)} %get-tuple-element.147.refs_0_.slot_ref, bf16[2,2048,768]{2,1,0:T(8,128)(2,1)} %get-tuple-element.179.value_ref, ...), custom_call_target="tpu_custom_call" | custom-call | tf_op jit(solution)/shard_map/token_terms/pallas_call | solution.py:297
  533.2 4.0 add_convert_fusion.12
  541.6 5.0 fusion.26
  546.6 5.0 fusion.29
  555.3 13.3 %token_terms.6 = (bf16[2048,512]{1,0:T(8,128)(2,1)}, bf16[2048,512]{1,0:T(8,128)(2,1)}, bf16[2048,512]{1,0:T(8,128)(2,1)}, bf16[2048,512]{1,0:T(8,128)(2,1)}) custom-call(s32[32,1,128]{2,1,0:T(1,128)} %get-tuple-element.147.refs_0_.slot_ref, bf16[2,2048,384]{2,1,0:T(8,128)(2,1)} %get-tuple-element.180.value_ref, ...), custom_call_target="tpu_custom_call" | custom-call | tf_op jit(solution)/shard_map/token_terms/pallas_call | solution.py:297
  568.6 13.0 %token_terms.7 = (bf16[2048,512]{1,0:T(8,128)(2,1)}, bf16[2048,512]{1,0:T(8,128)(2,1)}, bf16[2048,512]{1,0:T(8,128)(2,1)}, bf16[2048,512]{1,0:T(8,128)(2,1)}) custom-call(s32[32,1,128]{2,1,0:T(1,128)} %get-tuple-element.147.refs_0_.slot_ref, bf16[2,2048,384]{2,1,0:T(8,128)(2,1)} %get-tuple-element.180.value_ref, ...), custom_call_target="tpu_custom_call" | custom-call | tf_op jit(solution)/shard_map/token_terms/pallas_call | solution.py:297
  583.1 3.9 add_convert_fusion.9
  587.8 5.9 pad_maximum_fusion
  599.2 6.2 fusion.32
  619.7 7.5 collective-permute-done.44
  654.1 4.4 all-to-all-start.1
  658.8 5.8 fusion.38
  664.7 5.7 fusion.41
  677.9 8.7 collective-permute-done.46
  686.7 5.6 collective-permute-done.45
  692.3 5.6 collective-permute-done.52
  703.5 5.4 collective-permute-done.47
  709.4 5.3 collective-permute-done.48
  715.3 5.4 collective-permute-done.53
  721.2 7.4 collective-permute-done.58
  737.1 5.6 collective-permute-start.59
  758.1 3.8 collective-permute-done.66
  764.4 13.8 %collective-permute-done.65 = bf16[1024,512]{1,0:T(8,128)(2,1)S(1)} collective-permute-done((bf16[1024,512]{1,0:T(8,128)(2,1)}, bf16[1024,512]{1,0:T(8,128)(2,1)S(1)}, u32[]{:S(2)}, u32[]{:S(2)}) %collective-permute-start.65) | collective-permute-done | bytes 1048608 | tf_op jit(solution)/shard_map/ppermute | solution.py:60
  783.1 17.5 %collective-permute-done.74 = bf16[1024,512]{1,0:T(8,128)(2,1)S(1)} collective-permute-done((bf16[1024,512]{1,0:T(8,128)(2,1)S(1)}, bf16[1024,512]{1,0:T(8,128)(2,1)S(1)}, u32[]{:S(2)}, u32[]{:S(2)}) %collective-permute-start.74) | collective-permute-done | bytes 1048608 | tf_op jit(solution)/shard_map/ppermute | solution.py:60
  810.1 4.2 convolution_convert_fusion.2
  832.3 5.2 convolution_convert_fusion.3
  837.5 5.3 concatenate.230
  852.2 4.5 pad_maximum_fusion.3
  872.2 7.6 collective-permute-done.62
  886.4 4.3 fusion.78
  892.3 6.6 concatenate.237
  898.9 4.3 gather_fusion.1
  916.1 17.6 %collective-permute-done.71 = bf16[128,512]{1,0:T(8,128)(2,1)S(1)} collective-permute-done((bf16[128,512]{1,0:T(8,128)(2,1)S(1)}, bf16[128,512]{1,0:T(8,128)(2,1)S(1)}, u32[]{:S(2)}, u32[]{:S(2)}) %collective-permute-start.71) | collective-permute-done | bytes 131104 | tf_op jit(solution)/shard_map/ppermute | solution.py:60
  934.7 7.8 collective-permute-done.72
  945.0 6.0 collective-permute-done.77
  951.9 5.4 collective-permute-done.82
  963.0 11.9 %collective-permute-done.85 = bf16[256,640]{1,0:T(8,128)(2,1)S(1)} collective-permute-done((bf16[256,640]{1,0:T(8,128)(2,1)S(1)}, bf16[256,640]{1,0:T(8,128)(2,1)S(1)}, u32[]{:S(2)}, u32[]{:S(2)}) %collective-permute-start.85) | collective-permute-done | bytes 327712 | tf_op jit(solution)/shard_map/ppermute | solution.py:60
  975.9 5.0 collective-permute-done.86
  983.1 3.8 collective-permute-done.87
  988.3 16.1 %reduce-scatter.3.cloned.1.call-done = bf16[256,1024]{0,1:T(8,128)(2,1)} async-done(((bf16[2048,1024]{0,1:T(8,128)(2,1)}), bf16[256,1024]{0,1:T(8,128)(2,1)}) %reduce-scatter.3.cloned.1.call-update) | async-done | bytes 524304 | tf_op jit(solution)/shard_map/reduce_scatter | solution.py:744
  (692 shorter events, 353.0 us)
Async XLA Ops:
  7.2 220.7 %all-gather.2.cloned.1.call-start = ((), (), s32[]{:S(2)}) async-start(), calls=%async_computation.4 | async-start | bytes 10027008 | tf_op jit(solution)/shard_map/all_gather | solution.py:404
  17.8 32.8 %collective-permute-start = (f32[1,2,1024]{2,1,0:T(2,128)S(1)}, f32[1,2,1024]{2,1,0:T(2,128)S(1)}, u32[]{:S(2)}, u32[]{:S(2)}) collective-permute-start(f32[1,2,1024]{2,1,0:T(2,128)S(1)} %maximum_bitcast_fusion.2), channel_id=1, source_target_pairs={{0,16},{1,17},{2,18},{3,19},{4,20},{5,21},{6,22},{7,23},{8,24},{9,... | collective-permute-start | bytes 24584 | tf_op jit(solution)/shard_map/ppermute | solution.py:60
  25.1 200.2 %all-to-all-start = ((bf16[8,3,88,256]{3,2,1,0:T(8,128)(2,1)}), bf16[8,3,88,256]{3,2,1,0:T(8,128)(2,1)}, u32[]{:S(2)}, u32[]{:S(2)}) async-start(bf16[8,3,88,256]{3,2,1,0:T(8,128)(2,1)} %copy.284), calls=%async_computation | async-start | bytes 2162688 | tf_op jit(solution)/shard_map/all_to_all | solution.py:417
  30.1 86.9 %collective-permute-start.5 = (bf16[128,2048]{1,0:T(8,128)(2,1)S(1)}, bf16[128,2048]{1,0:T(8,128)(2,1)S(1)}, u32[]{:S(2)}, u32[]{:S(2)}) collective-permute-start(bf16[128,2048]{1,0:T(8,128)(2,1)S(1)} %copy-done.13), channel_id=1, source_target_pairs={{0,2},{1,3},{2,0},{3,1},{4,6},{5,7},{6,4},{7,5},{8,10},{9,11},{10,... | collective-permute-start | bytes 1572872 | tf_op jit(solution)/shard_map/ppermute | solution.py:60
  32.4 80.9 %collective-permute-start.7 = (bf16[128,1024]{1,0:T(8,128)(2,1)S(1)}, bf16[128,1024]{1,0:T(8,128)(2,1)S(1)}, u32[]{:S(2)}, u32[]{:S(2)}) collective-permute-start(bf16[128,1024]{1,0:T(8,128)(2,1)S(1)} %get-tuple-element.375), channel_id=1, source_target_pairs={{0,16},{1,17},{2,18},{3,19},{4,20},{5,21},{6,22},{7,23},{8,24},{9,... | collective-permute-start | bytes 786440 | tf_op jit(solution)/shard_map/ppermute | solution.py:60
  35.3 77.9 %collective-permute-start.12 = (bf16[128,1024]{1,0:T(8,128)(2,1)S(1)}, bf16[128,1024]{1,0:T(8,128)(2,1)S(1)}, u32[]{:S(2)}, u32[]{:S(2)}) collective-permute-start(bf16[128,1024]{1,0:T(8,128)(2,1)S(1)} %get-tuple-element.373), channel_id=1, source_target_pairs={{0,16},{1,17},{2,18},{3,19},{4,20},{5,21},{6,22},{7,23},{8,24},{9,... | collective-permute-start | bytes 786440 | tf_op jit(solution)/shard_map/ppermute | solution.py:60
  50.6 38.2 %collective-permute-start.1 = (f32[2,2,1024]{2,1,0:T(2,128)S(1)}, f32[2,2,1024]{2,1,0:T(2,128)S(1)}, u32[]{:S(2)}, u32[]{:S(2)}) collective-permute-start(f32[2,2,1024]{2,1,0:T(2,128)S(1)} %pad_maximum_fusion.46), channel_id=1, source_target_pairs={{0,8},{1,9},{2,10},{3,11},{4,12},{5,13},{6,14},{7,15},{8,0},{9,1},... | collective-permute-start | bytes 49160 | tf_op jit(solution)/shard_map/ppermute | solution.py:60
  88.9 26.6 %collective-permute-start.2 = (f32[4,2,1024]{2,1,0:T(2,128)S(1)}, f32[4,2,1024]{2,1,0:T(2,128)S(1)}, u32[]{:S(2)}, u32[]{:S(2)}) collective-permute-start(f32[4,2,1024]{2,1,0:T(2,128)S(1)} %pad_maximum_fusion.45), channel_id=1, source_target_pairs={{0,4},{1,5},{2,6},{3,7},{4,0},{5,1},{6,2},{7,3},{8,12},{9,13},{10,... | collective-permute-start | bytes 98312 | tf_op jit(solution)/shard_map/ppermute | solution.py:60
  113.2 45.6 %collective-permute-start.13 = (bf16[256,1024]{1,0:T(8,128)(2,1)S(1)}, bf16[256,1024]{1,0:T(8,128)(2,1)S(1)}, u32[]{:S(2)}, u32[]{:S(2)}) collective-permute-start(bf16[256,1024]{1,0:T(8,128)(2,1)S(1)} %pad_maximum_fusion.28), channel_id=1, source_target_pairs={{0,8},{1,9},{2,10},{3,11},{4,12},{5,13},{6,14},{7,15},{8,0},{9,1},... | collective-permute-start | bytes 1572872 | tf_op jit(solution)/shard_map/ppermute | solution.py:60
  113.4 82.7 %collective-permute-start.8 = (bf16[256,1024]{1,0:T(8,128)(2,1)S(1)}, bf16[256,1024]{1,0:T(8,128)(2,1)S(1)}, u32[]{:S(2)}, u32[]{:S(2)}) collective-permute-start(bf16[256,1024]{1,0:T(8,128)(2,1)S(1)} %pad_maximum_fusion.27), channel_id=1, source_target_pairs={{0,8},{1,9},{2,10},{3,11},{4,12},{5,13},{6,14},{7,15},{8,0},{9,1},... | collective-permute-start | bytes 1572872 | tf_op jit(solution)/shard_map/ppermute | solution.py:60
  115.5 83.2 %collective-permute-start.3 = (f32[8,2,1024]{2,1,0:T(2,128)S(1)}, f32[8,2,1024]{2,1,0:T(2,128)S(1)}, u32[]{:S(2)}, u32[]{:S(2)}) collective-permute-start(f32[8,2,1024]{2,1,0:T(2,128)S(1)} %pad_maximum_fusion.42), channel_id=1, source_target_pairs={{0,2},{1,3},{2,0},{3,1},{4,6},{5,7},{6,4},{7,5},{8,10},{9,11},{10,... | collective-permute-start | bytes 196616 | tf_op jit(solution)/shard_map/ppermute | solution.py:60
  118.1 85.9 %collective-permute-start.6 = (bf16[256,2048]{1,0:T(8,128)(2,1)}, bf16[256,2048]{1,0:T(8,128)(2,1)}, u32[]{:S(2)}, u32[]{:S(2)}) collective-permute-start(bf16[256,2048]{1,0:T(8,128)(2,1)} %pad_maximum_fusion.8), channel_id=1, source_target_pairs={{0,1},{1,0},{2,3},{3,2},{4,5},{5,4},{6,7},{7,6},{8,9},{9,8},{10,11... | collective-permute-start | bytes 3145736 | tf_op jit(solution)/shard_map/ppermute | solution.py:60
  160.0 45.6 %collective-permute-start.14 = (bf16[512,1024]{1,0:T(8,128)(2,1)}, bf16[512,1024]{1,0:T(8,128)(2,1)}, u32[]{:S(2)}, u32[]{:S(2)}) collective-permute-start(bf16[512,1024]{1,0:T(8,128)(2,1)} %pad_maximum_fusion.10), channel_id=1, source_target_pairs={{0,4},{1,5},{2,6},{3,7},{4,0},{5,1},{6,2},{7,3},{8,12},{9,13},{10,... | collective-permute-start | bytes 3145736 | tf_op jit(solution)/shard_map/ppermute | solution.py:60
  197.2 25.3 %collective-permute-start.9 = (bf16[512,1024]{1,0:T(8,128)(2,1)}, bf16[512,1024]{1,0:T(8,128)(2,1)}, u32[]{:S(2)}, u32[]{:S(2)}) collective-permute-start(bf16[512,1024]{1,0:T(8,128)(2,1)} %pad_maximum_fusion.9), channel_id=1, source_target_pairs={{0,4},{1,5},{2,6},{3,7},{4,0},{5,1},{6,2},{7,3},{8,12},{9,13},{10,... | collective-permute-start | bytes 3145736 | tf_op jit(solution)/shard_map/ppermute | solution.py:60
  208.4 63.2 %collective-permute-start.15 = (bf16[1024,1024]{1,0:T(8,128)(2,1)}, bf16[1024,1024]{1,0:T(8,128)(2,1)}, u32[]{:S(2)}, u32[]{:S(2)}) collective-permute-start(bf16[1024,1024]{1,0:T(8,128)(2,1)} %pad_maximum_fusion.6), channel_id=1, source_target_pairs={{0,2},{1,3},{2,0},{3,1},{4,6},{5,7},{6,4},{7,5},{8,10},{9,11},{10,... | collective-permute-start | bytes 6291464 | tf_op jit(solution)/shard_map/ppermute | solution.py:60
  273.6 128.1 %collective-permute-start.16 = (bf16[2048,1024]{1,0:T(8,128)(2,1)S(1)}, bf16[2048,1024]{1,0:T(8,128)(2,1)}, u32[]{:S(2)}, u32[]{:S(2)}) collective-permute-start(bf16[2048,1024]{1,0:T(8,128)(2,1)S(1)} %constant_dynamic-update-slice_fusion.11.refs_2_), channel_id=1, source_target_pairs={{0,1},{1,0},{2,3},{3,2},{4,5},{5,4},{6,7},{7,6},{8,9},{9,8},{10,11... | collective-permute-start | bytes 12582920 | tf_op jit(solution)/shard_map/ppermute | solution.py:60
  273.8 66.6 %collective-permute-start.17 = (bf16[1024,1024]{1,0:T(8,128)(2,1)S(1)}, bf16[1024,1024]{1,0:T(8,128)(2,1)S(1)}, u32[]{:S(2)}, u32[]{:S(2)}) collective-permute-start(bf16[1024,1024]{1,0:T(8,128)(2,1)S(1)} %copy-done.12), channel_id=1, source_target_pairs={{0,2},{1,3},{2,0},{3,1},{4,6},{5,7},{6,4},{7,5},{8,10},{9,11},{10,... | collective-permute-start | bytes 6291464 | tf_op jit(solution)/shard_map/ppermute | solution.py:60
  312.1 26.8 %collective-permute-start.36 = (bf16[512,512]{1,0:T(8,128)(2,1)S(1)}, bf16[512,512]{1,0:T(8,128)(2,1)S(1)}, u32[]{:S(2)}, u32[]{:S(2)}) collective-permute-start(bf16[512,512]{1,0:T(8,128)(2,1)S(1)} %pad_maximum_fusion.32), channel_id=1, source_target_pairs={{0,2},{1,3},{2,0},{3,1},{4,6},{5,7},{6,4},{7,5},{8,10},{9,11},{10,... | collective-permute-start | bytes 1572872 | tf_op jit(solution)/shard_map/ppermute | solution.py:60
  317.7 25.8 %collective-permute-start.20 = (bf16[256,512]{1,0:T(8,128)(2,1)S(1)}, bf16[256,512]{1,0:T(8,128)(2,1)S(1)}, u32[]{:S(2)}, u32[]{:S(2)}) collective-permute-start(bf16[256,512]{1,0:T(8,128)(2,1)S(1)} %pad_maximum_fusion.36), channel_id=1, source_target_pairs={{0,8},{1,9},{2,10},{3,11},{4,12},{5,13},{6,14},{7,15},{8,0},{9,1},... | collective-permute-start | bytes 786440 | tf_op jit(solution)/shard_map/ppermute | solution.py:60
  340.4 36.9 %collective-permute-start.37 = (bf16[1024,512]{1,0:T(8,128)(2,1)S(1)}, bf16[1024,512]{1,0:T(8,128)(2,1)S(1)}, u32[]{:S(2)}, u32[]{:S(2)}) collective-permute-start(bf16[1024,512]{1,0:T(8,128)(2,1)S(1)} %pad_maximum_fusion.14), channel_id=1, source_target_pairs={{0,4},{1,5},{2,6},{3,7},{4,0},{5,1},{6,2},{7,3},{8,12},{9,13},{10,... | collective-permute-start | bytes 3145736 | tf_op jit(solution)/shard_map/ppermute | solution.py:60
  343.5 90.5 %collective-permute-start.18 = (bf16[2048,1024]{1,0:T(8,128)(2,1)}, bf16[2048,1024]{1,0:T(8,128)(2,1)}, u32[]{:S(2)}, u32[]{:S(2)}) collective-permute-start(bf16[2048,1024]{1,0:T(8,128)(2,1)} %constant_dynamic-update-slice_fusion.16.refs_3_), channel_id=1, source_target_pairs={{0,1},{1,0},{2,3},{3,2},{4,5},{5,4},{6,7},{7,6},{8,9},{9,8},{10,11... | collective-permute-start | bytes 12582920 | tf_op jit(solution)/shard_map/ppermute | solution.py:60
  343.5 32.3 %collective-permute-start.21 = (bf16[512,512]{1,0:T(8,128)(2,1)S(1)}, bf16[512,512]{1,0:T(8,128)(2,1)S(1)}, u32[]{:S(2)}, u32[]{:S(2)}) collective-permute-start(bf16[512,512]{1,0:T(8,128)(2,1)S(1)} %pad_maximum_fusion.29), channel_id=1, source_target_pairs={{0,4},{1,5},{2,6},{3,7},{4,0},{5,1},{6,2},{7,3},{8,12},{9,13},{10,... | collective-permute-start | bytes 1572872 | tf_op jit(solution)/shard_map/ppermute | solution.py:60
  352.0 31.8 %collective-permute-start.32 = (bf16[1024,512]{1,0:T(8,128)(2,1)S(1)}, bf16[1024,512]{1,0:T(8,128)(2,1)S(1)}, u32[]{:S(2)}, u32[]{:S(2)}) collective-permute-start(bf16[1024,512]{1,0:T(8,128)(2,1)S(1)} %pad_maximum_fusion.13), channel_id=1, source_target_pairs={{0,2},{1,3},{2,0},{3,1},{4,6},{5,7},{6,4},{7,5},{8,10},{9,11},{10,... | collective-permute-start | bytes 3145736 | tf_op jit(solution)/shard_map/ppermute | solution.py:60
  375.8 23.2 %collective-permute-start.27 = (bf16[1024,512]{1,0:T(8,128)(2,1)S(1)}, bf16[1024,512]{1,0:T(8,128)(2,1)S(1)}, u32[]{:S(2)}, u32[]{:S(2)}) collective-permute-start(bf16[1024,512]{1,0:T(8,128)(2,1)S(1)} %pad_maximum_fusion.12), channel_id=1, source_target_pairs={{0,4},{1,5},{2,6},{3,7},{4,0},{5,1},{6,2},{7,3},{8,12},{9,13},{10,... | collective-permute-start | bytes 3145736 | tf_op jit(solution)/shard_map/ppermute | solution.py:60
  377.4 23.0 %collective-permute-start.22 = (bf16[1024,512]{1,0:T(8,128)(2,1)S(1)}, bf16[1024,512]{1,0:T(8,128)(2,1)S(1)}, u32[]{:S(2)}, u32[]{:S(2)}) collective-permute-start(bf16[1024,512]{1,0:T(8,128)(2,1)S(1)} %pad_maximum_fusion.11), channel_id=1, source_target_pairs={{0,2},{1,3},{2,0},{3,1},{4,6},{5,7},{6,4},{7,5},{8,10},{9,11},{10,... | collective-permute-start | bytes 3145736 | tf_op jit(solution)/shard_map/ppermute | solution.py:60
  383.8 82.9 %collective-permute-start.38 = (bf16[2048,512]{1,0:T(8,128)(2,1)}, bf16[2048,512]{1,0:T(8,128)(2,1)}, u32[]{:S(2)}, u32[]{:S(2)}) collective-permute-start(bf16[2048,512]{1,0:T(8,128)(2,1)} %constant_dynamic-update-slice_fusion.33.refs_7_), channel_id=1, source_target_pairs={{0,1},{1,0},{2,3},{3,2},{4,5},{5,4},{6,7},{7,6},{8,9},{9,8},{10,11... | collective-permute-start | bytes 6291464 | tf_op jit(solution)/shard_map/ppermute | solution.py:60
  399.0 67.7 %collective-permute-start.33 = (bf16[2048,512]{1,0:T(8,128)(2,1)}, bf16[2048,512]{1,0:T(8,128)(2,1)}, u32[]{:S(2)}, u32[]{:S(2)}) collective-permute-start(bf16[2048,512]{1,0:T(8,128)(2,1)} %constant_dynamic-update-slice_fusion.28.refs_6_), channel_id=1, source_target_pairs={{0,1},{1,0},{2,3},{3,2},{4,5},{5,4},{6,7},{7,6},{8,9},{9,8},{10,11... | collective-permute-start | bytes 6291464 | tf_op jit(solution)/shard_map/ppermute | solution.py:60
  400.4 66.4 %collective-permute-start.28 = (bf16[2048,512]{1,0:T(8,128)(2,1)}, bf16[2048,512]{1,0:T(8,128)(2,1)}, u32[]{:S(2)}, u32[]{:S(2)}) collective-permute-start(bf16[2048,512]{1,0:T(8,128)(2,1)} %constant_dynamic-update-slice_fusion.23.refs_5_), channel_id=1, source_target_pairs={{0,1},{1,0},{2,3},{3,2},{4,5},{5,4},{6,7},{7,6},{8,9},{9,8},{10,11... | collective-permute-start | bytes 6291464 | tf_op jit(solution)/shard_map/ppermute | solution.py:60
  401.7 65.1 %collective-permute-start.23 = (bf16[2048,512]{1,0:T(8,128)(2,1)}, bf16[2048,512]{1,0:T(8,128)(2,1)}, u32[]{:S(2)}, u32[]{:S(2)}) collective-permute-start(bf16[2048,512]{1,0:T(8,128)(2,1)} %constant_dynamic-update-slice_fusion.18.refs_4_), channel_id=1, source_target_pairs={{0,1},{1,0},{2,3},{3,2},{4,5},{5,4},{6,7},{7,6},{8,9},{9,8},{10,11... | collective-permute-start | bytes 6291464 | tf_op jit(solution)/shard_map/ppermute | solution.py:60
  501.5 30.3 %collective-permute-start.40 = (bf16[2048,512]{1,0:T(8,128)(2,1)}, bf16[2048,512]{1,0:T(8,128)(2,1)S(1)}, u32[]{:S(2)}, u32[]{:S(2)}) collective-permute-start(bf16[2048,512]{1,0:T(8,128)(2,1)} %get-tuple-element.124), channel_id=1, source_target_pairs={{0,1},{1,0},{2,3},{3,2},{4,5},{5,4},{6,7},{7,6},{8,9},{9,8},{10,11... | collective-permute-start | bytes 6291464 | tf_op jit(solution)/shard_map/ppermute | solution.py:60
  502.4 34.8 %collective-permute-start.39 = (bf16[2048,512]{1,0:T(8,128)(2,1)}, bf16[2048,512]{1,0:T(8,128)(2,1)}, u32[]{:S(2)}, u32[]{:S(2)}) collective-permute-start(bf16[2048,512]{1,0:T(8,128)(2,1)} %get-tuple-element.123), channel_id=1, source_target_pairs={{0,1},{1,0},{2,3},{3,2},{4,5},{5,4},{6,7},{7,6},{8,9},{9,8},{10,11... | collective-permute-start | bytes 6291464 | tf_op jit(solution)/shard_map/ppermute | solution.py:60
  503.2 49.0 %collective-permute-start.49 = (bf16[2048,512]{1,0:T(8,128)(2,1)}, bf16[2048,512]{1,0:T(8,128)(2,1)}, u32[]{:S(2)}, u32[]{:S(2)}) collective-permute-start(bf16[2048,512]{1,0:T(8,128)(2,1)} %get-tuple-element.125), channel_id=1, source_target_pairs={{0,1},{1,0},{2,3},{3,2},{4,5},{5,4},{6,7},{7,6},{8,9},{9,8},{10,11... | collective-permute-start | bytes 6291464 | tf_op jit(solution)/shard_map/ppermute | solution.py:60
  503.5 79.7 %collective-permute-start.54 = (bf16[2048,512]{1,0:T(8,128)(2,1)}, bf16[2048,512]{1,0:T(8,128)(2,1)}, u32[]{:S(2)}, u32[]{:S(2)}) collective-permute-start(bf16[2048,512]{1,0:T(8,128)(2,1)} %get-tuple-element.126), channel_id=1, source_target_pairs={{0,1},{1,0},{2,3},{3,2},{4,5},{5,4},{6,7},{7,6},{8,9},{9,8},{10,11... | collective-permute-start | bytes 6291464 | tf_op jit(solution)/shard_map/ppermute | solution.py:60
  540.3 53.4 %collective-permute-start.42 = (bf16[1024,512]{1,0:T(8,128)(2,1)}, bf16[1024,512]{1,0:T(8,128)(2,1)}, u32[]{:S(2)}, u32[]{:S(2)}) collective-permute-start(bf16[1024,512]{1,0:T(8,128)(2,1)} %get-tuple-element.133), channel_id=1, source_target_pairs={{0,4},{1,5},{2,6},{3,7},{4,0},{5,1},{6,2},{7,3},{8,12},{9,13},{10,... | collective-permute-start | bytes 3145736 | tf_op jit(solution)/shard_map/ppermute | solution.py:60
  551.6 44.9 %collective-permute-start.41 = (bf16[1024,512]{1,0:T(8,128)(2,1)}, bf16[1024,512]{1,0:T(8,128)(2,1)}, u32[]{:S(2)}, u32[]{:S(2)}) collective-permute-start(bf16[1024,512]{1,0:T(8,128)(2,1)} %get-tuple-element.132), channel_id=1, source_target_pairs={{0,2},{1,3},{2,0},{3,1},{4,6},{5,7},{6,4},{7,5},{8,10},{9,11},{10,... | collective-permute-start | bytes 3145736 | tf_op jit(solution)/shard_map/ppermute | solution.py:60
  581.7 31.1 %collective-permute-start.50 = (bf16[1024,512]{1,0:T(8,128)(2,1)}, bf16[1024,512]{1,0:T(8,128)(2,1)}, u32[]{:S(2)}, u32[]{:S(2)}) collective-permute-start(bf16[1024,512]{1,0:T(8,128)(2,1)} %get-tuple-element.304), channel_id=1, source_target_pairs={{0,2},{1,3},{2,0},{3,1},{4,6},{5,7},{6,4},{7,5},{8,10},{9,11},{10,... | collective-permute-start | bytes 3145736 | tf_op jit(solution)/shard_map/ppermute | solution.py:60
  587.1 28.8 %collective-permute-start.55 = (bf16[1024,512]{1,0:T(8,128)(2,1)}, bf16[1024,512]{1,0:T(8,128)(2,1)}, u32[]{:S(2)}, u32[]{:S(2)}) collective-permute-start(bf16[1024,512]{1,0:T(8,128)(2,1)} %get-tuple-element.306), channel_id=1, source_target_pairs={{0,4},{1,5},{2,6},{3,7},{4,0},{5,1},{6,2},{7,3},{8,12},{9,13},{10,... | collective-permute-start | bytes 3145736 | tf_op jit(solution)/shard_map/ppermute | solution.py:60
  587.8 141.2 %collective-permute-start.64 = (bf16[2048,512]{1,0:T(8,128)(2,1)}, bf16[2048,512]{1,0:T(8,128)(2,1)}, u32[]{:S(2)}, u32[]{:S(2)}) collective-permute-start(bf16[2048,512]{1,0:T(8,128)(2,1)} %get-tuple-element.164), channel_id=1, source_target_pairs={{0,1},{1,0},{2,3},{3,2},{4,5},{5,4},{6,7},{7,6},{8,9},{9,8},{10,11... | collective-permute-start | bytes 6291464 | tf_op jit(solution)/shard_map/ppermute | solution.py:60
  593.7 138.6 %collective-permute-start.63 = (bf16[2048,512]{1,0:T(8,128)(2,1)}, bf16[2048,512]{1,0:T(8,128)(2,1)}, u32[]{:S(2)}, u32[]{:S(2)}) collective-permute-start(bf16[2048,512]{1,0:T(8,128)(2,1)} %get-tuple-element.162), channel_id=1, source_target_pairs={{0,1},{1,0},{2,3},{3,2},{4,5},{5,4},{6,7},{7,6},{8,9},{9,8},{10,11... | collective-permute-start | bytes 6291464 | tf_op jit(solution)/shard_map/ppermute | solution.py:60
  596.5 148.0 %collective-permute-start.73 = (bf16[2048,512]{1,0:T(8,128)(2,1)}, bf16[2048,512]{1,0:T(8,128)(2,1)}, u32[]{:S(2)}, u32[]{:S(2)}) collective-permute-start(bf16[2048,512]{1,0:T(8,128)(2,1)} %get-tuple-element.174), channel_id=1, source_target_pairs={{0,1},{1,0},{2,3},{3,2},{4,5},{5,4},{6,7},{7,6},{8,9},{9,8},{10,11... | collective-permute-start | bytes 6291464 | tf_op jit(solution)/shard_map/ppermute | solution.py:60
  627.2 46.1 %collective-permute-start.51 = (bf16[512,512]{1,0:T(8,128)(2,1)}, bf16[512,512]{1,0:T(8,128)(2,1)}, u32[]{:S(2)}, u32[]{:S(2)}) collective-permute-start(bf16[512,512]{1,0:T(8,128)(2,1)} %get-tuple-element.328), channel_id=1, source_target_pairs={{0,4},{1,5},{2,6},{3,7},{4,0},{5,1},{6,2},{7,3},{8,12},{9,13},{10,... | collective-permute-start | bytes 1572872 | tf_op jit(solution)/shard_map/ppermute | solution.py:60
  630.3 46.2 %collective-permute-start.56 = (bf16[512,512]{1,0:T(8,128)(2,1)}, bf16[512,512]{1,0:T(8,128)(2,1)}, u32[]{:S(2)}, u32[]{:S(2)}) collective-permute-start(bf16[512,512]{1,0:T(8,128)(2,1)} %get-tuple-element.330), channel_id=1, source_target_pairs={{0,2},{1,3},{2,0},{3,1},{4,6},{5,7},{6,4},{7,5},{8,10},{9,11},{10,... | collective-permute-start | bytes 1572872 | tf_op jit(solution)/shard_map/ppermute | solution.py:60
  654.1 152.8 %all-to-all-start.1 = ((bf16[8,3,88,256]{3,2,1,0:T(8,128)(2,1)}), bf16[8,3,88,256]{3,2,1,0:T(8,128)(2,1)}, u32[]{:S(2)}, u32[]{:S(2)}) async-start(bf16[8,3,88,256]{3,2,1,0:T(8,128)(2,1)} %maximum_bitcast_fusion.1), calls=%async_computation.3 | async-start | bytes 2162688 | tf_op jit(solution)/shard_map/all_to_all | solution.py:668
  658.5 322.6 %reduce-scatter.5.cloned.1.call-start = ((), (), s32[]{:S(2)}) async-start(), calls=%async_computation.6 | async-start | bytes 2359296 | tf_op jit(solution)/shard_map/reduce_scatter | solution.py:688
  697.8 51.6 %collective-permute-start.78 = (bf16[2048,512]{1,0:T(8,128)(2,1)}, bf16[2048,512]{1,0:T(8,128)(2,1)}, u32[]{:S(2)}, u32[]{:S(2)}) collective-permute-start(bf16[2048,512]{1,0:T(8,128)(2,1)} %get-tuple-element.176), channel_id=1, source_target_pairs={{0,1},{1,0},{2,3},{3,2},{4,5},{5,4},{6,7},{7,6},{8,9},{9,8},{10,11... | collective-permute-start | bytes 6291464 | tf_op jit(solution)/shard_map/ppermute | solution.py:60
  735.5 26.3 %collective-permute-start.66 = (bf16[1024,512]{1,0:T(8,128)(2,1)}, bf16[1024,512]{1,0:T(8,128)(2,1)}, u32[]{:S(2)}, u32[]{:S(2)}) collective-permute-start(bf16[1024,512]{1,0:T(8,128)(2,1)} %get-tuple-element.166), channel_id=1, source_target_pairs={{0,4},{1,5},{2,6},{3,7},{4,0},{5,1},{6,2},{7,3},{8,12},{9,13},{10,... | collective-permute-start | bytes 3145736 | tf_op jit(solution)/shard_map/ppermute | solution.py:60
  744.5 33.6 %collective-permute-start.65 = (bf16[1024,512]{1,0:T(8,128)(2,1)}, bf16[1024,512]{1,0:T(8,128)(2,1)S(1)}, u32[]{:S(2)}, u32[]{:S(2)}) collective-permute-start(bf16[1024,512]{1,0:T(8,128)(2,1)} %get-tuple-element.165), channel_id=1, source_target_pairs={{0,2},{1,3},{2,0},{3,1},{4,6},{5,7},{6,4},{7,5},{8,10},{9,11},{10,... | collective-permute-start | bytes 3145736 | tf_op jit(solution)/shard_map/ppermute | solution.py:60
  747.5 53.2 %collective-permute-start.74 = (bf16[1024,512]{1,0:T(8,128)(2,1)S(1)}, bf16[1024,512]{1,0:T(8,128)(2,1)S(1)}, u32[]{:S(2)}, u32[]{:S(2)}) collective-permute-start(bf16[1024,512]{1,0:T(8,128)(2,1)S(1)} %get-tuple-element.296), channel_id=1, source_target_pairs={{0,2},{1,3},{2,0},{3,1},{4,6},{5,7},{6,4},{7,5},{8,10},{9,11},{10,... | collective-permute-start | bytes 3145736 | tf_op jit(solution)/shard_map/ppermute | solution.py:60
  751.6 52.0 %collective-permute-start.79 = (bf16[1024,512]{1,0:T(8,128)(2,1)S(1)}, bf16[1024,512]{1,0:T(8,128)(2,1)S(1)}, u32[]{:S(2)}, u32[]{:S(2)}) collective-permute-start(bf16[1024,512]{1,0:T(8,128)(2,1)S(1)} %get-tuple-element.298), channel_id=1, source_target_pairs={{0,4},{1,5},{2,6},{3,7},{4,0},{5,1},{6,2},{7,3},{8,12},{9,13},{10,... | collective-permute-start | bytes 3145736 | tf_op jit(solution)/shard_map/ppermute | solution.py:60
  758.1 51.9 %collective-permute-start.60 = (bf16[256,2048]{1,0:T(8,128)(2,1)}, bf16[256,2048]{1,0:T(8,128)(2,1)}, u32[]{:S(2)}, u32[]{:S(2)}) collective-permute-start(bf16[256,2048]{1,0:T(8,128)(2,1)} %pad_maximum_fusion.16), channel_id=1, source_target_pairs={{0,1},{1,0},{2,3},{3,2},{4,5},{5,4},{6,7},{7,6},{8,9},{9,8},{10,11... | collective-permute-start | bytes 3145736 | tf_op jit(solution)/shard_map/ppermute | solution.py:60
  779.5 77.2 %collective-permute-start.68 = (bf16[512,512]{1,0:T(8,128)(2,1)}, bf16[512,512]{1,0:T(8,128)(2,1)}, u32[]{:S(2)}, u32[]{:S(2)}) collective-permute-start(bf16[512,512]{1,0:T(8,128)(2,1)} %get-tuple-element.168), channel_id=1, source_target_pairs={{0,2},{1,3},{2,0},{3,1},{4,6},{5,7},{6,4},{7,5},{8,10},{9,11},{10,... | collective-permute-start | bytes 1572872 | tf_op jit(solution)/shard_map/ppermute | solution.py:60
  781.5 80.5 %collective-permute-start.67 = (bf16[512,512]{1,0:T(8,128)(2,1)}, bf16[512,512]{1,0:T(8,128)(2,1)}, u32[]{:S(2)}, u32[]{:S(2)}) collective-permute-start(bf16[512,512]{1,0:T(8,128)(2,1)} %get-tuple-element.167), channel_id=1, source_target_pairs={{0,4},{1,5},{2,6},{3,7},{4,0},{5,1},{6,2},{7,3},{8,12},{9,13},{10,... | collective-permute-start | bytes 1572872 | tf_op jit(solution)/shard_map/ppermute | solution.py:60
  801.9 64.2 %collective-permute-start.75 = (bf16[512,512]{1,0:T(8,128)(2,1)}, bf16[512,512]{1,0:T(8,128)(2,1)}, u32[]{:S(2)}, u32[]{:S(2)}) collective-permute-start(bf16[512,512]{1,0:T(8,128)(2,1)} %get-tuple-element.320), channel_id=1, source_target_pairs={{0,4},{1,5},{2,6},{3,7},{4,0},{5,1},{6,2},{7,3},{8,12},{9,13},{10,... | collective-permute-start | bytes 1572872 | tf_op jit(solution)/shard_map/ppermute | solution.py:60
  804.8 64.9 %collective-permute-start.80 = (bf16[512,512]{1,0:T(8,128)(2,1)}, bf16[512,512]{1,0:T(8,128)(2,1)}, u32[]{:S(2)}, u32[]{:S(2)}) collective-permute-start(bf16[512,512]{1,0:T(8,128)(2,1)} %get-tuple-element.322), channel_id=1, source_target_pairs={{0,2},{1,3},{2,0},{3,1},{4,6},{5,7},{6,4},{7,5},{8,10},{9,11},{10,... | collective-permute-start | bytes 1572872 | tf_op jit(solution)/shard_map/ppermute | solution.py:60
  814.3 190.1 %reduce-scatter.3.cloned.1.call-start = ((), (), s32[]{:S(2)}) async-start(), calls=%async_computation.5 | async-start | bytes 4718592 | tf_op jit(solution)/shard_map/reduce_scatter | solution.py:744
  864.1 41.6 %collective-permute-start.70 = (bf16[256,512]{1,0:T(8,128)(2,1)}, bf16[256,512]{1,0:T(8,128)(2,1)}, u32[]{:S(2)}, u32[]{:S(2)}) collective-permute-start(bf16[256,512]{1,0:T(8,128)(2,1)} %get-tuple-element.170), channel_id=1, source_target_pairs={{0,8},{1,9},{2,10},{3,11},{4,12},{5,13},{6,14},{7,15},{8,0},{9,1},... | collective-permute-start | bytes 786440 | tf_op jit(solution)/shard_map/ppermute | solution.py:60
  865.8 41.5 %collective-permute-start.69 = (bf16[256,512]{1,0:T(8,128)(2,1)}, bf16[256,512]{1,0:T(8,128)(2,1)}, u32[]{:S(2)}, u32[]{:S(2)}) collective-permute-start(bf16[256,512]{1,0:T(8,128)(2,1)} %get-tuple-element.169), channel_id=1, source_target_pairs={{0,8},{1,9},{2,10},{3,11},{4,12},{5,13},{6,14},{7,15},{8,0},{9,1},... | collective-permute-start | bytes 786440 | tf_op jit(solution)/shard_map/ppermute | solution.py:60
  868.1 43.1 %collective-permute-start.76 = (bf16[256,512]{1,0:T(8,128)(2,1)}, bf16[256,512]{1,0:T(8,128)(2,1)}, u32[]{:S(2)}, u32[]{:S(2)}) collective-permute-start(bf16[256,512]{1,0:T(8,128)(2,1)} %get-tuple-element.351), channel_id=1, source_target_pairs={{0,8},{1,9},{2,10},{3,11},{4,12},{5,13},{6,14},{7,15},{8,0},{9,1},... | collective-permute-start | bytes 786440 | tf_op jit(solution)/shard_map/ppermute | solution.py:60
  871.7 40.6 %collective-permute-start.81 = (bf16[256,512]{1,0:T(8,128)(2,1)}, bf16[256,512]{1,0:T(8,128)(2,1)}, u32[]{:S(2)}, u32[]{:S(2)}) collective-permute-start(bf16[256,512]{1,0:T(8,128)(2,1)} %get-tuple-element.353), channel_id=1, source_target_pairs={{0,8},{1,9},{2,10},{3,11},{4,12},{5,13},{6,14},{7,15},{8,0},{9,1},... | collective-permute-start | bytes 786440 | tf_op jit(solution)/shard_map/ppermute | solution.py:60
  905.6 37.8 %collective-permute-start.83 = (bf16[1024,640]{1,0:T(8,128)(2,1)S(1)}, bf16[1024,640]{1,0:T(8,128)(2,1)S(1)}, u32[]{:S(2)}, u32[]{:S(2)}) collective-permute-start(bf16[1024,640]{1,0:T(8,128)(2,1)S(1)} %bitcast.221), channel_id=1, source_target_pairs={{0,1},{1,0},{2,3},{3,2},{4,5},{5,4},{6,7},{7,6},{8,9},{9,8},{10,11... | collective-permute-start | bytes 3932168 | tf_op jit(solution)/shard_map/ppermute | solution.py:60
  908.2 25.6 %collective-permute-start.71 = (bf16[128,512]{1,0:T(8,128)(2,1)S(1)}, bf16[128,512]{1,0:T(8,128)(2,1)S(1)}, u32[]{:S(2)}, u32[]{:S(2)}) collective-permute-start(bf16[128,512]{1,0:T(8,128)(2,1)S(1)} %add_convert_fusion.54), channel_id=1, source_target_pairs={{0,16},{1,17},{2,18},{3,19},{4,20},{5,21},{6,22},{7,23},{8,24},{9,... | collective-permute-start | bytes 393224 | tf_op jit(solution)/shard_map/ppermute | solution.py:60
  908.3 34.2 %collective-permute-start.72 = (bf16[128,512]{1,0:T(8,128)(2,1)S(1)}, bf16[128,512]{1,0:T(8,128)(2,1)S(1)}, u32[]{:S(2)}, u32[]{:S(2)}) collective-permute-start(bf16[128,512]{1,0:T(8,128)(2,1)S(1)} %add_convert_fusion.53), channel_id=1, source_target_pairs={{0,16},{1,17},{2,18},{3,19},{4,20},{5,21},{6,22},{7,23},{8,24},{9,... | collective-permute-start | bytes 393224 | tf_op jit(solution)/shard_map/ppermute | solution.py:60
  912.1 38.8 %collective-permute-start.77 = (bf16[128,512]{1,0:T(8,128)(2,1)S(1)}, bf16[128,512]{1,0:T(8,128)(2,1)S(1)}, u32[]{:S(2)}, u32[]{:S(2)}) collective-permute-start(bf16[128,512]{1,0:T(8,128)(2,1)S(1)} %add_convert_fusion.50), channel_id=1, source_target_pairs={{0,16},{1,17},{2,18},{3,19},{4,20},{5,21},{6,22},{7,23},{8,24},{9,... | collective-permute-start | bytes 393224 | tf_op jit(solution)/shard_map/ppermute | solution.py:60
  913.2 44.0 %collective-permute-start.82 = (bf16[128,512]{1,0:T(8,128)(2,1)S(1)}, bf16[128,512]{1,0:T(8,128)(2,1)S(1)}, u32[]{:S(2)}, u32[]{:S(2)}) collective-permute-start(bf16[128,512]{1,0:T(8,128)(2,1)S(1)} %add_convert_fusion.48), channel_id=1, source_target_pairs={{0,16},{1,17},{2,18},{3,19},{4,20},{5,21},{6,22},{7,23},{8,24},{9,... | collective-permute-start | bytes 393224 | tf_op jit(solution)/shard_map/ppermute | solution.py:60
  (160 other events, 1936.0 us)
Sparse Core Ops, SparseCore 0:
  16.1 192.5 all-gather.1
  814.4 71.8 reduce-scatter.4
  889.9 114.4 reduce-scatter.2

commit v4 on v2

--- a/solution.py
+++ b/solution.py
@@ -76,9 +76,13 @@
         (k[half:].astype(F32) + r[half:].astype(F32)).astype(BF)
         for k, r in zip(keeps, receiveds)
     ]
-    upper, follow = tie(upper, follow)
+    first, follow = tie(upper[:2], follow)
+    upper = [*first, *upper[2:]]
     sent = [swap_with(value, mask, count) for value, mask in zip(upper, masks)]
-    lower = [k[:half].astype(F32) + r[:half].astype(F32) for k, r in zip(keeps, receiveds)]
+    lower = [
+        (k[:half].astype(F32) + r[:half].astype(F32)).astype(BF)
+        for k, r in zip(keeps, receiveds)
+    ]
     return lower, sent, follow
 
 
@@ -508,14 +512,9 @@
     )
 
     near = [
-        cube_gather(normed_second[:, s * part : (s + 1) * part], order[:-1], count)
+        cube_gather(normed_second[:, s * part : (s + 1) * part], order, count)
         for s, order in enumerate(stream_orders)
     ]
-    last = [swap_with(block, order[-1], count) for block, order in zip(near, stream_orders)]
-    last, (grad_rows, grad_hidden, grad_hidden_common) = tie(
-        last, (grad_rows, grad_hidden, grad_hidden_common)
-    )
-    near = [jnp.concatenate(pair, axis=0) for pair in zip(near, last)]
     far = [swap_with(block, CORE, count) for block in near]
     hidden_weights = (gate_up, common_gu_t)
     kept = None
@@ -546,8 +545,15 @@
                     grads = jnp.swapaxes(grads.reshape(shape), 0, 1).reshape(half_rows, 2 * unit_pad)
                 total = total + dot(grads, tokens, ((0,), (0,)))
             parts.append(total)
-        grad_common_gu = jnp.concatenate(parts, axis=1)
-        return grad_common_gu
+        return jnp.concatenate(parts, axis=1)
+
+    def common_down_gradient(hidden, cotangents):
+        canon_ids = jnp.zeros((count,), jnp.int32)
+        offset = me ^ canon
+        for bit, mask in enumerate(order_a + (CORE,)):
+            canon_ids = canon_ids + (1 << bit) * ((offset // mask) & 1)
+        in_order = jnp.take(hidden.reshape(count, shard_rows, unit_pad), canon_ids, axis=0)
+        return dot(in_order.reshape(count * shard_rows, unit_pad), cotangents, ((0,), (0,)))
 
     if count > 32:
         grad_common_gu = common_gradients(grad_common)
@@ -591,6 +597,7 @@
             (near_results, hidden_late, grad_common_late),
         )
         grad_common_gu = common_gradients(grad_common_late)
+        grad_common_down = common_down_gradient(hidden_common, cotangent_all)
         result_lower, result_sent, _ = halve_stage(
             near_results, far_results_received, [turn[0] for turn in turns], count
         )
@@ -599,23 +606,16 @@
     for k in range(3, len(order_a)):
         lower, sent, _ = halve_stage(lower, sent, [turn[k] for turn in turns], count)
     grad_normed_second = jnp.concatenate(
-        [a + b.astype(F32) for a, b in zip(lower, sent)], axis=1
+        [a.astype(F32) + b.astype(F32) for a, b in zip(lower, sent)], axis=1
     )
     grad_expert_down = jnp.stack(
         [dot(hidden_late[j][:, :width], grad_rows[j], ((0,), (0,))) for j in range(expert_local)]
     )
 
-    canon_ids = jnp.zeros((count,), jnp.int32)
-    offset = me ^ canon
-    for bit, mask in enumerate(order_a + (CORE,)):
-        canon_ids = canon_ids + (1 << bit) * ((offset // mask) & 1)
-    hidden_global = jnp.take(
-        hidden_common.reshape(count, shard_rows, unit_pad), canon_ids, axis=0
-    ).reshape(count * shard_rows, unit_pad)
     if count > 32:
-        again, _ = tie(out_cotangent, grad_normed_second)
+        again, grad_normed_second = tie(out_cotangent, grad_normed_second)
         cotangent_all = lax.all_gather(again, BOTH, axis=0, tiled=True)
-    grad_common_down = dot(hidden_global, cotangent_all, ((0,), (0,)))
+        grad_common_down = common_down_gradient(hidden_common, cotangent_all)
     common_grads = jnp.stack(
         [grad_common_gu[:units], grad_common_gu[unit_pad : unit_pad + units], grad_common_down[:units]]
     ).astype(BF)
@@ -737,7 +737,7 @@
             result_lower, result_sent, [turn[k] for turn in turns], count
         )
     result = jnp.concatenate(
-        [a + b.astype(F32) for a, b in zip(result_lower, result_sent)], axis=1
+        [a.astype(F32) + b.astype(F32) for a, b in zip(result_lower, result_sent)], axis=1
     )
     small_terms = jnp.take(small_terms.reshape(count, D // count, latent_pad), group_ids, axis=0)
     small_grads = scatter_rows(small_terms.reshape(D, latent_pad), (CORE,) + order_a[::-1], count)

time: 1000 us -> 1010 us (1.010)
  waiting for transfers between devices: 410 us -> 452 us
  other arithmetic: 141 us -> 128 us
    convert_element_type x0 -> x24, other arithmetic: none -> 54.5 us  [halve_stage(): (k[:half].astype(F32) + r[:half].astype(F32)).astype(BF)]
    add x24 -> x8, other arithmetic: 48.9 us -> 4.01 us  [local(): a.astype(F32) + b.astype(F32)]
    ppermute x78, waiting for transfers between devices: 305 us -> 345 us  [swap_with(): return lax.ppermute(values, BOTH, [(i, i ^ mask) for i in range(count)])]
    convert_element_type x16 -> x8, other arithmetic: 18.8 us -> 3.9 us  [halve_stage(): (k[half:].astype(F32) + r[half:].astype(F32)).astype(BF)]
    unnamed x295 -> x274, local copies, waits for them, and re-layouts: 32.1 us -> 27.5 us
  transfers between devices with their start and end apart: 84 -> 84, of which waited for: 43 -> 42; matrix products, arithmetic and copies ran while one was open for 33% -> 31% of each run, Pallas kernels for 9% -> 9%
where the time goes in v4:
time: 1010 us; the launch traced here: 1000 us
  waiting for transfers between devices  452 us (45%)
  other arithmetic  128 us (13%)
  Pallas kernels  121 us (12%)
  local copies, waits for them, and re-layouts  117 us (12%)
  matrix products  95.1 us (9%)
  starting transfers between devices  74.6 us (7%)
  between operations  16.4 us (2%)
    ppermute x78, waiting for transfers between devices, swap_with(): return lax.ppermute(values, BOTH, [(i, i ^ mask) for i in range(count)])  345 us
    dot_general x27, matrix products, dot(): lax.dot_general(left, right, (dims, ((), ())), preferred_element_type=F32)  88.2 us
    all_gather x1, waiting for transfers between devices, local(): packed_full = lax.all_gather(packed, 'dp', axis=0, tiled=True)  83.1 us
    ppermute x78, starting transfers between devices, swap_with(): return lax.ppermute(values, BOTH, [(i, i ^ mask) for i in range(count)])  65.9 us
    pallas_call x4, Pallas kernels, token_terms(): pl.pallas_call(body, grid=(blocks,), in_specs=[pl.BlockSpec((GB, 1, slots...  59 us
    convert_element_type x24, other arithmetic, halve_stage(): (k[:half].astype(F32) + r[:half].astype(F32)).astype(BF)  54.5 us
    pallas_call x2, Pallas kernels, expert_hidden(): pl.pallas_call(body, grid=(blocks,), in_specs=in_specs, out_specs=[pl.Blo...  36.6 us
    unnamed x274, local copies, waits for them, and re-layouts  27.5 us
  transfers between devices with their start and end apart: 84, of which 42 were waited for; matrix products, arithmetic and copies ran while one was open for 31% of the time, Pallas kernels for 9%

profile of v4, /device:TPU:0, one launch (start us, length us, event | category | flops | bytes accessed | tf_op | source)
XLA Modules:
  0.0 1004.4 jit_solution(6417378971057671674)
XLA Ops:
  18.5 4.1 collective-permute-start
  25.9 4.8 all-to-all-start
  32.9 5.5 pad_bitcast_fusion.1
  38.4 7.8 fusion.157
  48.5 18.5 %collective-permute-done.1 = f32[2,2,1024]{2,1,0:T(2,128)S(1)} collective-permute-done((f32[2,2,1024]{2,1,0:T(2,128)S(1)}, f32[2,2,1024]{2,1,0:T(2,128)S(1)}, u32[]{:S(2)}, u32[]{:S(2)}) %collective-permute-start.1) | collective-permute-done | bytes 16416 | tf_op jit(solution)/shard_map/ppermute | solution.py:60
  79.1 7.0 all-to-all-done
  89.6 83.1 %all-gather.3.cloned.1.call-done = bf16[2048,2176]{1,0:T(8,128)(2,1)} async-done(((bf16[256,2176]{1,0:T(8,128)(2,1)}), bf16[2048,2176]{1,0:T(8,128)(2,1)}) %all-gather.3.cloned.1.call-update) | async-done | bytes 8912912 | tf_op jit(solution)/shard_map/all_gather | solution.py:385
  211.0 20.2 %collective-permute-done.8 = bf16[128,2048]{1,0:T(8,128)(2,1)S(1)} collective-permute-done((bf16[128,2048]{1,0:T(8,128)(2,1)S(1)}, bf16[128,2048]{1,0:T(8,128)(2,1)S(1)}, u32[]{:S(2)}, u32[]{:S(2)}) %collective-permute-start.8) | collective-permute-done | bytes 524320 | tf_op jit(solution)/shard_map/ppermute | solution.py:60
  239.0 14.6 %collective-permute-done.24 = bf16[128,512]{1,0:T(8,128)(2,1)S(1)} collective-permute-done((bf16[128,512]{1,0:T(8,128)(2,1)S(1)}, bf16[128,512]{1,0:T(8,128)(2,1)S(1)}, u32[]{:S(2)}, u32[]{:S(2)}) %collective-permute-start.24) | collective-permute-done | bytes 131104 | tf_op jit(solution)/shard_map/ppermute | solution.py:60
  259.5 6.1 collective-permute-done.9
  268.4 16.0 %collective-permute-done.25 = bf16[256,512]{1,0:T(8,128)(2,1)S(1)} collective-permute-done((bf16[256,512]{1,0:T(8,128)(2,1)S(1)}, bf16[256,512]{1,0:T(8,128)(2,1)S(1)}, u32[]{:S(2)}, u32[]{:S(2)}) %collective-permute-start.25) | collective-permute-done | bytes 262176 | tf_op jit(solution)/shard_map/ppermute | solution.py:60
  284.4 16.7 %collective-permute-done.20 = bf16[256,512]{1,0:T(8,128)(2,1)S(1)} collective-permute-done((bf16[256,512]{1,0:T(8,128)(2,1)S(1)}, bf16[256,512]{1,0:T(8,128)(2,1)S(1)}, u32[]{:S(2)}, u32[]{:S(2)}) %collective-permute-start.20) | collective-permute-done | bytes 262176 | tf_op jit(solution)/shard_map/ppermute | solution.py:60
  303.6 14.4 %collective-permute-done.15 = bf16[256,512]{1,0:T(8,128)(2,1)S(1)} collective-permute-done((bf16[256,512]{1,0:T(8,128)(2,1)S(1)}, bf16[256,512]{1,0:T(8,128)(2,1)S(1)}, u32[]{:S(2)}, u32[]{:S(2)}) %collective-permute-start.15) | collective-permute-done | bytes 262176 | tf_op jit(solution)/shard_map/ppermute | solution.py:60
  318.2 11.0 %collective-permute-done.10 = bf16[256,512]{1,0:T(8,128)(2,1)S(1)} collective-permute-done((bf16[256,512]{1,0:T(8,128)(2,1)S(1)}, bf16[256,512]{1,0:T(8,128)(2,1)S(1)}, u32[]{:S(2)}, u32[]{:S(2)}) %collective-permute-start.10) | collective-permute-done | bytes 262176 | tf_op jit(solution)/shard_map/ppermute | solution.py:60
  335.6 8.8 collective-permute-done.11
  349.4 17.5 %collective-permute-done.27 = bf16[1024,512]{1,0:T(8,128)(2,1)S(1)} collective-permute-done((bf16[1024,512]{1,0:T(8,128)(2,1)S(1)}, bf16[1024,512]{1,0:T(8,128)(2,1)S(1)}, u32[]{:S(2)}, u32[]{:S(2)}) %collective-permute-start.27) | collective-permute-done | bytes 1048608 | tf_op jit(solution)/shard_map/ppermute | solution.py:60
  369.5 19.1 %collective-permute-done.17 = bf16[1024,512]{1,0:T(8,128)(2,1)S(1)} collective-permute-done((bf16[1024,512]{1,0:T(8,128)(2,1)S(1)}, bf16[1024,512]{1,0:T(8,128)(2,1)S(1)}, u32[]{:S(2)}, u32[]{:S(2)}) %collective-permute-start.17) | collective-permute-done | bytes 1048608 | tf_op jit(solution)/shard_map/ppermute | solution.py:60
  393.1 4.7 copy.286.down_ref
  398.8 8.8 copy.290.refs_8_
  410.5 25.8 %cotangent_rows.1 = (bf16[2,2048,2048]{2,1,0:T(8,128)(2,1)}, f32[2,2048,384]{2,1,0:T(8,128)}, f32[4096,128]{1,0:T(8,128)}) custom-call(s32[32]{0:T(128)} %fusion.123.ids_ref, s32[32,1,128]{2,1,0:T(1,128)} %get-tuple-element.137.slot_ref.refs_0_, f32[2,2048,128]{2,1,0:T(8,128)} %broadcast_in_dim.150.weight_ref.refs_1_, ...), custom_call_target="tpu_custom_call" | custom-call | tf_op jit(solution)/shard_map/cotangent_rows/pallas_call | solution.py:133
  436.3 18.3 %expert_hidden.2 = (bf16[2,2048,2048]{2,1,0:T(8,128)(2,1)}, bf16[2,2048,384]{2,1,0:T(8,128)(2,1)}, bf16[2,2048,768]{2,1,0:T(8,128)(2,1)}, bf16[4096,128]{1,0:T(8,128)(2,1)}, bf16[4096,256]{1,0:T(8,128)(2,1)}) custom-call(s32[32,1,128]{2,1,0:T(1,128)} %get-tuple-element.137.slot_ref.refs_0_, f32[2,2048,128]{2,1,0:T(8,128)} %broadcast_in_dim.150.weight_ref.refs_1_, ...), custom_call_target="tpu_custom_call" | custom-call | tf_op jit(solution)/shard_map/expert_hidden/pallas_call | solution.py:231
  454.6 18.3 %expert_hidden.3 = (bf16[2,2048,2048]{2,1,0:T(8,128)(2,1)}, bf16[2,2048,384]{2,1,0:T(8,128)(2,1)}, bf16[2,2048,768]{2,1,0:T(8,128)(2,1)}, bf16[4096,128]{1,0:T(8,128)(2,1)}, bf16[4096,256]{1,0:T(8,128)(2,1)}) custom-call(s32[32,1,128]{2,1,0:T(1,128)} %get-tuple-element.137.slot_ref.ref, ...), custom_call_target="tpu_custom_call", output_to_operand_aliasing={{0}: (10, {}), {1}: (11, {}), {2}: (12, {}), {3}: (13, {}),... | custom-call | tf_op jit(solution)/shard_map/expert_hidden/pallas_call | solution.py:231
  472.9 16.4 %token_terms.4 = (bf16[2048,512]{1,0:T(8,128)(2,1)}, bf16[2048,512]{1,0:T(8,128)(2,1)}, bf16[2048,512]{1,0:T(8,128)(2,1)}, bf16[2048,512]{1,0:T(8,128)(2,1)}) custom-call(s32[32,1,128]{2,1,0:T(1,128)} %get-tuple-element.137.slot_ref.refs_0_, bf16[2,2048,768]{2,1,0:T(8,128)(2,1)} %get-tuple-element.169.value_ref, ...), custom_call_target="tpu_custom_call" | custom-call | tf_op jit(solution)/shard_map/token_terms/pallas_call | solution.py:278
  490.9 16.3 %token_terms.5 = (bf16[2048,512]{1,0:T(8,128)(2,1)}, bf16[2048,512]{1,0:T(8,128)(2,1)}, bf16[2048,512]{1,0:T(8,128)(2,1)}, bf16[2048,512]{1,0:T(8,128)(2,1)}) custom-call(s32[32,1,128]{2,1,0:T(1,128)} %get-tuple-element.137.slot_ref.refs_0_, bf16[2,2048,768]{2,1,0:T(8,128)(2,1)} %get-tuple-element.169.value_ref, ...), custom_call_target="tpu_custom_call" | custom-call | tf_op jit(solution)/shard_map/token_terms/pallas_call | solution.py:278
  510.6 8.3 fusion.167
  520.6 3.9 add_convert_fusion.12
  529.4 5.0 fusion.26
  534.4 5.0 fusion.29
  542.6 13.2 %token_terms.6 = (bf16[2048,512]{1,0:T(8,128)(2,1)}, bf16[2048,512]{1,0:T(8,128)(2,1)}, bf16[2048,512]{1,0:T(8,128)(2,1)}, bf16[2048,512]{1,0:T(8,128)(2,1)}) custom-call(s32[32,1,128]{2,1,0:T(1,128)} %get-tuple-element.137.slot_ref.refs_0_, bf16[2,2048,384]{2,1,0:T(8,128)(2,1)} %get-tuple-element.170.value_ref, ...), custom_call_target="tpu_custom_call" | custom-call | tf_op jit(solution)/shard_map/token_terms/pallas_call | solution.py:278
  555.8 13.1 %token_terms.7 = (bf16[2048,512]{1,0:T(8,128)(2,1)}, bf16[2048,512]{1,0:T(8,128)(2,1)}, bf16[2048,512]{1,0:T(8,128)(2,1)}, bf16[2048,512]{1,0:T(8,128)(2,1)}) custom-call(s32[32,1,128]{2,1,0:T(1,128)} %get-tuple-element.137.slot_ref.refs_0_, bf16[2,2048,384]{2,1,0:T(8,128)(2,1)} %get-tuple-element.170.value_ref, ...), custom_call_target="tpu_custom_call" | custom-call | tf_op jit(solution)/shard_map/token_terms/pallas_call | solution.py:278
  570.9 3.9 add_convert_fusion.9
  575.1 6.1 pad_maximum_fusion
  586.8 6.0 fusion.32
  606.7 7.8 collective-permute-done.34
  640.7 3.6 all-to-all-start.1
  646.6 6.1 fusion.38
  652.7 5.7 fusion.41
  665.9 8.7 collective-permute-done.36
  674.6 5.6 collective-permute-done.35
  680.2 5.6 collective-permute-done.42
  690.9 7.3 collective-permute-done.37
  698.2 9.5 collective-permute-done.38
  707.7 7.9 collective-permute-done.43
  715.7 7.0 collective-permute-done.48
  723.1 3.7 add_convert_fusion.4
  742.8 3.8 collective-permute-done.49
  748.7 7.9 collective-permute-done.56
  759.1 9.9 collective-permute-done.55
  772.4 19.1 %collective-permute-done.64 = bf16[1024,512]{1,0:T(8,128)(2,1)S(1)} collective-permute-done((bf16[1024,512]{1,0:T(8,128)(2,1)S(1)}, bf16[1024,512]{1,0:T(8,128)(2,1)S(1)}, u32[]{:S(2)}, u32[]{:S(2)}) %collective-permute-start.64) | collective-permute-done | bytes 1048608 | tf_op jit(solution)/shard_map/ppermute | solution.py:60
  798.8 4.0 convolution_convert_fusion.2
  824.6 5.4 concatenate.189
  839.4 4.4 pad_maximum_fusion.3
  861.2 6.0 collective-permute-done.52
  871.9 4.4 copy.301
  876.4 3.8 fusion.76
  881.7 6.7 concatenate.196
  888.5 4.3 gather_fusion.1
  905.6 17.9 %collective-permute-done.61 = bf16[128,512]{1,0:T(8,128)(2,1)S(1)} collective-permute-done((bf16[128,512]{1,0:T(8,128)(2,1)S(1)}, bf16[128,512]{1,0:T(8,128)(2,1)S(1)}, u32[]{:S(2)}, u32[]{:S(2)}) %collective-permute-start.61) | collective-permute-done | bytes 131104 | tf_op jit(solution)/shard_map/ppermute | solution.py:60
  924.5 7.5 collective-permute-done.62
  935.1 5.2 collective-permute-done.67
  941.3 4.8 collective-permute-done.72
  952.0 12.8 %collective-permute-done.75 = bf16[256,640]{1,0:T(8,128)(2,1)S(1)} collective-permute-done((bf16[256,640]{1,0:T(8,128)(2,1)S(1)}, bf16[256,640]{1,0:T(8,128)(2,1)S(1)}, u32[]{:S(2)}, u32[]{:S(2)}) %collective-permute-start.75) | collective-permute-done | bytes 327712 | tf_op jit(solution)/shard_map/ppermute | solution.py:60
  965.8 5.1 collective-permute-done.76
  977.9 16.5 %reduce-scatter.3.cloned.1.call-done = bf16[256,1024]{0,1:T(8,128)(2,1)} async-done(((bf16[2048,1024]{0,1:T(8,128)(2,1)}), bf16[256,1024]{0,1:T(8,128)(2,1)}) %reduce-scatter.3.cloned.1.call-update) | async-done | bytes 524304 | tf_op jit(solution)/shard_map/reduce_scatter | solution.py:701
  (651 shorter events, 312.0 us)
Async XLA Ops:
  7.2 165.5 %all-gather.3.cloned.1.call-start = ((), (), s32[]{:S(2)}) async-start(), calls=%async_computation.4 | async-start | bytes 10027008 | tf_op jit(solution)/shard_map/all_gather | solution.py:385
  15.9 394.6 %all-gather.5.cloned.1.call-start = ((), (), s32[]{:S(2)}) async-start(), calls=%async_computation.5 | async-start | bytes 17301504 | tf_op jit(solution)/shard_map/all_gather | solution.py:509
  18.5 27.8 %collective-permute-start = (f32[1,2,1024]{2,1,0:T(2,128)S(1)}, f32[1,2,1024]{2,1,0:T(2,128)S(1)}, u32[]{:S(2)}, u32[]{:S(2)}) collective-permute-start(f32[1,2,1024]{2,1,0:T(2,128)S(1)} %maximum_bitcast_fusion.2), channel_id=1, source_target_pairs={{0,16},{1,17},{2,18},{3,19},{4,20},{5,21},{6,22},{7,23},{8,24},{9,... | collective-permute-start | bytes 24584 | tf_op jit(solution)/shard_map/ppermute | solution.py:60
  25.9 60.2 %all-to-all-start = ((bf16[8,3,88,256]{3,2,1,0:T(8,128)(2,1)}), bf16[8,3,88,256]{3,2,1,0:T(8,128)(2,1)}, u32[]{:S(2)}, u32[]{:S(2)}) async-start(bf16[8,3,88,256]{3,2,1,0:T(8,128)(2,1)} %copy.271), calls=%async_computation | async-start | bytes 2162688 | tf_op jit(solution)/shard_map/all_to_all | solution.py:398
  30.7 17.7 %collective-permute-start.5 = (bf16[128,2048]{1,0:T(8,128)(2,1)S(1)}, bf16[128,2048]{1,0:T(8,128)(2,1)S(1)}, u32[]{:S(2)}, u32[]{:S(2)}) collective-permute-start(bf16[128,2048]{1,0:T(8,128)(2,1)S(1)} %copy-done.7), channel_id=1, source_target_pairs={{0,2},{1,3},{2,0},{3,1},{4,6},{5,7},{6,4},{7,5},{8,10},{9,11},{10,... | collective-permute-start | bytes 1572872 | tf_op jit(solution)/shard_map/ppermute | solution.py:60
  46.3 20.7 %collective-permute-start.1 = (f32[2,2,1024]{2,1,0:T(2,128)S(1)}, f32[2,2,1024]{2,1,0:T(2,128)S(1)}, u32[]{:S(2)}, u32[]{:S(2)}) collective-permute-start(f32[2,2,1024]{2,1,0:T(2,128)S(1)} %pad_maximum_fusion.39), channel_id=1, source_target_pairs={{0,8},{1,9},{2,10},{3,11},{4,12},{5,13},{6,14},{7,15},{8,0},{9,1},... | collective-permute-start | bytes 49160 | tf_op jit(solution)/shard_map/ppermute | solution.py:60
  48.4 29.2 %collective-permute-start.6 = (bf16[256,2048]{1,0:T(8,128)(2,1)S(1)}, bf16[256,2048]{1,0:T(8,128)(2,1)}, u32[]{:S(2)}, u32[]{:S(2)}) collective-permute-start(bf16[256,2048]{1,0:T(8,128)(2,1)S(1)} %pad_maximum_fusion.6), channel_id=1, source_target_pairs={{0,1},{1,0},{2,3},{3,2},{4,5},{5,4},{6,7},{7,6},{8,9},{9,8},{10,11... | collective-permute-start | bytes 3145736 | tf_op jit(solution)/shard_map/ppermute | solution.py:60
  209.3 21.9 %collective-permute-start.8 = (bf16[128,2048]{1,0:T(8,128)(2,1)S(1)}, bf16[128,2048]{1,0:T(8,128)(2,1)S(1)}, u32[]{:S(2)}, u32[]{:S(2)}) collective-permute-start(bf16[128,2048]{1,0:T(8,128)(2,1)S(1)} %slice.1335), channel_id=1, source_target_pairs={{0,2},{1,3},{2,0},{3,1},{4,6},{5,7},{6,4},{7,5},{8,10},{9,11},{10,... | collective-permute-start | bytes 1572872 | tf_op jit(solution)/shard_map/ppermute | solution.py:60
  233.2 20.5 %collective-permute-start.24 = (bf16[128,512]{1,0:T(8,128)(2,1)S(1)}, bf16[128,512]{1,0:T(8,128)(2,1)S(1)}, u32[]{:S(2)}, u32[]{:S(2)}) collective-permute-start(bf16[128,512]{1,0:T(8,128)(2,1)S(1)} %get-tuple-element.355), channel_id=1, source_target_pairs={{0,16},{1,17},{2,18},{3,19},{4,20},{5,21},{6,22},{7,23},{8,24},{9,... | collective-permute-start | bytes 393224 | tf_op jit(solution)/shard_map/ppermute | solution.py:60
  235.6 20.9 %collective-permute-start.19 = (bf16[128,512]{1,0:T(8,128)(2,1)S(1)}, bf16[128,512]{1,0:T(8,128)(2,1)S(1)}, u32[]{:S(2)}, u32[]{:S(2)}) collective-permute-start(bf16[128,512]{1,0:T(8,128)(2,1)S(1)} %get-tuple-element.360), channel_id=1, source_target_pairs={{0,16},{1,17},{2,18},{3,19},{4,20},{5,21},{6,22},{7,23},{8,24},{9,... | collective-permute-start | bytes 393224 | tf_op jit(solution)/shard_map/ppermute | solution.py:60
  236.1 23.3 %collective-permute-start.14 = (bf16[128,512]{1,0:T(8,128)(2,1)S(1)}, bf16[128,512]{1,0:T(8,128)(2,1)S(1)}, u32[]{:S(2)}, u32[]{:S(2)}) collective-permute-start(bf16[128,512]{1,0:T(8,128)(2,1)S(1)} %get-tuple-element.361), channel_id=1, source_target_pairs={{0,16},{1,17},{2,18},{3,19},{4,20},{5,21},{6,22},{7,23},{8,24},{9,... | collective-permute-start | bytes 393224 | tf_op jit(solution)/shard_map/ppermute | solution.py:60
  238.5 27.1 %collective-permute-start.9 = (bf16[128,512]{1,0:T(8,128)(2,1)S(1)}, bf16[128,512]{1,0:T(8,128)(2,1)S(1)}, u32[]{:S(2)}, u32[]{:S(2)}) collective-permute-start(bf16[128,512]{1,0:T(8,128)(2,1)S(1)} %get-tuple-element.362), channel_id=1, source_target_pairs={{0,16},{1,17},{2,18},{3,19},{4,20},{5,21},{6,22},{7,23},{8,24},{9,... | collective-permute-start | bytes 393224 | tf_op jit(solution)/shard_map/ppermute | solution.py:60
  253.7 30.6 %collective-permute-start.25 = (bf16[256,512]{1,0:T(8,128)(2,1)S(1)}, bf16[256,512]{1,0:T(8,128)(2,1)S(1)}, u32[]{:S(2)}, u32[]{:S(2)}) collective-permute-start(bf16[256,512]{1,0:T(8,128)(2,1)S(1)} %pad_maximum_fusion.32), channel_id=1, source_target_pairs={{0,8},{1,9},{2,10},{3,11},{4,12},{5,13},{6,14},{7,15},{8,0},{9,1},... | collective-permute-start | bytes 786440 | tf_op jit(solution)/shard_map/ppermute | solution.py:60
  256.6 44.6 %collective-permute-start.20 = (bf16[256,512]{1,0:T(8,128)(2,1)S(1)}, bf16[256,512]{1,0:T(8,128)(2,1)S(1)}, u32[]{:S(2)}, u32[]{:S(2)}) collective-permute-start(bf16[256,512]{1,0:T(8,128)(2,1)S(1)} %pad_maximum_fusion.31), channel_id=1, source_target_pairs={{0,8},{1,9},{2,10},{3,11},{4,12},{5,13},{6,14},{7,15},{8,0},{9,1},... | collective-permute-start | bytes 786440 | tf_op jit(solution)/shard_map/ppermute | solution.py:60
  259.4 58.6 %collective-permute-start.15 = (bf16[256,512]{1,0:T(8,128)(2,1)S(1)}, bf16[256,512]{1,0:T(8,128)(2,1)S(1)}, u32[]{:S(2)}, u32[]{:S(2)}) collective-permute-start(bf16[256,512]{1,0:T(8,128)(2,1)S(1)} %pad_maximum_fusion.30), channel_id=1, source_target_pairs={{0,8},{1,9},{2,10},{3,11},{4,12},{5,13},{6,14},{7,15},{8,0},{9,1},... | collective-permute-start | bytes 786440 | tf_op jit(solution)/shard_map/ppermute | solution.py:60
  265.6 63.6 %collective-permute-start.10 = (bf16[256,512]{1,0:T(8,128)(2,1)S(1)}, bf16[256,512]{1,0:T(8,128)(2,1)S(1)}, u32[]{:S(2)}, u32[]{:S(2)}) collective-permute-start(bf16[256,512]{1,0:T(8,128)(2,1)S(1)} %pad_maximum_fusion.29), channel_id=1, source_target_pairs={{0,8},{1,9},{2,10},{3,11},{4,12},{5,13},{6,14},{7,15},{8,0},{9,1},... | collective-permute-start | bytes 786440 | tf_op jit(solution)/shard_map/ppermute | solution.py:60
  284.4 48.7 %collective-permute-start.26 = (bf16[512,512]{1,0:T(8,128)(2,1)S(1)}, bf16[512,512]{1,0:T(8,128)(2,1)S(1)}, u32[]{:S(2)}, u32[]{:S(2)}) collective-permute-start(bf16[512,512]{1,0:T(8,128)(2,1)S(1)} %pad_maximum_fusion.26), channel_id=1, source_target_pairs={{0,2},{1,3},{2,0},{3,1},{4,6},{5,7},{6,4},{7,5},{8,10},{9,11},{10,... | collective-permute-start | bytes 1572872 | tf_op jit(solution)/shard_map/ppermute | solution.py:60
  301.2 32.0 %collective-permute-start.21 = (bf16[512,512]{1,0:T(8,128)(2,1)S(1)}, bf16[512,512]{1,0:T(8,128)(2,1)S(1)}, u32[]{:S(2)}, u32[]{:S(2)}) collective-permute-start(bf16[512,512]{1,0:T(8,128)(2,1)S(1)} %pad_maximum_fusion.25), channel_id=1, source_target_pairs={{0,4},{1,5},{2,6},{3,7},{4,0},{5,1},{6,2},{7,3},{8,12},{9,13},{10,... | collective-permute-start | bytes 1572872 | tf_op jit(solution)/shard_map/ppermute | solution.py:60
  333.2 33.7 %collective-permute-start.27 = (bf16[1024,512]{1,0:T(8,128)(2,1)S(1)}, bf16[1024,512]{1,0:T(8,128)(2,1)S(1)}, u32[]{:S(2)}, u32[]{:S(2)}) collective-permute-start(bf16[1024,512]{1,0:T(8,128)(2,1)S(1)} %pad_maximum_fusion.10), channel_id=1, source_target_pairs={{0,4},{1,5},{2,6},{3,7},{4,0},{5,1},{6,2},{7,3},{8,12},{9,13},{10,... | collective-permute-start | bytes 3145736 | tf_op jit(solution)/shard_map/ppermute | solution.py:60
  333.3 34.6 %collective-permute-start.22 = (bf16[1024,512]{1,0:T(8,128)(2,1)S(1)}, bf16[1024,512]{1,0:T(8,128)(2,1)S(1)}, u32[]{:S(2)}, u32[]{:S(2)}) collective-permute-start(bf16[1024,512]{1,0:T(8,128)(2,1)S(1)} %pad_maximum_fusion.9), channel_id=1, source_target_pairs={{0,2},{1,3},{2,0},{3,1},{4,6},{5,7},{6,4},{7,5},{8,10},{9,11},{10,... | collective-permute-start | bytes 3145736 | tf_op jit(solution)/shard_map/ppermute | solution.py:60
  333.5 55.1 %collective-permute-start.17 = (bf16[1024,512]{1,0:T(8,128)(2,1)S(1)}, bf16[1024,512]{1,0:T(8,128)(2,1)S(1)}, u32[]{:S(2)}, u32[]{:S(2)}) collective-permute-start(bf16[1024,512]{1,0:T(8,128)(2,1)S(1)} %pad_maximum_fusion.8), channel_id=1, source_target_pairs={{0,4},{1,5},{2,6},{3,7},{4,0},{5,1},{6,2},{7,3},{8,12},{9,13},{10,... | collective-permute-start | bytes 3145736 | tf_op jit(solution)/shard_map/ppermute | solution.py:60
  344.5 45.2 %collective-permute-start.12 = (bf16[1024,512]{1,0:T(8,128)(2,1)S(1)}, bf16[1024,512]{1,0:T(8,128)(2,1)S(1)}, u32[]{:S(2)}, u32[]{:S(2)}) collective-permute-start(bf16[1024,512]{1,0:T(8,128)(2,1)S(1)} %pad_maximum_fusion.7), channel_id=1, source_target_pairs={{0,2},{1,3},{2,0},{3,1},{4,6},{5,7},{6,4},{7,5},{8,10},{9,11},{10,... | collective-permute-start | bytes 3145736 | tf_op jit(solution)/shard_map/ppermute | solution.py:60
  368.0 86.6 %collective-permute-start.28 = (bf16[2048,512]{1,0:T(8,128)(2,1)}, bf16[2048,512]{1,0:T(8,128)(2,1)}, u32[]{:S(2)}, u32[]{:S(2)}) collective-permute-start(bf16[2048,512]{1,0:T(8,128)(2,1)} %constant_dynamic-update-slice_fusion.26.refs_7_), channel_id=1, source_target_pairs={{0,1},{1,0},{2,3},{3,2},{4,5},{5,4},{6,7},{7,6},{8,9},{9,8},{10,11... | collective-permute-start | bytes 6291464 | tf_op jit(solution)/shard_map/ppermute | solution.py:60
  369.0 85.6 %collective-permute-start.23 = (bf16[2048,512]{1,0:T(8,128)(2,1)}, bf16[2048,512]{1,0:T(8,128)(2,1)}, u32[]{:S(2)}, u32[]{:S(2)}) collective-permute-start(bf16[2048,512]{1,0:T(8,128)(2,1)} %constant_dynamic-update-slice_fusion.21.refs_6_), channel_id=1, source_target_pairs={{0,1},{1,0},{2,3},{3,2},{4,5},{5,4},{6,7},{7,6},{8,9},{9,8},{10,11... | collective-permute-start | bytes 6291464 | tf_op jit(solution)/shard_map/ppermute | solution.py:60
  389.6 65.0 %collective-permute-start.18 = (bf16[2048,512]{1,0:T(8,128)(2,1)}, bf16[2048,512]{1,0:T(8,128)(2,1)}, u32[]{:S(2)}, u32[]{:S(2)}) collective-permute-start(bf16[2048,512]{1,0:T(8,128)(2,1)} %constant_dynamic-update-slice_fusion.16.refs_5_), channel_id=1, source_target_pairs={{0,1},{1,0},{2,3},{3,2},{4,5},{5,4},{6,7},{7,6},{8,9},{9,8},{10,11... | collective-permute-start | bytes 6291464 | tf_op jit(solution)/shard_map/ppermute | solution.py:60
  390.7 63.9 %collective-permute-start.13 = (bf16[2048,512]{1,0:T(8,128)(2,1)}, bf16[2048,512]{1,0:T(8,128)(2,1)}, u32[]{:S(2)}, u32[]{:S(2)}) collective-permute-start(bf16[2048,512]{1,0:T(8,128)(2,1)} %constant_dynamic-update-slice_fusion.11.refs_4_), channel_id=1, source_target_pairs={{0,1},{1,0},{2,3},{3,2},{4,5},{5,4},{6,7},{7,6},{8,9},{9,8},{10,11... | collective-permute-start | bytes 6291464 | tf_op jit(solution)/shard_map/ppermute | solution.py:60
  489.3 29.8 %collective-permute-start.30 = (bf16[2048,512]{1,0:T(8,128)(2,1)}, bf16[2048,512]{1,0:T(8,128)(2,1)}, u32[]{:S(2)}, u32[]{:S(2)}) collective-permute-start(bf16[2048,512]{1,0:T(8,128)(2,1)} %get-tuple-element.114), channel_id=1, source_target_pairs={{0,1},{1,0},{2,3},{3,2},{4,5},{5,4},{6,7},{7,6},{8,9},{9,8},{10,11... | collective-permute-start | bytes 6291464 | tf_op jit(solution)/shard_map/ppermute | solution.py:60
  489.9 34.6 %collective-permute-start.29 = (bf16[2048,512]{1,0:T(8,128)(2,1)}, bf16[2048,512]{1,0:T(8,128)(2,1)}, u32[]{:S(2)}, u32[]{:S(2)}) collective-permute-start(bf16[2048,512]{1,0:T(8,128)(2,1)} %get-tuple-element.113), channel_id=1, source_target_pairs={{0,1},{1,0},{2,3},{3,2},{4,5},{5,4},{6,7},{7,6},{8,9},{9,8},{10,11... | collective-permute-start | bytes 6291464 | tf_op jit(solution)/shard_map/ppermute | solution.py:60
  490.4 49.0 %collective-permute-start.39 = (bf16[2048,512]{1,0:T(8,128)(2,1)}, bf16[2048,512]{1,0:T(8,128)(2,1)}, u32[]{:S(2)}, u32[]{:S(2)}) collective-permute-start(bf16[2048,512]{1,0:T(8,128)(2,1)} %get-tuple-element.115), channel_id=1, source_target_pairs={{0,1},{1,0},{2,3},{3,2},{4,5},{5,4},{6,7},{7,6},{8,9},{9,8},{10,11... | collective-permute-start | bytes 6291464 | tf_op jit(solution)/shard_map/ppermute | solution.py:60
  490.4 80.5 %collective-permute-start.44 = (bf16[2048,512]{1,0:T(8,128)(2,1)}, bf16[2048,512]{1,0:T(8,128)(2,1)}, u32[]{:S(2)}, u32[]{:S(2)}) collective-permute-start(bf16[2048,512]{1,0:T(8,128)(2,1)} %get-tuple-element.116), channel_id=1, source_target_pairs={{0,1},{1,0},{2,3},{3,2},{4,5},{5,4},{6,7},{7,6},{8,9},{9,8},{10,11... | collective-permute-start | bytes 6291464 | tf_op jit(solution)/shard_map/ppermute | solution.py:60
  527.6 53.6 %collective-permute-start.32 = (bf16[1024,512]{1,0:T(8,128)(2,1)}, bf16[1024,512]{1,0:T(8,128)(2,1)}, u32[]{:S(2)}, u32[]{:S(2)}) collective-permute-start(bf16[1024,512]{1,0:T(8,128)(2,1)} %get-tuple-element.123), channel_id=1, source_target_pairs={{0,4},{1,5},{2,6},{3,7},{4,0},{5,1},{6,2},{7,3},{8,12},{9,13},{10,... | collective-permute-start | bytes 3145736 | tf_op jit(solution)/shard_map/ppermute | solution.py:60
  539.4 44.6 %collective-permute-start.31 = (bf16[1024,512]{1,0:T(8,128)(2,1)}, bf16[1024,512]{1,0:T(8,128)(2,1)}, u32[]{:S(2)}, u32[]{:S(2)}) collective-permute-start(bf16[1024,512]{1,0:T(8,128)(2,1)} %get-tuple-element.122), channel_id=1, source_target_pairs={{0,2},{1,3},{2,0},{3,1},{4,6},{5,7},{6,4},{7,5},{8,10},{9,11},{10,... | collective-permute-start | bytes 3145736 | tf_op jit(solution)/shard_map/ppermute | solution.py:60
  568.9 31.3 %collective-permute-start.40 = (bf16[1024,512]{1,0:T(8,128)(2,1)}, bf16[1024,512]{1,0:T(8,128)(2,1)}, u32[]{:S(2)}, u32[]{:S(2)}) collective-permute-start(bf16[1024,512]{1,0:T(8,128)(2,1)} %get-tuple-element.294), channel_id=1, source_target_pairs={{0,2},{1,3},{2,0},{3,1},{4,6},{5,7},{6,4},{7,5},{8,10},{9,11},{10,... | collective-permute-start | bytes 3145736 | tf_op jit(solution)/shard_map/ppermute | solution.py:60
  574.8 27.7 %collective-permute-start.45 = (bf16[1024,512]{1,0:T(8,128)(2,1)}, bf16[1024,512]{1,0:T(8,128)(2,1)}, u32[]{:S(2)}, u32[]{:S(2)}) collective-permute-start(bf16[1024,512]{1,0:T(8,128)(2,1)} %get-tuple-element.296), channel_id=1, source_target_pairs={{0,4},{1,5},{2,6},{3,7},{4,0},{5,1},{6,2},{7,3},{8,12},{9,13},{10,... | collective-permute-start | bytes 3145736 | tf_op jit(solution)/shard_map/ppermute | solution.py:60
  575.1 148.0 %collective-permute-start.54 = (bf16[2048,512]{1,0:T(8,128)(2,1)}, bf16[2048,512]{1,0:T(8,128)(2,1)}, u32[]{:S(2)}, u32[]{:S(2)}) collective-permute-start(bf16[2048,512]{1,0:T(8,128)(2,1)} %get-tuple-element.154), channel_id=1, source_target_pairs={{0,1},{1,0},{2,3},{3,2},{4,5},{5,4},{6,7},{7,6},{8,9},{9,8},{10,11... | collective-permute-start | bytes 6291464 | tf_op jit(solution)/shard_map/ppermute | solution.py:60
  581.2 145.5 %collective-permute-start.53 = (bf16[2048,512]{1,0:T(8,128)(2,1)}, bf16[2048,512]{1,0:T(8,128)(2,1)}, u32[]{:S(2)}, u32[]{:S(2)}) collective-permute-start(bf16[2048,512]{1,0:T(8,128)(2,1)} %get-tuple-element.152), channel_id=1, source_target_pairs={{0,1},{1,0},{2,3},{3,2},{4,5},{5,4},{6,7},{7,6},{8,9},{9,8},{10,11... | collective-permute-start | bytes 6291464 | tf_op jit(solution)/shard_map/ppermute | solution.py:60
  584.0 151.6 %collective-permute-start.63 = (bf16[2048,512]{1,0:T(8,128)(2,1)}, bf16[2048,512]{1,0:T(8,128)(2,1)}, u32[]{:S(2)}, u32[]{:S(2)}) collective-permute-start(bf16[2048,512]{1,0:T(8,128)(2,1)} %get-tuple-element.164), channel_id=1, source_target_pairs={{0,1},{1,0},{2,3},{3,2},{4,5},{5,4},{6,7},{7,6},{8,9},{9,8},{10,11... | collective-permute-start | bytes 6291464 | tf_op jit(solution)/shard_map/ppermute | solution.py:60
  614.6 46.8 %collective-permute-start.41 = (bf16[512,512]{1,0:T(8,128)(2,1)}, bf16[512,512]{1,0:T(8,128)(2,1)}, u32[]{:S(2)}, u32[]{:S(2)}) collective-permute-start(bf16[512,512]{1,0:T(8,128)(2,1)} %get-tuple-element.318), channel_id=1, source_target_pairs={{0,4},{1,5},{2,6},{3,7},{4,0},{5,1},{6,2},{7,3},{8,12},{9,13},{10,... | collective-permute-start | bytes 1572872 | tf_op jit(solution)/shard_map/ppermute | solution.py:60
  617.2 47.4 %collective-permute-start.46 = (bf16[512,512]{1,0:T(8,128)(2,1)}, bf16[512,512]{1,0:T(8,128)(2,1)}, u32[]{:S(2)}, u32[]{:S(2)}) collective-permute-start(bf16[512,512]{1,0:T(8,128)(2,1)} %get-tuple-element.320), channel_id=1, source_target_pairs={{0,2},{1,3},{2,0},{3,1},{4,6},{5,7},{6,4},{7,5},{8,10},{9,11},{10,... | collective-permute-start | bytes 1572872 | tf_op jit(solution)/shard_map/ppermute | solution.py:60
  640.7 155.3 %all-to-all-start.1 = ((bf16[8,3,88,256]{3,2,1,0:T(8,128)(2,1)}), bf16[8,3,88,256]{3,2,1,0:T(8,128)(2,1)S(1)}, u32[]{:S(2)}, u32[]{:S(2)}) async-start(bf16[8,3,88,256]{3,2,1,0:T(8,128)(2,1)} %maximum_bitcast_fusion.1), calls=%async_computation.3 | async-start | bytes 2162688 | tf_op jit(solution)/shard_map/all_to_all | solution.py:625
  644.4 326.8 %reduce-scatter.5.cloned.1.call-start = ((), (), s32[]{:S(2)}) async-start(), calls=%async_computation.7 | async-start | bytes 2359296 | tf_op jit(solution)/shard_map/reduce_scatter | solution.py:645
  664.6 15.6 %collective-permute-start.35 = (bf16[256,512]{1,0:T(8,128)(2,1)S(1)}, bf16[256,512]{1,0:T(8,128)(2,1)S(1)}, u32[]{:S(2)}, u32[]{:S(2)}) collective-permute-start(bf16[256,512]{1,0:T(8,128)(2,1)S(1)} %copy-done.80), channel_id=1, source_target_pairs={{0,8},{1,9},{2,10},{3,11},{4,12},{5,13},{6,14},{7,15},{8,0},{9,1},... | collective-permute-start | bytes 786440 | tf_op jit(solution)/shard_map/ppermute | solution.py:60
  685.8 53.1 %collective-permute-start.68 = (bf16[2048,512]{1,0:T(8,128)(2,1)}, bf16[2048,512]{1,0:T(8,128)(2,1)}, u32[]{:S(2)}, u32[]{:S(2)}) collective-permute-start(bf16[2048,512]{1,0:T(8,128)(2,1)} %get-tuple-element.166), channel_id=1, source_target_pairs={{0,1},{1,0},{2,3},{3,2},{4,5},{5,4},{6,7},{7,6},{8,9},{9,8},{10,11... | collective-permute-start | bytes 6291464 | tf_op jit(solution)/shard_map/ppermute | solution.py:60
  730.3 26.3 %collective-permute-start.56 = (bf16[1024,512]{1,0:T(8,128)(2,1)}, bf16[1024,512]{1,0:T(8,128)(2,1)}, u32[]{:S(2)}, u32[]{:S(2)}) collective-permute-start(bf16[1024,512]{1,0:T(8,128)(2,1)} %get-tuple-element.156), channel_id=1, source_target_pairs={{0,4},{1,5},{2,6},{3,7},{4,0},{5,1},{6,2},{7,3},{8,12},{9,13},{10,... | collective-permute-start | bytes 3145736 | tf_op jit(solution)/shard_map/ppermute | solution.py:60
  733.8 35.2 %collective-permute-start.55 = (bf16[1024,512]{1,0:T(8,128)(2,1)}, bf16[1024,512]{1,0:T(8,128)(2,1)S(1)}, u32[]{:S(2)}, u32[]{:S(2)}) collective-permute-start(bf16[1024,512]{1,0:T(8,128)(2,1)} %get-tuple-element.155), channel_id=1, source_target_pairs={{0,2},{1,3},{2,0},{3,1},{4,6},{5,7},{6,4},{7,5},{8,10},{9,11},{10,... | collective-permute-start | bytes 3145736 | tf_op jit(solution)/shard_map/ppermute | solution.py:60
  738.3 53.1 %collective-permute-start.64 = (bf16[1024,512]{1,0:T(8,128)(2,1)S(1)}, bf16[1024,512]{1,0:T(8,128)(2,1)S(1)}, u32[]{:S(2)}, u32[]{:S(2)}) collective-permute-start(bf16[1024,512]{1,0:T(8,128)(2,1)S(1)} %get-tuple-element.286), channel_id=1, source_target_pairs={{0,2},{1,3},{2,0},{3,1},{4,6},{5,7},{6,4},{7,5},{8,10},{9,11},{10,... | collective-permute-start | bytes 3145736 | tf_op jit(solution)/shard_map/ppermute | solution.py:60
  741.0 53.8 %collective-permute-start.69 = (bf16[1024,512]{1,0:T(8,128)(2,1)S(1)}, bf16[1024,512]{1,0:T(8,128)(2,1)S(1)}, u32[]{:S(2)}, u32[]{:S(2)}) collective-permute-start(bf16[1024,512]{1,0:T(8,128)(2,1)S(1)} %get-tuple-element.288), channel_id=1, source_target_pairs={{0,4},{1,5},{2,6},{3,7},{4,0},{5,1},{6,2},{7,3},{8,12},{9,13},{10,... | collective-permute-start | bytes 3145736 | tf_op jit(solution)/shard_map/ppermute | solution.py:60
  748.7 50.1 %collective-permute-start.50 = (bf16[256,2048]{1,0:T(8,128)(2,1)}, bf16[256,2048]{1,0:T(8,128)(2,1)}, u32[]{:S(2)}, u32[]{:S(2)}) collective-permute-start(bf16[256,2048]{1,0:T(8,128)(2,1)} %pad_maximum_fusion.12), channel_id=1, source_target_pairs={{0,1},{1,0},{2,3},{3,2},{4,5},{5,4},{6,7},{7,6},{8,9},{9,8},{10,11... | collective-permute-start | bytes 3145736 | tf_op jit(solution)/shard_map/ppermute | solution.py:60
  770.3 73.5 %collective-permute-start.58 = (bf16[512,512]{1,0:T(8,128)(2,1)}, bf16[512,512]{1,0:T(8,128)(2,1)}, u32[]{:S(2)}, u32[]{:S(2)}) collective-permute-start(bf16[512,512]{1,0:T(8,128)(2,1)} %get-tuple-element.158), channel_id=1, source_target_pairs={{0,2},{1,3},{2,0},{3,1},{4,6},{5,7},{6,4},{7,5},{8,10},{9,11},{10,... | collective-permute-start | bytes 1572872 | tf_op jit(solution)/shard_map/ppermute | solution.py:60
  770.6 80.5 %collective-permute-start.57 = (bf16[512,512]{1,0:T(8,128)(2,1)}, bf16[512,512]{1,0:T(8,128)(2,1)}, u32[]{:S(2)}, u32[]{:S(2)}) collective-permute-start(bf16[512,512]{1,0:T(8,128)(2,1)} %get-tuple-element.157), channel_id=1, source_target_pairs={{0,4},{1,5},{2,6},{3,7},{4,0},{5,1},{6,2},{7,3},{8,12},{9,13},{10,... | collective-permute-start | bytes 1572872 | tf_op jit(solution)/shard_map/ppermute | solution.py:60
  792.8 62.4 %collective-permute-start.65 = (bf16[512,512]{1,0:T(8,128)(2,1)}, bf16[512,512]{1,0:T(8,128)(2,1)}, u32[]{:S(2)}, u32[]{:S(2)}) collective-permute-start(bf16[512,512]{1,0:T(8,128)(2,1)} %get-tuple-element.310), channel_id=1, source_target_pairs={{0,4},{1,5},{2,6},{3,7},{4,0},{5,1},{6,2},{7,3},{8,12},{9,13},{10,... | collective-permute-start | bytes 1572872 | tf_op jit(solution)/shard_map/ppermute | solution.py:60
  796.1 61.1 %collective-permute-start.70 = (bf16[512,512]{1,0:T(8,128)(2,1)}, bf16[512,512]{1,0:T(8,128)(2,1)}, u32[]{:S(2)}, u32[]{:S(2)}) collective-permute-start(bf16[512,512]{1,0:T(8,128)(2,1)} %get-tuple-element.312), channel_id=1, source_target_pairs={{0,2},{1,3},{2,0},{3,1},{4,6},{5,7},{6,4},{7,5},{8,10},{9,11},{10,... | collective-permute-start | bytes 1572872 | tf_op jit(solution)/shard_map/ppermute | solution.py:60
  802.8 191.6 %reduce-scatter.3.cloned.1.call-start = ((), (), s32[]{:S(2)}) async-start(), calls=%async_computation.6 | async-start | bytes 4718592 | tf_op jit(solution)/shard_map/reduce_scatter | solution.py:701
  849.0 18.2 %collective-permute-start.52 = (bf16[128,2688]{1,0:T(8,128)(2,1)S(1)}, bf16[128,2688]{1,0:T(8,128)(2,1)S(1)}, u32[]{:S(2)}, u32[]{:S(2)}) collective-permute-start(bf16[128,2688]{1,0:T(8,128)(2,1)S(1)} %slice.1332), channel_id=1, source_target_pairs={{0,2},{1,3},{2,0},{3,1},{4,6},{5,7},{6,4},{7,5},{8,10},{9,11},{10,... | collective-permute-start | bytes 2064392 | tf_op jit(solution)/shard_map/ppermute | solution.py:60
  853.2 42.0 %collective-permute-start.60 = (bf16[256,512]{1,0:T(8,128)(2,1)}, bf16[256,512]{1,0:T(8,128)(2,1)}, u32[]{:S(2)}, u32[]{:S(2)}) collective-permute-start(bf16[256,512]{1,0:T(8,128)(2,1)} %get-tuple-element.160), channel_id=1, source_target_pairs={{0,8},{1,9},{2,10},{3,11},{4,12},{5,13},{6,14},{7,15},{8,0},{9,1},... | collective-permute-start | bytes 786440 | tf_op jit(solution)/shard_map/ppermute | solution.py:60
  853.2 43.6 %collective-permute-start.59 = (bf16[256,512]{1,0:T(8,128)(2,1)}, bf16[256,512]{1,0:T(8,128)(2,1)}, u32[]{:S(2)}, u32[]{:S(2)}) collective-permute-start(bf16[256,512]{1,0:T(8,128)(2,1)} %get-tuple-element.159), channel_id=1, source_target_pairs={{0,8},{1,9},{2,10},{3,11},{4,12},{5,13},{6,14},{7,15},{8,0},{9,1},... | collective-permute-start | bytes 786440 | tf_op jit(solution)/shard_map/ppermute | solution.py:60
  857.2 43.5 %collective-permute-start.66 = (bf16[256,512]{1,0:T(8,128)(2,1)}, bf16[256,512]{1,0:T(8,128)(2,1)}, u32[]{:S(2)}, u32[]{:S(2)}) collective-permute-start(bf16[256,512]{1,0:T(8,128)(2,1)} %get-tuple-element.341), channel_id=1, source_target_pairs={{0,8},{1,9},{2,10},{3,11},{4,12},{5,13},{6,14},{7,15},{8,0},{9,1},... | collective-permute-start | bytes 786440 | tf_op jit(solution)/shard_map/ppermute | solution.py:60
  859.2 42.6 %collective-permute-start.71 = (bf16[256,512]{1,0:T(8,128)(2,1)}, bf16[256,512]{1,0:T(8,128)(2,1)}, u32[]{:S(2)}, u32[]{:S(2)}) collective-permute-start(bf16[256,512]{1,0:T(8,128)(2,1)} %get-tuple-element.343), channel_id=1, source_target_pairs={{0,8},{1,9},{2,10},{3,11},{4,12},{5,13},{6,14},{7,15},{8,0},{9,1},... | collective-permute-start | bytes 786440 | tf_op jit(solution)/shard_map/ppermute | solution.py:60
  895.1 37.8 %collective-permute-start.73 = (bf16[1024,640]{1,0:T(8,128)(2,1)S(1)}, bf16[1024,640]{1,0:T(8,128)(2,1)S(1)}, u32[]{:S(2)}, u32[]{:S(2)}) collective-permute-start(bf16[1024,640]{1,0:T(8,128)(2,1)S(1)} %bitcast.234), channel_id=1, source_target_pairs={{0,1},{1,0},{2,3},{3,2},{4,5},{5,4},{6,7},{7,6},{8,9},{9,8},{10,11... | collective-permute-start | bytes 3932168 | tf_op jit(solution)/shard_map/ppermute | solution.py:60
  897.7 25.8 %collective-permute-start.61 = (bf16[128,512]{1,0:T(8,128)(2,1)S(1)}, bf16[128,512]{1,0:T(8,128)(2,1)S(1)}, u32[]{:S(2)}, u32[]{:S(2)}) collective-permute-start(bf16[128,512]{1,0:T(8,128)(2,1)S(1)} %add_convert_fusion.54), channel_id=1, source_target_pairs={{0,16},{1,17},{2,18},{3,19},{4,20},{5,21},{6,22},{7,23},{8,24},{9,... | collective-permute-start | bytes 393224 | tf_op jit(solution)/shard_map/ppermute | solution.py:60
  897.8 34.2 %collective-permute-start.62 = (bf16[128,512]{1,0:T(8,128)(2,1)S(1)}, bf16[128,512]{1,0:T(8,128)(2,1)S(1)}, u32[]{:S(2)}, u32[]{:S(2)}) collective-permute-start(bf16[128,512]{1,0:T(8,128)(2,1)S(1)} %add_convert_fusion.53), channel_id=1, source_target_pairs={{0,16},{1,17},{2,18},{3,19},{4,20},{5,21},{6,22},{7,23},{8,24},{9,... | collective-permute-start | bytes 393224 | tf_op jit(solution)/shard_map/ppermute | solution.py:60
  901.6 38.7 %collective-permute-start.67 = (bf16[128,512]{1,0:T(8,128)(2,1)S(1)}, bf16[128,512]{1,0:T(8,128)(2,1)S(1)}, u32[]{:S(2)}, u32[]{:S(2)}) collective-permute-start(bf16[128,512]{1,0:T(8,128)(2,1)S(1)} %add_convert_fusion.50), channel_id=1, source_target_pairs={{0,16},{1,17},{2,18},{3,19},{4,20},{5,21},{6,22},{7,23},{8,24},{9,... | collective-permute-start | bytes 393224 | tf_op jit(solution)/shard_map/ppermute | solution.py:60
  902.7 43.4 %collective-permute-start.72 = (bf16[128,512]{1,0:T(8,128)(2,1)S(1)}, bf16[128,512]{1,0:T(8,128)(2,1)S(1)}, u32[]{:S(2)}, u32[]{:S(2)}) collective-permute-start(bf16[128,512]{1,0:T(8,128)(2,1)S(1)} %add_convert_fusion.48), channel_id=1, source_target_pairs={{0,16},{1,17},{2,18},{3,19},{4,20},{5,21},{6,22},{7,23},{8,24},{9,... | collective-permute-start | bytes 393224 | tf_op jit(solution)/shard_map/ppermute | solution.py:60
  933.5 16.7 %collective-permute-start.74 = (bf16[512,640]{1,0:T(8,128)(2,1)S(1)}, bf16[512,640]{1,0:T(8,128)(2,1)S(1)}, u32[]{:S(2)}, u32[]{:S(2)}) collective-permute-start(bf16[512,640]{1,0:T(8,128)(2,1)S(1)} %slice.1333), channel_id=1, source_target_pairs={{0,2},{1,3},{2,0},{3,1},{4,6},{5,7},{6,4},{7,5},{8,10},{9,11},{10,... | collective-permute-start | bytes 1966088 | tf_op jit(solution)/shard_map/ppermute | solution.py:60
  (144 other events, 1406.0 us)
Sparse Core Ops, SparseCore 0:
  16.1 156.6 all-gather.2
  175.6 156.3 all-gather.4
  802.9 72.2 reduce-scatter.4
  878.8 115.6 reduce-scatter.2
